TPU v7x, 512 devices: a whole 4x4x16 slice. The times are simulated.
512 devices in a mesh: row: 4 (over y_hi, core), sector: 64 (over z, x), band: 2 (over y_lo).
Axes of the slice: x: 4, y: 4 (y_hi: 2, y_lo: 2; y = y_hi * 2 + y_lo), z: 16, core: 2. Of those that a mesh axis runs over, the one named last changes fastest.
Arguments:
- residual: float32 [4, 64, 2, 320, 128], P('row', 'sector', 'band'), may hold values from -8 to 8
- block_inverse: float32 [4, 64, 2, 320, 320], P('row', 'sector', 'band'), may hold values from -0.3125 to 0.3125
- cycle_coupling: float32 [4, 64, 320, 320], P('row', 'sector'), as said below
- outlet_flux: float32 [4, 64, 2, 80, 320], P('row', 'sector', 'band'), may hold values from -0.3125 to 0.3125
- inlet_lift: float32 [4, 64, 2, 320, 80], P('row', 'sector', 'band'), may hold values from -0.5 to 0.5
- mortar_shift: int32 [3], replicated, may hold values from 0 to 63
Outputs:
- correction: float32 [4, 64, 2, 320, 128], P('row', 'sector', 'band')
- outlet_traces: float32 [4, 64, 2, 80, 128], P('row', 'sector', 'band')
Inputs may be any that keep to these rules, and one draw needn't show every extreme that they name: `mortar_shift`: one sector shift for each of the 3 interfaces between consecutive rows. `cycle_coupling`: each matrix is a positive diagonal plus full off-diagonal entries.
All inputs are finite; a program needn't handle non-finite values.
Results may differ from a plain program's by a relative error of at most 0.00017.
Values sent between devices are 32-bit elements; how exact they have to be, the bound alone decides.
No kernel may reach another device: no remote copies, remote signals or barrier semaphores. Data moves between devices by JAX's collectives and lax.ppermute only.
A program may use at most 64 MiB of HBM per device.

v0:
```python
import jax
import jax.numpy as jnp
from jax import lax
from jax.sharding import PartitionSpec as P

HIGH = lax.Precision.HIGHEST


def from_behind(block, axis, distance):
    devices = range(lax.axis_size(axis))
    route = [((i - distance) % len(devices), i) for i in devices]
    return lax.ppermute(block, axis, route)


def from_behind_2(value, axis, steps):
    count = lax.axis_size(axis)
    leading, last = (max(0, -steps), min(count, count - steps))
    return lax.ppermute(value, axis, [(source, source + steps) for source in range(leading, last)])


def apply_block(matrix, state):
    return jnp.einsum("ij,bjl->bil", matrix, state, precision=HIGH)


def turn_sectors(trace, offset, levels):
    for level in range(levels):
        moved = from_behind(trace, "sector", 2**level)
        trace = jnp.where(offset // 2**level % 2 == 1, moved, trace)
    return trace


def pass_down(trace):
    return from_behind_2(trace, "row", 1)


def on_device(residual, block_inverse, cycle_coupling, outlet_flux, inlet_lift, mortar_shift):
    res_local = residual[0, 0]
    inverse = block_inverse[0, 0]
    coupling = cycle_coupling[0, 0]
    flux = outlet_flux[0, 0]
    lift = inlet_lift[0, 0]
    source = jnp.einsum("bij,bjl->bil", inverse, res_local, precision=HIGH)
    levels = lax.axis_size("sector").bit_length() - 1
    matrix = coupling
    state = source
    for level in range(levels):
        if level + 1 < levels:
            prev_matrix, prev_state = from_behind((matrix, state), "sector", 2**level)
            state = state + apply_block(matrix, prev_state)
            matrix = jnp.dot(matrix, prev_matrix, precision=HIGH)
        else:
            prev_state = from_behind(state, "sector", 2**level)
            state = state + apply_block(matrix, prev_state)
    row_count = lax.axis_size("row")
    row_index = lax.axis_index("row")
    offset = jnp.sum(
        jnp.where(jnp.arange(row_count - 1, dtype=jnp.int32) == row_index - 1, mortar_shift, 0)
    )
    current = state
    for section in range(1, row_count):
        trace = jnp.einsum("bfj,bjl->bfl", flux, current, precision=HIGH)
        moved = turn_sectors(pass_down(trace), offset, levels)
        update = state + jnp.einsum("bjf,bfl->bjl", lift, moved, precision=HIGH)
        current = jnp.where(row_index == section, update, current)
    outlet = jnp.einsum("bfj,bjl->bfl", flux, current, precision=HIGH)
    return (current[None, None], outlet[None, None])


def solution(mesh):
    in_specs = (
        P("row", "sector", "band", None, None),
        P("row", "sector", "band", None, None),
        P("row", "sector", None, None),
        P("row", "sector", "band", None, None),
        P("row", "sector", "band", None, None),
        P(),
    )
    out_specs = (P("row", "sector", "band", None, None), P("row", "sector", "band", None, None))
    return jax.shard_map(
        on_device, mesh=mesh, in_specs=in_specs, out_specs=out_specs, check_vma=False
    )
```

profile of v0, /device:TPU:24, one launch (start us, length us, event | category | flops | bytes accessed | tf_op | source)
XLA Modules:
  0.0 370.2 jit_solution(5395684810242599682)
XLA Ops:
  3.1 3.4 collective-permute-start
  6.5 3.4 collective-permute-start.2
  10.0 11.8 %collective-permute-done = f32[1,320,128]{2,1,0:T(8,128)S(1)} collective-permute-done((f32[1,320,128]{2,1,0:T(8,128)S(1)}, f32[1,320,128]{2,1,0:T(8,128)S(1)}, u32[]{:S(2)}, u32[]{:S(2)}) %collective-permute-start) | collective-permute-done | bytes 163872 | tf_op jit(solution)/shard_map/ppermute | solution.py:12
  22.3 1.9 collective-permute-start.1
  24.2 9.5 %collective-permute-done.2 = f32[320,320]{1,0:T(8,128)S(1)} collective-permute-done((f32[320,320]{1,0:T(8,128)S(1)}, f32[320,320]{1,0:T(8,128)S(1)}, u32[]{:S(2)}, u32[]{:S(2)}) %collective-permute-start.2) | collective-permute-done | bytes 409632 | tf_op jit(solution)/shard_map/ppermute | solution.py:12
  34.9 1.9 collective-permute-start.4
  37.3 1.9 collective-permute-start.3
  39.3 14.1 %collective-permute-done.4 = f32[320,320]{1,0:T(8,128)S(1)} collective-permute-done((f32[320,320]{1,0:T(8,128)S(1)}, f32[320,320]{1,0:T(8,128)S(1)}, u32[]{:S(2)}, u32[]{:S(2)}) %collective-permute-start.4) | collective-permute-done | bytes 409632 | tf_op jit(solution)/shard_map/ppermute | solution.py:12
  54.5 1.9 collective-permute-start.6
  57.0 1.9 collective-permute-start.5
  58.9 15.5 %collective-permute-done.6 = f32[320,320]{1,0:T(8,128)S(1)} collective-permute-done((f32[320,320]{1,0:T(8,128)S(1)}, f32[320,320]{1,0:T(8,128)S(1)}, u32[]{:S(2)}, u32[]{:S(2)}) %collective-permute-start.6) | collective-permute-done | bytes 409632 | tf_op jit(solution)/shard_map/ppermute | solution.py:12
  75.5 1.9 collective-permute-start.8
  77.4 4.4 %collective-permute-done.5 = f32[1,320,128]{2,1,0:T(8,128)S(1)} collective-permute-done((f32[1,320,128]{2,1,0:T(8,128)S(1)}, f32[1,320,128]{2,1,0:T(8,128)S(1)}, u32[]{:S(2)}, u32[]{:S(2)}) %collective-permute-start.5) | collective-permute-done | bytes 163872 | tf_op jit(solution)/shard_map/ppermute | solution.py:12
  84.3 24.5 %collective-permute-done.8 = f32[320,320]{1,0:T(8,128)S(1)} collective-permute-done((f32[320,320]{1,0:T(8,128)S(1)}, f32[320,320]{1,0:T(8,128)S(1)}, u32[]{:S(2)}, u32[]{:S(2)}) %collective-permute-start.8) | collective-permute-done | bytes 409632 | tf_op jit(solution)/shard_map/ppermute | solution.py:12
  109.9 1.9 collective-permute-start.10
  111.8 4.9 %collective-permute-done.7 = f32[1,320,128]{2,1,0:T(8,128)S(1)} collective-permute-done((f32[1,320,128]{2,1,0:T(8,128)S(1)}, f32[1,320,128]{2,1,0:T(8,128)S(1)}, u32[]{:S(2)}, u32[]{:S(2)}) %collective-permute-start.7) | collective-permute-done | bytes 163872 | tf_op jit(solution)/shard_map/ppermute | solution.py:12
  117.3 16.5 %collective-permute-start.9 = (f32[1,320,128]{2,1,0:T(8,128)S(1)}, f32[1,320,128]{2,1,0:T(8,128)S(1)}, u32[]{:S(2)}, u32[]{:S(2)}) collective-permute-start(f32[1,320,128]{2,1,0:T(8,128)S(1)} %fusion.10), channel_id=1, source_target_pairs={{64,0},{66,2},{68,4},{70,6},{72,8},{74,10},{76,12},{78,14},{80,16}... | collective-permute-start | bytes 491528 | tf_op jit(solution)/shard_map/ppermute | solution.py:12
  133.8 25.1 %collective-permute-done.10 = f32[320,320]{1,0:T(8,128)S(1)} collective-permute-done((f32[320,320]{1,0:T(8,128)S(1)}, f32[320,320]{1,0:T(8,128)S(1)}, u32[]{:S(2)}, u32[]{:S(2)}) %collective-permute-start.10) | collective-permute-done | bytes 409632 | tf_op jit(solution)/shard_map/ppermute | solution.py:12
  160.0 5.5 %collective-permute-done.9 = f32[1,320,128]{2,1,0:T(8,128)S(1)} collective-permute-done((f32[1,320,128]{2,1,0:T(8,128)S(1)}, f32[1,320,128]{2,1,0:T(8,128)S(1)}, u32[]{:S(2)}, u32[]{:S(2)}) %collective-permute-start.9) | collective-permute-done | bytes 163872 | tf_op jit(solution)/shard_map/ppermute | solution.py:12
  166.3 1.9 collective-permute-start.11
  168.2 4.9 %collective-permute-done.11 = f32[1,80,128]{2,1,0:T(8,128)S(1)} collective-permute-done((f32[1,80,128]{2,1,0:T(8,128)S(1)}, f32[1,80,128]{2,1,0:T(8,128)S(1)}, u32[]{:S(2)}, u32[]{:S(2)}) %collective-permute-start.11) | collective-permute-done | bytes 40992 | tf_op jit(solution)/shard_map/ppermute | solution.py:18
  177.6 4.7 %collective-permute-done.12 = f32[1,80,128]{2,1,0:T(8,128)S(1)} collective-permute-done((f32[1,80,128]{2,1,0:T(8,128)S(1)}, f32[1,80,128]{2,1,0:T(8,128)S(1)}, u32[]{:S(2)}, u32[]{:S(2)}) %collective-permute-start.12) | collective-permute-done | bytes 40992 | tf_op jit(solution)/shard_map/ppermute | solution.py:12
  182.3 2.4 collective-permute-start.13
  185.4 6.4 %collective-permute-done.13 = f32[1,80,128]{2,1,0:T(8,128)S(1)} collective-permute-done((f32[1,80,128]{2,1,0:T(8,128)S(1)}, f32[1,80,128]{2,1,0:T(8,128)S(1)}, u32[]{:S(2)}, u32[]{:S(2)}) %collective-permute-start.13) | collective-permute-done | bytes 40992 | tf_op jit(solution)/shard_map/ppermute | solution.py:12
  191.8 3.4 collective-permute-start.14
  195.2 3.7 collective-permute-done.14
  200.9 7.0 %collective-permute-done.15 = f32[1,80,128]{2,1,0:T(8,128)S(1)} collective-permute-done((f32[1,80,128]{2,1,0:T(8,128)S(1)}, f32[1,80,128]{2,1,0:T(8,128)S(1)}, u32[]{:S(2)}, u32[]{:S(2)}) %collective-permute-start.15) | collective-permute-done | bytes 40992 | tf_op jit(solution)/shard_map/ppermute | solution.py:12
  207.9 3.9 %collective-permute-start.16 = (f32[1,80,128]{2,1,0:T(8,128)S(1)}, f32[1,80,128]{2,1,0:T(8,128)S(1)}, u32[]{:S(2)}, u32[]{:S(2)}) collective-permute-start(f32[1,80,128]{2,1,0:T(8,128)S(1)} %broadcast_select_fusion.11), channel_id=1, source_target_pairs={{96,0},{98,2},{100,4},{102,6},{104,8},{106,10},{108,12},{110,14},{... | collective-permute-start | bytes 122888 | tf_op jit(solution)/shard_map/ppermute | solution.py:12
  211.8 7.1 %collective-permute-done.16 = f32[1,80,128]{2,1,0:T(8,128)S(1)} collective-permute-done((f32[1,80,128]{2,1,0:T(8,128)S(1)}, f32[1,80,128]{2,1,0:T(8,128)S(1)}, u32[]{:S(2)}, u32[]{:S(2)}) %collective-permute-start.16) | collective-permute-done | bytes 40992 | tf_op jit(solution)/shard_map/ppermute | solution.py:12
  218.9 6.3 %collective-permute-start.17 = (f32[1,80,128]{2,1,0:T(8,128)S(1)}, f32[1,80,128]{2,1,0:T(8,128)S(1)}, u32[]{:S(2)}, u32[]{:S(2)}) collective-permute-start(f32[1,80,128]{2,1,0:T(8,128)S(1)} %broadcast_select_fusion.14), channel_id=1, source_target_pairs={{64,0},{66,2},{68,4},{70,6},{72,8},{74,10},{76,12},{78,14},{80,16}... | collective-permute-start | bytes 122888 | tf_op jit(solution)/shard_map/ppermute | solution.py:12
  225.3 8.3 %collective-permute-done.17 = f32[1,80,128]{2,1,0:T(8,128)S(1)} collective-permute-done((f32[1,80,128]{2,1,0:T(8,128)S(1)}, f32[1,80,128]{2,1,0:T(8,128)S(1)}, u32[]{:S(2)}, u32[]{:S(2)}) %collective-permute-start.17) | collective-permute-done | bytes 40992 | tf_op jit(solution)/shard_map/ppermute | solution.py:12
  236.3 4.9 %collective-permute-done.18 = f32[1,80,128]{2,1,0:T(8,128)S(1)} collective-permute-done((f32[1,80,128]{2,1,0:T(8,128)S(1)}, f32[1,80,128]{2,1,0:T(8,128)S(1)}, u32[]{:S(2)}, u32[]{:S(2)}) %collective-permute-start.18) | collective-permute-done | bytes 40992 | tf_op jit(solution)/shard_map/ppermute | solution.py:18
  243.1 7.5 %collective-permute-done.19 = f32[1,80,128]{2,1,0:T(8,128)S(1)} collective-permute-done((f32[1,80,128]{2,1,0:T(8,128)S(1)}, f32[1,80,128]{2,1,0:T(8,128)S(1)}, u32[]{:S(2)}, u32[]{:S(2)}) %collective-permute-start.19) | collective-permute-done | bytes 40992 | tf_op jit(solution)/shard_map/ppermute | solution.py:12
  252.5 7.6 %collective-permute-done.20 = f32[1,80,128]{2,1,0:T(8,128)S(1)} collective-permute-done((f32[1,80,128]{2,1,0:T(8,128)S(1)}, f32[1,80,128]{2,1,0:T(8,128)S(1)}, u32[]{:S(2)}, u32[]{:S(2)}) %collective-permute-start.20) | collective-permute-done | bytes 40992 | tf_op jit(solution)/shard_map/ppermute | solution.py:12
  262.0 5.6 %collective-permute-done.21 = f32[1,80,128]{2,1,0:T(8,128)S(1)} collective-permute-done((f32[1,80,128]{2,1,0:T(8,128)S(1)}, f32[1,80,128]{2,1,0:T(8,128)S(1)}, u32[]{:S(2)}, u32[]{:S(2)}) %collective-permute-start.21) | collective-permute-done | bytes 40992 | tf_op jit(solution)/shard_map/ppermute | solution.py:12
  269.5 6.5 %collective-permute-done.22 = f32[1,80,128]{2,1,0:T(8,128)S(1)} collective-permute-done((f32[1,80,128]{2,1,0:T(8,128)S(1)}, f32[1,80,128]{2,1,0:T(8,128)S(1)}, u32[]{:S(2)}, u32[]{:S(2)}) %collective-permute-start.22) | collective-permute-done | bytes 40992 | tf_op jit(solution)/shard_map/ppermute | solution.py:12
  276.0 2.1 collective-permute-start.23
  278.1 8.6 %collective-permute-done.23 = f32[1,80,128]{2,1,0:T(8,128)S(1)} collective-permute-done((f32[1,80,128]{2,1,0:T(8,128)S(1)}, f32[1,80,128]{2,1,0:T(8,128)S(1)}, u32[]{:S(2)}, u32[]{:S(2)}) %collective-permute-start.23) | collective-permute-done | bytes 40992 | tf_op jit(solution)/shard_map/ppermute | solution.py:12
  286.7 5.8 %collective-permute-start.24 = (f32[1,80,128]{2,1,0:T(8,128)S(1)}, f32[1,80,128]{2,1,0:T(8,128)S(1)}, u32[]{:S(2)}, u32[]{:S(2)}) collective-permute-start(f32[1,80,128]{2,1,0:T(8,128)S(1)} %broadcast_select_fusion.13), channel_id=1, source_target_pairs={{64,0},{66,2},{68,4},{70,6},{72,8},{74,10},{76,12},{78,14},{80,16}... | collective-permute-start | bytes 122888 | tf_op jit(solution)/shard_map/ppermute | solution.py:12
  292.5 9.1 %collective-permute-done.24 = f32[1,80,128]{2,1,0:T(8,128)S(1)} collective-permute-done((f32[1,80,128]{2,1,0:T(8,128)S(1)}, f32[1,80,128]{2,1,0:T(8,128)S(1)}, u32[]{:S(2)}, u32[]{:S(2)}) %collective-permute-start.24) | collective-permute-done | bytes 40992 | tf_op jit(solution)/shard_map/ppermute | solution.py:12
  304.3 4.9 %collective-permute-done.25 = f32[1,80,128]{2,1,0:T(8,128)S(1)} collective-permute-done((f32[1,80,128]{2,1,0:T(8,128)S(1)}, f32[1,80,128]{2,1,0:T(8,128)S(1)}, u32[]{:S(2)}, u32[]{:S(2)}) %collective-permute-start.25) | collective-permute-done | bytes 40992 | tf_op jit(solution)/shard_map/ppermute | solution.py:18
  311.1 7.5 %collective-permute-done.26 = f32[1,80,128]{2,1,0:T(8,128)S(1)} collective-permute-done((f32[1,80,128]{2,1,0:T(8,128)S(1)}, f32[1,80,128]{2,1,0:T(8,128)S(1)}, u32[]{:S(2)}, u32[]{:S(2)}) %collective-permute-start.26) | collective-permute-done | bytes 40992 | tf_op jit(solution)/shard_map/ppermute | solution.py:12
  320.5 7.6 %collective-permute-done.27 = f32[1,80,128]{2,1,0:T(8,128)S(1)} collective-permute-done((f32[1,80,128]{2,1,0:T(8,128)S(1)}, f32[1,80,128]{2,1,0:T(8,128)S(1)}, u32[]{:S(2)}, u32[]{:S(2)}) %collective-permute-start.27) | collective-permute-done | bytes 40992 | tf_op jit(solution)/shard_map/ppermute | solution.py:12
  330.0 5.6 %collective-permute-done.28 = f32[1,80,128]{2,1,0:T(8,128)S(1)} collective-permute-done((f32[1,80,128]{2,1,0:T(8,128)S(1)}, f32[1,80,128]{2,1,0:T(8,128)S(1)}, u32[]{:S(2)}, u32[]{:S(2)}) %collective-permute-start.28) | collective-permute-done | bytes 40992 | tf_op jit(solution)/shard_map/ppermute | solution.py:12
  337.5 6.5 %collective-permute-done.29 = f32[1,80,128]{2,1,0:T(8,128)S(1)} collective-permute-done((f32[1,80,128]{2,1,0:T(8,128)S(1)}, f32[1,80,128]{2,1,0:T(8,128)S(1)}, u32[]{:S(2)}, u32[]{:S(2)}) %collective-permute-start.29) | collective-permute-done | bytes 40992 | tf_op jit(solution)/shard_map/ppermute | solution.py:12
  345.9 8.3 %collective-permute-done.30 = f32[1,80,128]{2,1,0:T(8,128)S(1)} collective-permute-done((f32[1,80,128]{2,1,0:T(8,128)S(1)}, f32[1,80,128]{2,1,0:T(8,128)S(1)}, u32[]{:S(2)}, u32[]{:S(2)}) %collective-permute-start.30) | collective-permute-done | bytes 40992 | tf_op jit(solution)/shard_map/ppermute | solution.py:12
  354.2 5.3 %collective-permute-start.31 = (f32[1,80,128]{2,1,0:T(8,128)S(1)}, f32[1,80,128]{2,1,0:T(8,128)S(1)}, u32[]{:S(2)}, u32[]{:S(2)}) collective-permute-start(f32[1,80,128]{2,1,0:T(8,128)S(1)} %broadcast_select_fusion.12), channel_id=1, source_target_pairs={{64,0},{66,2},{68,4},{70,6},{72,8},{74,10},{76,12},{78,14},{80,16}... | collective-permute-start | bytes 122888 | tf_op jit(solution)/shard_map/ppermute | solution.py:12
  359.5 9.3 %collective-permute-done.31 = f32[1,80,128]{2,1,0:T(8,128)S(1)} collective-permute-done((f32[1,80,128]{2,1,0:T(8,128)S(1)}, f32[1,80,128]{2,1,0:T(8,128)S(1)}, u32[]{:S(2)}, u32[]{:S(2)}) %collective-permute-start.31) | collective-permute-done | bytes 40992 | tf_op jit(solution)/shard_map/ppermute | solution.py:12
  (63 shorter events, 41.7 us)
Async XLA Ops:
  0.6 1.0 copy-start
  0.6 5.9 %copy-start.1 = (f32[1,1,320,320]{3,2,1,0:T(8,128)S(1)}, f32[1,1,320,320]{3,2,1,0:T(8,128)}, u32[]{:S(2)}) copy-start(f32[1,1,320,320]{3,2,1,0:T(8,128)} %param.8) | copy-start | bytes 1228804
  3.1 18.6 %collective-permute-start = (f32[1,320,128]{2,1,0:T(8,128)S(1)}, f32[1,320,128]{2,1,0:T(8,128)S(1)}, u32[]{:S(2)}, u32[]{:S(2)}) collective-permute-start(f32[1,320,128]{2,1,0:T(8,128)S(1)} %convolution_bitcast_fusion.6), channel_id=1, source_target_pairs={{126,0},{0,2},{2,4},{4,6},{6,8},{8,10},{10,12},{12,14},{14,16},{16... | collective-permute-start | bytes 491528 | tf_op jit(solution)/shard_map/ppermute | solution.py:12
  6.5 27.2 %collective-permute-start.2 = (f32[320,320]{1,0:T(8,128)S(1)}, f32[320,320]{1,0:T(8,128)S(1)}, u32[]{:S(2)}, u32[]{:S(2)}) collective-permute-start(f32[320,320]{1,0:T(8,128)S(1)} %bitcast.159), channel_id=1, source_target_pairs={{126,0},{0,2},{2,4},{4,6},{6,8},{8,10},{10,12},{12,14},{14,16},{16... | collective-permute-start | bytes 1228808 | tf_op jit(solution)/shard_map/ppermute | solution.py:12
  22.3 14.5 %collective-permute-start.1 = (f32[1,320,128]{2,1,0:T(8,128)S(1)}, f32[1,320,128]{2,1,0:T(8,128)S(1)}, u32[]{:S(2)}, u32[]{:S(2)}) collective-permute-start(f32[1,320,128]{2,1,0:T(8,128)S(1)} %fusion.6), channel_id=1, source_target_pairs={{124,0},{126,2},{0,4},{2,6},{4,8},{6,10},{8,12},{10,14},{12,16},{1... | collective-permute-start | bytes 491528 | tf_op jit(solution)/shard_map/ppermute | solution.py:12
  34.9 18.5 %collective-permute-start.4 = (f32[320,320]{1,0:T(8,128)S(1)}, f32[320,320]{1,0:T(8,128)S(1)}, u32[]{:S(2)}, u32[]{:S(2)}) collective-permute-start(f32[320,320]{1,0:T(8,128)S(1)} %fusion.41), channel_id=1, source_target_pairs={{124,0},{126,2},{0,4},{2,6},{4,8},{6,10},{8,12},{10,14},{12,16},{1... | collective-permute-start | bytes 1228808 | tf_op jit(solution)/shard_map/ppermute | solution.py:12
  37.3 19.1 %collective-permute-start.3 = (f32[1,320,128]{2,1,0:T(8,128)S(1)}, f32[1,320,128]{2,1,0:T(8,128)S(1)}, u32[]{:S(2)}, u32[]{:S(2)}) collective-permute-start(f32[1,320,128]{2,1,0:T(8,128)S(1)} %fusion.7), channel_id=1, source_target_pairs={{120,0},{122,2},{124,4},{126,6},{0,8},{2,10},{4,12},{6,14},{8,16},... | collective-permute-start | bytes 491528 | tf_op jit(solution)/shard_map/ppermute | solution.py:12
  54.5 19.9 %collective-permute-start.6 = (f32[320,320]{1,0:T(8,128)S(1)}, f32[320,320]{1,0:T(8,128)S(1)}, u32[]{:S(2)}, u32[]{:S(2)}) collective-permute-start(f32[320,320]{1,0:T(8,128)S(1)} %fusion.44), channel_id=1, source_target_pairs={{120,0},{122,2},{124,4},{126,6},{0,8},{2,10},{4,12},{6,14},{8,16},... | collective-permute-start | bytes 1228808 | tf_op jit(solution)/shard_map/ppermute | solution.py:12
  57.0 24.8 %collective-permute-start.5 = (f32[1,320,128]{2,1,0:T(8,128)S(1)}, f32[1,320,128]{2,1,0:T(8,128)S(1)}, u32[]{:S(2)}, u32[]{:S(2)}) collective-permute-start(f32[1,320,128]{2,1,0:T(8,128)S(1)} %fusion.8), channel_id=1, source_target_pairs={{112,0},{114,2},{116,4},{118,6},{120,8},{122,10},{124,12},{126,14}... | collective-permute-start | bytes 491528 | tf_op jit(solution)/shard_map/ppermute | solution.py:12
  75.5 33.3 %collective-permute-start.8 = (f32[320,320]{1,0:T(8,128)S(1)}, f32[320,320]{1,0:T(8,128)S(1)}, u32[]{:S(2)}, u32[]{:S(2)}) collective-permute-start(f32[320,320]{1,0:T(8,128)S(1)} %fusion.45), channel_id=1, source_target_pairs={{112,0},{114,2},{116,4},{118,6},{120,8},{122,10},{124,12},{126,14}... | collective-permute-start | bytes 1228808 | tf_op jit(solution)/shard_map/ppermute | solution.py:12
  82.3 34.4 %collective-permute-start.7 = (f32[1,320,128]{2,1,0:T(8,128)S(1)}, f32[1,320,128]{2,1,0:T(8,128)S(1)}, u32[]{:S(2)}, u32[]{:S(2)}) collective-permute-start(f32[1,320,128]{2,1,0:T(8,128)S(1)} %fusion.9), channel_id=1, source_target_pairs={{96,0},{98,2},{100,4},{102,6},{104,8},{106,10},{108,12},{110,14},{... | collective-permute-start | bytes 491528 | tf_op jit(solution)/shard_map/ppermute | solution.py:12
  109.9 49.0 %collective-permute-start.10 = (f32[320,320]{1,0:T(8,128)S(1)}, f32[320,320]{1,0:T(8,128)S(1)}, u32[]{:S(2)}, u32[]{:S(2)}) collective-permute-start(f32[320,320]{1,0:T(8,128)S(1)} %fusion.46), channel_id=1, source_target_pairs={{96,0},{98,2},{100,4},{102,6},{104,8},{106,10},{108,12},{110,14},{... | collective-permute-start | bytes 1228808 | tf_op jit(solution)/shard_map/ppermute | solution.py:12
  117.3 48.2 %collective-permute-start.9 = (f32[1,320,128]{2,1,0:T(8,128)S(1)}, f32[1,320,128]{2,1,0:T(8,128)S(1)}, u32[]{:S(2)}, u32[]{:S(2)}) collective-permute-start(f32[1,320,128]{2,1,0:T(8,128)S(1)} %fusion.10), channel_id=1, source_target_pairs={{64,0},{66,2},{68,4},{70,6},{72,8},{74,10},{76,12},{78,14},{80,16}... | collective-permute-start | bytes 491528 | tf_op jit(solution)/shard_map/ppermute | solution.py:12
  159.9 6.0 %copy-start.2 = (f32[1,1,1,80,320]{4,3,2,1,0:T(8,128)S(1)}, f32[1,1,1,80,320]{4,3,2,1,0:T(8,128)}, u32[]{:S(2)}) copy-start(f32[1,1,1,80,320]{4,3,2,1,0:T(8,128)} %param.9) | copy-start | bytes 307204
  166.3 6.8 %collective-permute-start.11 = (f32[1,80,128]{2,1,0:T(8,128)S(1)}, f32[1,80,128]{2,1,0:T(8,128)S(1)}, u32[]{:S(2)}, u32[]{:S(2)}) collective-permute-start(f32[1,80,128]{2,1,0:T(8,128)S(1)} %convolution_bitcast_fusion.13), channel_id=1, source_target_pairs={{0,128},{128,256},{256,384},{1,129},{129,257},{257,385},{2,130},{1... | collective-permute-start | bytes 122888 | tf_op jit(solution)/shard_map/ppermute | solution.py:18
  168.2 6.8 %copy-start.5 = (s32[3]{0:T(128)S(1)}, s32[3]{0:T(128)}, u32[]{:S(2)}) copy-start(s32[3]{0:T(128)} %param.11) | copy-start | bytes 40
  173.1 9.2 %collective-permute-start.12 = (f32[1,80,128]{2,1,0:T(8,128)S(1)}, f32[1,80,128]{2,1,0:T(8,128)S(1)}, u32[]{:S(2)}, u32[]{:S(2)}) collective-permute-start(f32[1,80,128]{2,1,0:T(8,128)S(1)} %collective-permute-done.11), channel_id=1, source_target_pairs={{126,0},{0,2},{2,4},{4,6},{6,8},{8,10},{10,12},{12,14},{14,16},{16... | collective-permute-start | bytes 122888 | tf_op jit(solution)/shard_map/ppermute | solution.py:12
  182.3 9.5 %collective-permute-start.13 = (f32[1,80,128]{2,1,0:T(8,128)S(1)}, f32[1,80,128]{2,1,0:T(8,128)S(1)}, u32[]{:S(2)}, u32[]{:S(2)}) collective-permute-start(f32[1,80,128]{2,1,0:T(8,128)S(1)} %broadcast_select_fusion.2), channel_id=1, source_target_pairs={{124,0},{126,2},{0,4},{2,6},{4,8},{6,10},{8,12},{10,14},{12,16},{1... | collective-permute-start | bytes 122888 | tf_op jit(solution)/shard_map/ppermute | solution.py:12
  191.8 7.1 %collective-permute-start.14 = (f32[1,80,128]{2,1,0:T(8,128)S(1)}, f32[1,80,128]{2,1,0:T(8,128)S(1)}, u32[]{:S(2)}, u32[]{:S(2)}) collective-permute-start(f32[1,80,128]{2,1,0:T(8,128)S(1)} %broadcast_select_fusion.5), channel_id=1, source_target_pairs={{120,0},{122,2},{124,4},{126,6},{0,8},{2,10},{4,12},{6,14},{8,16},... | collective-permute-start | bytes 122888 | tf_op jit(solution)/shard_map/ppermute | solution.py:12
  198.9 9.0 %collective-permute-start.15 = (f32[1,80,128]{2,1,0:T(8,128)S(1)}, f32[1,80,128]{2,1,0:T(8,128)S(1)}, u32[]{:S(2)}, u32[]{:S(2)}) collective-permute-start(f32[1,80,128]{2,1,0:T(8,128)S(1)} %broadcast_select_fusion.8), channel_id=1, source_target_pairs={{112,0},{114,2},{116,4},{118,6},{120,8},{122,10},{124,12},{126,14}... | collective-permute-start | bytes 122888 | tf_op jit(solution)/shard_map/ppermute | solution.py:12
  207.9 25.7 %copy-start.3 = (f32[1,1,1,320,80]{3,4,2,1,0:T(8,128)S(1)}, f32[1,1,1,320,80]{3,4,2,1,0:T(8,128)}, u32[]{:S(2)}) copy-start(f32[1,1,1,320,80]{3,4,2,1,0:T(8,128)} %param.10) | copy-start | bytes 307204
  207.9 11.0 %collective-permute-start.16 = (f32[1,80,128]{2,1,0:T(8,128)S(1)}, f32[1,80,128]{2,1,0:T(8,128)S(1)}, u32[]{:S(2)}, u32[]{:S(2)}) collective-permute-start(f32[1,80,128]{2,1,0:T(8,128)S(1)} %broadcast_select_fusion.11), channel_id=1, source_target_pairs={{96,0},{98,2},{100,4},{102,6},{104,8},{106,10},{108,12},{110,14},{... | collective-permute-start | bytes 122888 | tf_op jit(solution)/shard_map/ppermute | solution.py:12
  218.9 14.7 %collective-permute-start.17 = (f32[1,80,128]{2,1,0:T(8,128)S(1)}, f32[1,80,128]{2,1,0:T(8,128)S(1)}, u32[]{:S(2)}, u32[]{:S(2)}) collective-permute-start(f32[1,80,128]{2,1,0:T(8,128)S(1)} %broadcast_select_fusion.14), channel_id=1, source_target_pairs={{64,0},{66,2},{68,4},{70,6},{72,8},{74,10},{76,12},{78,14},{80,16}... | collective-permute-start | bytes 122888 | tf_op jit(solution)/shard_map/ppermute | solution.py:12
  234.3 6.8 %collective-permute-start.18 = (f32[1,80,128]{2,1,0:T(8,128)S(1)}, f32[1,80,128]{2,1,0:T(8,128)S(1)}, u32[]{:S(2)}, u32[]{:S(2)}) collective-permute-start(f32[1,80,128]{2,1,0:T(8,128)S(1)} %convolution_bitcast_fusion.12), channel_id=1, source_target_pairs={{0,128},{128,256},{256,384},{1,129},{129,257},{257,385},{2,130},{1... | collective-permute-start | bytes 122888 | tf_op jit(solution)/shard_map/ppermute | solution.py:18
  241.1 9.4 %collective-permute-start.19 = (f32[1,80,128]{2,1,0:T(8,128)S(1)}, f32[1,80,128]{2,1,0:T(8,128)S(1)}, u32[]{:S(2)}, u32[]{:S(2)}) collective-permute-start(f32[1,80,128]{2,1,0:T(8,128)S(1)} %collective-permute-done.18), channel_id=1, source_target_pairs={{126,0},{0,2},{2,4},{4,6},{6,8},{8,10},{10,12},{12,14},{14,16},{16... | collective-permute-start | bytes 122888 | tf_op jit(solution)/shard_map/ppermute | solution.py:12
  250.6 9.5 %collective-permute-start.20 = (f32[1,80,128]{2,1,0:T(8,128)S(1)}, f32[1,80,128]{2,1,0:T(8,128)S(1)}, u32[]{:S(2)}, u32[]{:S(2)}) collective-permute-start(f32[1,80,128]{2,1,0:T(8,128)S(1)} %broadcast_select_fusion.1), channel_id=1, source_target_pairs={{124,0},{126,2},{0,4},{2,6},{4,8},{6,10},{8,12},{10,14},{12,16},{1... | collective-permute-start | bytes 122888 | tf_op jit(solution)/shard_map/ppermute | solution.py:12
  260.1 7.5 %collective-permute-start.21 = (f32[1,80,128]{2,1,0:T(8,128)S(1)}, f32[1,80,128]{2,1,0:T(8,128)S(1)}, u32[]{:S(2)}, u32[]{:S(2)}) collective-permute-start(f32[1,80,128]{2,1,0:T(8,128)S(1)} %broadcast_select_fusion.4), channel_id=1, source_target_pairs={{120,0},{122,2},{124,4},{126,6},{0,8},{2,10},{4,12},{6,14},{8,16},... | collective-permute-start | bytes 122888 | tf_op jit(solution)/shard_map/ppermute | solution.py:12
  267.6 8.4 %collective-permute-start.22 = (f32[1,80,128]{2,1,0:T(8,128)S(1)}, f32[1,80,128]{2,1,0:T(8,128)S(1)}, u32[]{:S(2)}, u32[]{:S(2)}) collective-permute-start(f32[1,80,128]{2,1,0:T(8,128)S(1)} %broadcast_select_fusion.7), channel_id=1, source_target_pairs={{112,0},{114,2},{116,4},{118,6},{120,8},{122,10},{124,12},{126,14}... | collective-permute-start | bytes 122888 | tf_op jit(solution)/shard_map/ppermute | solution.py:12
  276.0 10.7 %collective-permute-start.23 = (f32[1,80,128]{2,1,0:T(8,128)S(1)}, f32[1,80,128]{2,1,0:T(8,128)S(1)}, u32[]{:S(2)}, u32[]{:S(2)}) collective-permute-start(f32[1,80,128]{2,1,0:T(8,128)S(1)} %broadcast_select_fusion.10), channel_id=1, source_target_pairs={{96,0},{98,2},{100,4},{102,6},{104,8},{106,10},{108,12},{110,14},{... | collective-permute-start | bytes 122888 | tf_op jit(solution)/shard_map/ppermute | solution.py:12
  286.7 14.9 %collective-permute-start.24 = (f32[1,80,128]{2,1,0:T(8,128)S(1)}, f32[1,80,128]{2,1,0:T(8,128)S(1)}, u32[]{:S(2)}, u32[]{:S(2)}) collective-permute-start(f32[1,80,128]{2,1,0:T(8,128)S(1)} %broadcast_select_fusion.13), channel_id=1, source_target_pairs={{64,0},{66,2},{68,4},{70,6},{72,8},{74,10},{76,12},{78,14},{80,16}... | collective-permute-start | bytes 122888 | tf_op jit(solution)/shard_map/ppermute | solution.py:12
  302.3 6.8 %collective-permute-start.25 = (f32[1,80,128]{2,1,0:T(8,128)S(1)}, f32[1,80,128]{2,1,0:T(8,128)S(1)}, u32[]{:S(2)}, u32[]{:S(2)}) collective-permute-start(f32[1,80,128]{2,1,0:T(8,128)S(1)} %convolution_bitcast_fusion.11), channel_id=1, source_target_pairs={{0,128},{128,256},{256,384},{1,129},{129,257},{257,385},{2,130},{1... | collective-permute-start | bytes 122888 | tf_op jit(solution)/shard_map/ppermute | solution.py:18
  309.2 9.4 %collective-permute-start.26 = (f32[1,80,128]{2,1,0:T(8,128)S(1)}, f32[1,80,128]{2,1,0:T(8,128)S(1)}, u32[]{:S(2)}, u32[]{:S(2)}) collective-permute-start(f32[1,80,128]{2,1,0:T(8,128)S(1)} %collective-permute-done.25), channel_id=1, source_target_pairs={{126,0},{0,2},{2,4},{4,6},{6,8},{8,10},{10,12},{12,14},{14,16},{16... | collective-permute-start | bytes 122888 | tf_op jit(solution)/shard_map/ppermute | solution.py:12
  318.6 9.5 %collective-permute-start.27 = (f32[1,80,128]{2,1,0:T(8,128)S(1)}, f32[1,80,128]{2,1,0:T(8,128)S(1)}, u32[]{:S(2)}, u32[]{:S(2)}) collective-permute-start(f32[1,80,128]{2,1,0:T(8,128)S(1)} %broadcast_select_fusion), channel_id=1, source_target_pairs={{124,0},{126,2},{0,4},{2,6},{4,8},{6,10},{8,12},{10,14},{12,16},{1... | collective-permute-start | bytes 122888 | tf_op jit(solution)/shard_map/ppermute | solution.py:12
  328.1 7.5 %collective-permute-start.28 = (f32[1,80,128]{2,1,0:T(8,128)S(1)}, f32[1,80,128]{2,1,0:T(8,128)S(1)}, u32[]{:S(2)}, u32[]{:S(2)}) collective-permute-start(f32[1,80,128]{2,1,0:T(8,128)S(1)} %broadcast_select_fusion.3), channel_id=1, source_target_pairs={{120,0},{122,2},{124,4},{126,6},{0,8},{2,10},{4,12},{6,14},{8,16},... | collective-permute-start | bytes 122888 | tf_op jit(solution)/shard_map/ppermute | solution.py:12
  335.6 8.4 %collective-permute-start.29 = (f32[1,80,128]{2,1,0:T(8,128)S(1)}, f32[1,80,128]{2,1,0:T(8,128)S(1)}, u32[]{:S(2)}, u32[]{:S(2)}) collective-permute-start(f32[1,80,128]{2,1,0:T(8,128)S(1)} %broadcast_select_fusion.6), channel_id=1, source_target_pairs={{112,0},{114,2},{116,4},{118,6},{120,8},{122,10},{124,12},{126,14}... | collective-permute-start | bytes 122888 | tf_op jit(solution)/shard_map/ppermute | solution.py:12
  344.0 10.2 %collective-permute-start.30 = (f32[1,80,128]{2,1,0:T(8,128)S(1)}, f32[1,80,128]{2,1,0:T(8,128)S(1)}, u32[]{:S(2)}, u32[]{:S(2)}) collective-permute-start(f32[1,80,128]{2,1,0:T(8,128)S(1)} %broadcast_select_fusion.9), channel_id=1, source_target_pairs={{96,0},{98,2},{100,4},{102,6},{104,8},{106,10},{108,12},{110,14},{... | collective-permute-start | bytes 122888 | tf_op jit(solution)/shard_map/ppermute | solution.py:12
  354.2 14.6 %collective-permute-start.31 = (f32[1,80,128]{2,1,0:T(8,128)S(1)}, f32[1,80,128]{2,1,0:T(8,128)S(1)}, u32[]{:S(2)}, u32[]{:S(2)}) collective-permute-start(f32[1,80,128]{2,1,0:T(8,128)S(1)} %broadcast_select_fusion.12), channel_id=1, source_target_pairs={{64,0},{66,2},{68,4},{70,6},{72,8},{74,10},{76,12},{78,14},{80,16}... | collective-permute-start | bytes 122888 | tf_op jit(solution)/shard_map/ppermute | solution.py:12
  369.3 0.9 copy-start.4
where the time goes:
time: 371 us; the launch traced here: 370 us
  waiting for transfers between devices  257 us (69%)
  starting transfers between devices  94.5 us (25%)
  matrix products  13.1 us (4%)
  between operations  3.94 us (1%)
    ppermute x29, waiting for transfers between devices, from_behind(): return lax.ppermute(block, axis, route)  242 us
    ppermute x29, starting transfers between devices, from_behind(): return lax.ppermute(block, axis, route)  88.8 us
    ppermute x3, waiting for transfers between devices, from_behind_2(): lax.ppermute(value, axis, [(source, source + steps) for source in range(l...  14.7 us
  transfers between devices with their start and end apart: 32, of which 30 were waited for; matrix products, arithmetic and copies ran while one was open for 2% of the time, Pallas kernels for 0%

commit v1 on v0

v1 whole, which is shorter than its diff:
```python
import jax
import jax.numpy as jnp
from jax import lax
from jax.sharding import PartitionSpec as P

HIGH = lax.Precision.HIGHEST
FINE = 4


def from_behind(block, axis, distance):
    devices = range(lax.axis_size(axis))
    route = [((i - distance) % len(devices), i) for i in devices]
    return lax.ppermute(block, axis, route)


def apply_block(matrix, state):
    return jnp.einsum("ij,bjl->bil", matrix, state, precision=HIGH)


def hop_down(trace, rows, sectors, step):
    route = [
        (row * sectors + s, (row + 1) * sectors + (s + step) % sectors)
        for row in range(rows - 1)
        for s in range(sectors)
    ]
    return lax.ppermute(trace, ("row", "sector"), route)


def turn(trace, rows, sectors, step):
    if step == 0:
        return trace
    route = [
        (row * sectors + s, row * sectors + (s + step) % sectors)
        for row in range(1, rows)
        for s in range(sectors)
    ]
    return lax.ppermute(trace, ("row", "sector"), route)


def cross(trace, shift, rows, sectors):
    fine = [lambda t, k=k: hop_down(t, rows, sectors, k) for k in range(FINE)]
    coarse = [lambda t, k=k: turn(t, rows, sectors, k) for k in range(0, sectors, FINE)]
    trace = lax.switch(shift % FINE, fine, trace)
    return lax.switch(shift // FINE, coarse, trace)


def on_device(residual, block_inverse, cycle_coupling, outlet_flux, inlet_lift, mortar_shift):
    res_local = residual[0, 0]
    inverse = block_inverse[0, 0]
    coupling = cycle_coupling[0, 0]
    flux = outlet_flux[0, 0, 0]
    lift = inlet_lift[0, 0, 0]
    source = jnp.einsum("bij,bjl->bil", inverse, res_local, precision=HIGH)
    sectors = lax.axis_size("sector")
    levels = sectors.bit_length() - 1
    matrix = coupling
    state = source
    for level in range(levels):
        if level + 1 < levels:
            prev_matrix, prev_state = from_behind((matrix, state), "sector", 2**level)
            state = state + apply_block(matrix, prev_state)
            matrix = jnp.dot(matrix, prev_matrix, precision=HIGH)
        else:
            prev_state = from_behind(state, "sector", 2**level)
            state = state + apply_block(matrix, prev_state)
    state = state[0]
    rows = lax.axis_size("row")
    row_index = lax.axis_index("row")
    shifts = jnp.remainder(mortar_shift, sectors)
    gain = jnp.dot(flux, lift, precision=HIGH)
    base = jnp.dot(flux, state, precision=HIGH)
    trace = base
    inlet = jnp.zeros_like(base)
    for section in range(1, rows):
        moved = cross(trace, shifts[section - 1], rows, sectors)
        inlet = jnp.where(row_index == section, moved, inlet)
        trace = base + jnp.dot(gain, inlet, precision=HIGH)
    current = state + jnp.dot(lift, inlet, precision=HIGH)
    return (current[None, None, None], trace[None, None, None])


def solution(mesh):
    in_specs = (
        P("row", "sector", "band", None, None),
        P("row", "sector", "band", None, None),
        P("row", "sector", None, None),
        P("row", "sector", "band", None, None),
        P("row", "sector", "band", None, None),
        P(),
    )
    out_specs = (P("row", "sector", "band", None, None), P("row", "sector", "band", None, None))
    return jax.shard_map(
        on_device, mesh=mesh, in_specs=in_specs, out_specs=out_specs, check_vma=False
    )
```

time: 371 us -> 233 us (0.63)
  waiting for transfers between devices: 257 us -> 131 us
  starting transfers between devices: 94.5 us -> 78.6 us
  between operations: 3.94 us -> 8.72 us
    ppermute x29 -> x11, waiting for transfers between devices: 242 us -> 95.8 us  [from_behind(): return lax.ppermute(block, axis, route)]
    ppermute x29 -> x11, starting transfers between devices: 88.8 us -> 33.7 us  [from_behind(): return lax.ppermute(block, axis, route)]
    ppermute x3 -> x6, starting transfers between devices: 5.76 us -> 44.9 us  [the longest x3 28.7 us: turn(): return lax.ppermute(trace, ('row', 'sector'), route)]
    ppermute x3 -> x6, waiting for transfers between devices: 14.7 us -> 34.9 us  [the longest x3 21 us: hop_down(): return lax.ppermute(trace, ('row', 'sector'), route)]
  transfers between devices with their start and end apart: 32 -> 17, of which waited for: 30 -> 14; matrix products, arithmetic and copies ran while one was open for 2% -> 4% of each run, Pallas kernels for 0% -> 0%
where the time goes in v1:
time: 233 us; the launch traced here: 235 us
  waiting for transfers between devices  131 us (56%)
  starting transfers between devices  78.6 us (34%)
  matrix products  12.9 us (6%)
  between operations  8.72 us (4%)
  local copies, waits for them, and re-layouts  3.48 us (1%)
    ppermute x11, waiting for transfers between devices, from_behind(): return lax.ppermute(block, axis, route)  95.8 us
    ppermute x11, starting transfers between devices, from_behind(): return lax.ppermute(block, axis, route)  33.7 us
    ppermute x3, starting transfers between devices, turn(): return lax.ppermute(trace, ('row', 'sector'), route)  28.7 us
    ppermute x3, waiting for transfers between devices, hop_down(): return lax.ppermute(trace, ('row', 'sector'), route)  21 us
    ppermute x3, starting transfers between devices, hop_down(): return lax.ppermute(trace, ('row', 'sector'), route)  16.3 us
    ppermute x3, waiting for transfers between devices, turn(): return lax.ppermute(trace, ('row', 'sector'), route)  13.9 us
    dot_general x5, matrix products, on_device(): matrix = jnp.dot(matrix, prev_matrix, precision=HIGH)  5.4 us
  transfers between devices with their start and end apart: 17, of which 14 were waited for; matrix products, arithmetic and copies ran while one was open for 4% of the time, Pallas kernels for 0%

profile of v1, /device:TPU:24, one launch (start us, length us, event | category | flops | bytes accessed | tf_op | source)
XLA Modules:
  0.0 235.3 jit_solution(4803909238976879043)
XLA Ops:
  0.7 1.0 copy-done
  1.7 1.5 convolution_bitcast_fusion.6
  3.1 3.4 %collective-permute-start.57 = (f32[1,320,128]{2,1,0:T(8,128)S(1)}, f32[1,320,128]{2,1,0:T(8,128)S(1)}, u32[]{:S(2)}, u32[]{:S(2)}) collective-permute-start(f32[1,320,128]{2,1,0:T(8,128)S(1)} %convolution_bitcast_fusion.6), channel_id=1, source_target_pairs={{126,0},{0,2},{2,4},{4,6},{6,8},{8,10},{10,12},{12,14},{14,16},{16... | collective-permute-start | bytes 491528 | tf_op jit(solution)/shard_map/ppermute | solution.py:13
  6.5 3.4 %collective-permute-start.59 = (f32[320,320]{1,0:T(8,128)S(1)}, f32[320,320]{1,0:T(8,128)S(1)}, u32[]{:S(2)}, u32[]{:S(2)}) collective-permute-start(f32[320,320]{1,0:T(8,128)S(1)} %bitcast.115), channel_id=1, source_target_pairs={{126,0},{0,2},{2,4},{4,6},{6,8},{8,10},{10,12},{12,14},{14,16},{16... | collective-permute-start | bytes 1228808 | tf_op jit(solution)/shard_map/ppermute | solution.py:13
  10.0 11.8 %collective-permute-done.57 = f32[1,320,128]{2,1,0:T(8,128)S(1)} collective-permute-done((f32[1,320,128]{2,1,0:T(8,128)S(1)}, f32[1,320,128]{2,1,0:T(8,128)S(1)}, u32[]{:S(2)}, u32[]{:S(2)}) %collective-permute-start.57) | collective-permute-done | bytes 163872 | tf_op jit(solution)/shard_map/ppermute | solution.py:13
  22.3 1.9 collective-permute-start.58
  24.2 9.5 %collective-permute-done.59 = f32[320,320]{1,0:T(8,128)S(1)} collective-permute-done((f32[320,320]{1,0:T(8,128)S(1)}, f32[320,320]{1,0:T(8,128)S(1)}, u32[]{:S(2)}, u32[]{:S(2)}) %collective-permute-start.59) | collective-permute-done | bytes 409632 | tf_op jit(solution)/shard_map/ppermute | solution.py:13
  33.8 1.1 fusion.27
  34.9 1.9 collective-permute-start.61
  37.3 1.9 collective-permute-start.60
  39.3 14.1 %collective-permute-done.61 = f32[320,320]{1,0:T(8,128)S(1)} collective-permute-done((f32[320,320]{1,0:T(8,128)S(1)}, f32[320,320]{1,0:T(8,128)S(1)}, u32[]{:S(2)}, u32[]{:S(2)}) %collective-permute-start.61) | collective-permute-done | bytes 409632 | tf_op jit(solution)/shard_map/ppermute | solution.py:13
  53.4 1.1 fusion.32
  54.5 1.9 collective-permute-start.63
  57.0 1.9 collective-permute-start.62
  58.9 15.5 %collective-permute-done.63 = f32[320,320]{1,0:T(8,128)S(1)} collective-permute-done((f32[320,320]{1,0:T(8,128)S(1)}, f32[320,320]{1,0:T(8,128)S(1)}, u32[]{:S(2)}, u32[]{:S(2)}) %collective-permute-start.63) | collective-permute-done | bytes 409632 | tf_op jit(solution)/shard_map/ppermute | solution.py:13
  74.4 1.1 fusion.33
  75.5 1.9 collective-permute-start.65
  77.5 0.6 fusion.31
  86.4 2.6 %collective-permute-start.64 = (f32[1,320,128]{2,1,0:T(8,128)S(1)}, f32[1,320,128]{2,1,0:T(8,128)S(1)}, u32[]{:S(2)}, u32[]{:S(2)}) collective-permute-start(f32[1,320,128]{2,1,0:T(8,128)S(1)} %fusion.5), channel_id=1, source_target_pairs={{96,0},{98,2},{100,4},{102,6},{104,8},{106,10},{108,12},{110,14},{... | collective-permute-start | bytes 491528 | tf_op jit(solution)/shard_map/ppermute | solution.py:13
  89.0 18.4 %collective-permute-done.65 = f32[320,320]{1,0:T(8,128)S(1)} collective-permute-done((f32[320,320]{1,0:T(8,128)S(1)}, f32[320,320]{1,0:T(8,128)S(1)}, u32[]{:S(2)}, u32[]{:S(2)}) %collective-permute-start.65) | collective-permute-done | bytes 409632 | tf_op jit(solution)/shard_map/ppermute | solution.py:13
  107.4 1.1 fusion.34
  108.5 1.9 collective-permute-start.67
  110.7 2.4 %collective-permute-done.64 = f32[1,320,128]{2,1,0:T(8,128)S(1)} collective-permute-done((f32[1,320,128]{2,1,0:T(8,128)S(1)}, f32[1,320,128]{2,1,0:T(8,128)S(1)}, u32[]{:S(2)}, u32[]{:S(2)}) %collective-permute-start.64) | collective-permute-done | bytes 163872 | tf_op jit(solution)/shard_map/ppermute | solution.py:13
  113.6 10.9 %collective-permute-start.66 = (f32[1,320,128]{2,1,0:T(8,128)S(1)}, f32[1,320,128]{2,1,0:T(8,128)S(1)}, u32[]{:S(2)}, u32[]{:S(2)}) collective-permute-start(f32[1,320,128]{2,1,0:T(8,128)S(1)} %fusion.6), channel_id=1, source_target_pairs={{64,0},{66,2},{68,4},{70,6},{72,8},{74,10},{76,12},{78,14},{80,16}... | collective-permute-start | bytes 491528 | tf_op jit(solution)/shard_map/ppermute | solution.py:13
  124.5 15.0 %collective-permute-done.67 = f32[320,320]{1,0:T(8,128)S(1)} collective-permute-done((f32[320,320]{1,0:T(8,128)S(1)}, f32[320,320]{1,0:T(8,128)S(1)}, u32[]{:S(2)}, u32[]{:S(2)}) %collective-permute-start.67) | collective-permute-done | bytes 409632 | tf_op jit(solution)/shard_map/ppermute | solution.py:13
  139.5 1.1 fusion.35
  140.5 9.1 %collective-permute-done.66 = f32[1,320,128]{2,1,0:T(8,128)S(1)} collective-permute-done((f32[1,320,128]{2,1,0:T(8,128)S(1)}, f32[1,320,128]{2,1,0:T(8,128)S(1)}, u32[]{:S(2)}, u32[]{:S(2)}) %collective-permute-start.66) | collective-permute-done | bytes 163872 | tf_op jit(solution)/shard_map/ppermute | solution.py:13
  150.5 15.9 %conditional.6 = (f32[80,128]{1,0:T(8,128)}) conditional(s32[]{:T(128)} %clamp.23, f32[80,128]{1,0:T(8,128)S(1)} %convolution_bitcast_fusion.8, f32[80,128]{1,0:T(8,128)S(1)} %convolution_bitcast_fusion.8, f32[80,128]{1,0:T(8,128)S(1)} %convolution_bitcast_fusion.8, f32[80,128]{1,0:T(8,128)S(1)} %convolution_bitcast_fusion.8), branch_computations={%region_0.1_spmd, %region_1.2_spmd, %region_2.3_spmd, %region_3.4_... | conditional | bytes 163888 | solution.py:43
  150.5 12.4 %collective-permute-start.2 = (f32[80,128]{1,0:T(8,128)S(1)}, f32[80,128]{1,0:T(8,128)}, u32[]{:S(2)}, u32[]{:S(2)}) collective-permute-start(f32[80,128]{1,0:T(8,128)S(1)} %param.2), channel_id=1, source_target_pairs={{0,132},{2,134},{4,136},{6,138},{8,140},{10,142},{12,144},{14,146}... | collective-permute-start | bytes 122888 | tf_op jit(solution)/shard_map/cond/branch_2_fun/ppermute | solution.py:26
  162.9 3.5 %collective-permute-done.2 = f32[80,128]{1,0:T(8,128)} collective-permute-done((f32[80,128]{1,0:T(8,128)S(1)}, f32[80,128]{1,0:T(8,128)}, u32[]{:S(2)}, u32[]{:S(2)}) %collective-permute-start.2) | collective-permute-done | bytes 40992 | tf_op jit(solution)/shard_map/cond/branch_2_fun/ppermute | solution.py:26
  166.4 18.6 %conditional.7 = (f32[80,128]{1,0:T(8,128)}) conditional(s32[]{:T(128)} %clamp.22, f32[80,128]{1,0:T(8,128)} %get-tuple-element.131, f32[80,128]{1,0:T(8,128)} %get-tuple-element.131, f32[80,128]{1,0:T(8,128)} %get-tuple-element.131, f32[80,128]{1,0:T(8,128)} %get-tuple-element.131, ...), branch_computations={%region_4.5_spmd, %region_5.6_spmd, %region_6.7_spmd, %region_7.8_... | conditional | bytes 245808 | solution.py:44
  166.4 15.6 %collective-permute-start.4 = (f32[80,128]{1,0:T(8,128)}, f32[80,128]{1,0:T(8,128)S(1)}, u32[]{:S(2)}, u32[]{:S(2)}) collective-permute-start(f32[80,128]{1,0:T(8,128)} %param.5), channel_id=1, source_target_pairs={{128,136},{130,138},{132,140},{134,142},{136,144},{138,146},{140,1... | collective-permute-start | bytes 122888 | tf_op jit(solution)/shard_map/cond/branch_1_fun/ppermute | solution.py:37
  182.0 2.4 %collective-permute-done.4 = f32[80,128]{1,0:T(8,128)S(1)} collective-permute-done((f32[80,128]{1,0:T(8,128)}, f32[80,128]{1,0:T(8,128)S(1)}, u32[]{:S(2)}, u32[]{:S(2)}) %collective-permute-start.4) | collective-permute-done | bytes 40992 | tf_op jit(solution)/shard_map/cond/branch_1_fun/ppermute | solution.py:37
  185.2 11.5 %conditional.8 = (f32[80,128]{1,0:T(8,128)}) conditional(s32[]{:T(128)} %clamp.21, f32[80,128]{1,0:T(8,128)S(1)} %convolution_add_fusion.2, f32[80,128]{1,0:T(8,128)S(1)} %convolution_add_fusion.2, f32[80,128]{1,0:T(8,128)S(1)} %convolution_add_fusion.2, f32[80,128]{1,0:T(8,128)S(1)} %convolution_add_fusion.2), branch_computations={%region_20.21_spmd, %region_21.22_spmd, %region_22.23_spmd, %regio... | conditional | bytes 163888 | solution.py:43
  185.2 1.9 collective-permute-start.21
  187.2 9.5 %collective-permute-done.21 = f32[80,128]{1,0:T(8,128)} collective-permute-done((f32[80,128]{1,0:T(8,128)S(1)}, f32[80,128]{1,0:T(8,128)}, u32[]{:S(2)}, u32[]{:S(2)}) %collective-permute-start.21) | collective-permute-done | bytes 40992 | tf_op jit(solution)/shard_map/cond/branch_2_fun/ppermute | solution.py:26
  196.7 13.4 %conditional.9 = (f32[80,128]{1,0:T(8,128)}) conditional(s32[]{:T(128)} %clamp.20, f32[80,128]{1,0:T(8,128)} %get-tuple-element.133, f32[80,128]{1,0:T(8,128)} %get-tuple-element.133, f32[80,128]{1,0:T(8,128)} %get-tuple-element.133, f32[80,128]{1,0:T(8,128)} %get-tuple-element.133, ...), branch_computations={%region_24.25_spmd, %region_25.26_spmd, %region_26.27_spmd, %regio... | conditional | bytes 245808 | solution.py:44
  196.7 8.8 %collective-permute-start.34 = (f32[80,128]{1,0:T(8,128)}, f32[80,128]{1,0:T(8,128)S(1)}, u32[]{:S(2)}, u32[]{:S(2)}) collective-permute-start(f32[80,128]{1,0:T(8,128)} %param.36), channel_id=1, source_target_pairs={{128,224},{130,226},{132,228},{134,230},{136,232},{138,234},{140,2... | collective-permute-start | bytes 122888 | tf_op jit(solution)/shard_map/cond/branch_12_fun/ppermute | solution.py:37
  205.5 4.0 %collective-permute-done.34 = f32[80,128]{1,0:T(8,128)S(1)} collective-permute-done((f32[80,128]{1,0:T(8,128)}, f32[80,128]{1,0:T(8,128)S(1)}, u32[]{:S(2)}, u32[]{:S(2)}) %collective-permute-start.34) | collective-permute-done | bytes 40992 | tf_op jit(solution)/shard_map/cond/branch_12_fun/ppermute | solution.py:37
  210.1 0.8 select_select_fusion
  211.0 10.0 %conditional.10 = (f32[80,128]{1,0:T(8,128)}) conditional(s32[]{:T(128)} %clamp.19, f32[80,128]{1,0:T(8,128)S(1)} %convolution_add_fusion.1, f32[80,128]{1,0:T(8,128)S(1)} %convolution_add_fusion.1, f32[80,128]{1,0:T(8,128)S(1)} %convolution_add_fusion.1, f32[80,128]{1,0:T(8,128)S(1)} %convolution_add_fusion.1), branch_computations={%region_40.41_spmd, %region_41.42_spmd, %region_42.43_spmd, %regio... | conditional | bytes 163888 | solution.py:43
  211.1 1.9 collective-permute-start.41
  213.0 8.0 %collective-permute-done.41 = f32[80,128]{1,0:T(8,128)} collective-permute-done((f32[80,128]{1,0:T(8,128)S(1)}, f32[80,128]{1,0:T(8,128)}, u32[]{:S(2)}, u32[]{:S(2)}) %collective-permute-start.41) | collective-permute-done | bytes 40992 | tf_op jit(solution)/shard_map/cond/branch_3_fun/ppermute | solution.py:26
  221.0 12.4 %conditional.11 = (f32[80,128]{1,0:T(8,128)}) conditional(s32[]{:T(128)} %clamp.18, f32[80,128]{1,0:T(8,128)} %get-tuple-element.135, f32[80,128]{1,0:T(8,128)} %get-tuple-element.135, f32[80,128]{1,0:T(8,128)} %get-tuple-element.135, f32[80,128]{1,0:T(8,128)} %get-tuple-element.135, ...), branch_computations={%region_44.45_spmd, %region_45.46_spmd, %region_46.47_spmd, %regio... | conditional | bytes 245808 | solution.py:44
  221.0 4.3 %collective-permute-start.51 = (f32[80,128]{1,0:T(8,128)}, f32[80,128]{1,0:T(8,128)S(1)}, u32[]{:S(2)}, u32[]{:S(2)}) collective-permute-start(f32[80,128]{1,0:T(8,128)} %param.54), channel_id=1, source_target_pairs={{128,208},{130,210},{132,212},{134,214},{136,216},{138,218},{140,2... | collective-permute-start | bytes 122888 | tf_op jit(solution)/shard_map/cond/branch_10_fun/ppermute | solution.py:37
  225.3 7.5 %collective-permute-done.51 = f32[80,128]{1,0:T(8,128)S(1)} collective-permute-done((f32[80,128]{1,0:T(8,128)}, f32[80,128]{1,0:T(8,128)S(1)}, u32[]{:S(2)}, u32[]{:S(2)}) %collective-permute-start.51) | collective-permute-done | bytes 40992 | tf_op jit(solution)/shard_map/cond/branch_10_fun/ppermute | solution.py:37
  233.4 1.1 fusion.1
  234.5 0.8 fusion.9
  (26 shorter events, 6.0 us)
Async XLA Ops:
  0.6 1.0 copy-start
  0.6 5.9 %copy-start.1 = (f32[1,1,320,320]{3,2,1,0:T(8,128)S(1)}, f32[1,1,320,320]{3,2,1,0:T(8,128)}, u32[]{:S(2)}) copy-start(f32[1,1,320,320]{3,2,1,0:T(8,128)} %param.68) | copy-start | bytes 1228804
  3.1 18.6 %collective-permute-start.57 = (f32[1,320,128]{2,1,0:T(8,128)S(1)}, f32[1,320,128]{2,1,0:T(8,128)S(1)}, u32[]{:S(2)}, u32[]{:S(2)}) collective-permute-start(f32[1,320,128]{2,1,0:T(8,128)S(1)} %convolution_bitcast_fusion.6), channel_id=1, source_target_pairs={{126,0},{0,2},{2,4},{4,6},{6,8},{8,10},{10,12},{12,14},{14,16},{16... | collective-permute-start | bytes 491528 | tf_op jit(solution)/shard_map/ppermute | solution.py:13
  6.5 27.2 %collective-permute-start.59 = (f32[320,320]{1,0:T(8,128)S(1)}, f32[320,320]{1,0:T(8,128)S(1)}, u32[]{:S(2)}, u32[]{:S(2)}) collective-permute-start(f32[320,320]{1,0:T(8,128)S(1)} %bitcast.115), channel_id=1, source_target_pairs={{126,0},{0,2},{2,4},{4,6},{6,8},{8,10},{10,12},{12,14},{14,16},{16... | collective-permute-start | bytes 1228808 | tf_op jit(solution)/shard_map/ppermute | solution.py:13
  22.3 14.5 %collective-permute-start.58 = (f32[1,320,128]{2,1,0:T(8,128)S(1)}, f32[1,320,128]{2,1,0:T(8,128)S(1)}, u32[]{:S(2)}, u32[]{:S(2)}) collective-permute-start(f32[1,320,128]{2,1,0:T(8,128)S(1)} %fusion.2), channel_id=1, source_target_pairs={{124,0},{126,2},{0,4},{2,6},{4,8},{6,10},{8,12},{10,14},{12,16},{1... | collective-permute-start | bytes 491528 | tf_op jit(solution)/shard_map/ppermute | solution.py:13
  34.9 18.5 %collective-permute-start.61 = (f32[320,320]{1,0:T(8,128)S(1)}, f32[320,320]{1,0:T(8,128)S(1)}, u32[]{:S(2)}, u32[]{:S(2)}) collective-permute-start(f32[320,320]{1,0:T(8,128)S(1)} %fusion.27), channel_id=1, source_target_pairs={{124,0},{126,2},{0,4},{2,6},{4,8},{6,10},{8,12},{10,14},{12,16},{1... | collective-permute-start | bytes 1228808 | tf_op jit(solution)/shard_map/ppermute | solution.py:13
  37.3 19.1 %collective-permute-start.60 = (f32[1,320,128]{2,1,0:T(8,128)S(1)}, f32[1,320,128]{2,1,0:T(8,128)S(1)}, u32[]{:S(2)}, u32[]{:S(2)}) collective-permute-start(f32[1,320,128]{2,1,0:T(8,128)S(1)} %fusion.3), channel_id=1, source_target_pairs={{120,0},{122,2},{124,4},{126,6},{0,8},{2,10},{4,12},{6,14},{8,16},... | collective-permute-start | bytes 491528 | tf_op jit(solution)/shard_map/ppermute | solution.py:13
  54.5 19.9 %collective-permute-start.63 = (f32[320,320]{1,0:T(8,128)S(1)}, f32[320,320]{1,0:T(8,128)S(1)}, u32[]{:S(2)}, u32[]{:S(2)}) collective-permute-start(f32[320,320]{1,0:T(8,128)S(1)} %fusion.32), channel_id=1, source_target_pairs={{120,0},{122,2},{124,4},{126,6},{0,8},{2,10},{4,12},{6,14},{8,16},... | collective-permute-start | bytes 1228808 | tf_op jit(solution)/shard_map/ppermute | solution.py:13
  57.0 20.5 %copy-start.4 = (s32[3]{0:T(128)S(1)}, s32[3]{0:T(128)}, u32[]{:S(2)}) copy-start(s32[3]{0:T(128)} %param.71) | copy-start | bytes 40
  57.0 28.9 %collective-permute-start.62 = (f32[1,320,128]{2,1,0:T(8,128)S(1)}, f32[1,320,128]{2,1,0:T(8,128)S(1)}, u32[]{:S(2)}, u32[]{:S(2)}) collective-permute-start(f32[1,320,128]{2,1,0:T(8,128)S(1)} %fusion.4), channel_id=1, source_target_pairs={{112,0},{114,2},{116,4},{118,6},{120,8},{122,10},{124,12},{126,14}... | collective-permute-start | bytes 491528 | tf_op jit(solution)/shard_map/ppermute | solution.py:13
  75.5 31.9 %collective-permute-start.65 = (f32[320,320]{1,0:T(8,128)S(1)}, f32[320,320]{1,0:T(8,128)S(1)}, u32[]{:S(2)}, u32[]{:S(2)}) collective-permute-start(f32[320,320]{1,0:T(8,128)S(1)} %fusion.33), channel_id=1, source_target_pairs={{112,0},{114,2},{116,4},{118,6},{120,8},{122,10},{124,12},{126,14}... | collective-permute-start | bytes 1228808 | tf_op jit(solution)/shard_map/ppermute | solution.py:13
  86.4 24.0 %copy-start.2 = (f32[1,1,1,80,320]{4,3,2,1,0:T(8,128)S(1)}, f32[1,1,1,80,320]{4,3,2,1,0:T(8,128)}, u32[]{:S(2)}) copy-start(f32[1,1,1,80,320]{4,3,2,1,0:T(8,128)} %param.69) | copy-start | bytes 307204
  86.4 24.0 %copy-start.3 = (f32[1,1,1,320,80]{3,4,2,1,0:T(8,128)S(1)}, f32[1,1,1,320,80]{3,4,2,1,0:T(8,128)}, u32[]{:S(2)}) copy-start(f32[1,1,1,320,80]{3,4,2,1,0:T(8,128)} %param.70) | copy-start | bytes 307204
  86.4 26.6 %collective-permute-start.64 = (f32[1,320,128]{2,1,0:T(8,128)S(1)}, f32[1,320,128]{2,1,0:T(8,128)S(1)}, u32[]{:S(2)}, u32[]{:S(2)}) collective-permute-start(f32[1,320,128]{2,1,0:T(8,128)S(1)} %fusion.5), channel_id=1, source_target_pairs={{96,0},{98,2},{100,4},{102,6},{104,8},{106,10},{108,12},{110,14},{... | collective-permute-start | bytes 491528 | tf_op jit(solution)/shard_map/ppermute | solution.py:13
  108.5 31.0 %collective-permute-start.67 = (f32[320,320]{1,0:T(8,128)S(1)}, f32[320,320]{1,0:T(8,128)S(1)}, u32[]{:S(2)}, u32[]{:S(2)}) collective-permute-start(f32[320,320]{1,0:T(8,128)S(1)} %fusion.34), channel_id=1, source_target_pairs={{96,0},{98,2},{100,4},{102,6},{104,8},{106,10},{108,12},{110,14},{... | collective-permute-start | bytes 1228808 | tf_op jit(solution)/shard_map/ppermute | solution.py:13
  113.6 36.1 %collective-permute-start.66 = (f32[1,320,128]{2,1,0:T(8,128)S(1)}, f32[1,320,128]{2,1,0:T(8,128)S(1)}, u32[]{:S(2)}, u32[]{:S(2)}) collective-permute-start(f32[1,320,128]{2,1,0:T(8,128)S(1)} %fusion.6), channel_id=1, source_target_pairs={{64,0},{66,2},{68,4},{70,6},{72,8},{74,10},{76,12},{78,14},{80,16}... | collective-permute-start | bytes 491528 | tf_op jit(solution)/shard_map/ppermute | solution.py:13
  150.5 15.9 %collective-permute-start.2 = (f32[80,128]{1,0:T(8,128)S(1)}, f32[80,128]{1,0:T(8,128)}, u32[]{:S(2)}, u32[]{:S(2)}) collective-permute-start(f32[80,128]{1,0:T(8,128)S(1)} %param.2), channel_id=1, source_target_pairs={{0,132},{2,134},{4,136},{6,138},{8,140},{10,142},{12,144},{14,146}... | collective-permute-start | bytes 122888 | tf_op jit(solution)/shard_map/cond/branch_2_fun/ppermute | solution.py:26
  166.4 18.0 %collective-permute-start.4 = (f32[80,128]{1,0:T(8,128)}, f32[80,128]{1,0:T(8,128)S(1)}, u32[]{:S(2)}, u32[]{:S(2)}) collective-permute-start(f32[80,128]{1,0:T(8,128)} %param.5), channel_id=1, source_target_pairs={{128,136},{130,138},{132,140},{134,142},{136,144},{138,146},{140,1... | collective-permute-start | bytes 122888 | tf_op jit(solution)/shard_map/cond/branch_1_fun/ppermute | solution.py:37
  185.2 11.4 %collective-permute-start.21 = (f32[80,128]{1,0:T(8,128)S(1)}, f32[80,128]{1,0:T(8,128)}, u32[]{:S(2)}, u32[]{:S(2)}) collective-permute-start(f32[80,128]{1,0:T(8,128)S(1)} %param.22), channel_id=1, source_target_pairs={{0,132},{2,134},{4,136},{6,138},{8,140},{10,142},{12,144},{14,146}... | collective-permute-start | bytes 122888 | tf_op jit(solution)/shard_map/cond/branch_2_fun/ppermute | solution.py:26
  196.7 12.8 %collective-permute-start.34 = (f32[80,128]{1,0:T(8,128)}, f32[80,128]{1,0:T(8,128)S(1)}, u32[]{:S(2)}, u32[]{:S(2)}) collective-permute-start(f32[80,128]{1,0:T(8,128)} %param.36), channel_id=1, source_target_pairs={{128,224},{130,226},{132,228},{134,230},{136,232},{138,234},{140,2... | collective-permute-start | bytes 122888 | tf_op jit(solution)/shard_map/cond/branch_12_fun/ppermute | solution.py:37
  211.1 9.9 %collective-permute-start.41 = (f32[80,128]{1,0:T(8,128)S(1)}, f32[80,128]{1,0:T(8,128)}, u32[]{:S(2)}, u32[]{:S(2)}) collective-permute-start(f32[80,128]{1,0:T(8,128)S(1)} %param.43), channel_id=1, source_target_pairs={{0,134},{2,136},{4,138},{6,140},{8,142},{10,144},{12,146},{14,148}... | collective-permute-start | bytes 122888 | tf_op jit(solution)/shard_map/cond/branch_3_fun/ppermute | solution.py:26
  221.0 11.8 %collective-permute-start.51 = (f32[80,128]{1,0:T(8,128)}, f32[80,128]{1,0:T(8,128)S(1)}, u32[]{:S(2)}, u32[]{:S(2)}) collective-permute-start(f32[80,128]{1,0:T(8,128)} %param.54), channel_id=1, source_target_pairs={{128,208},{130,210},{132,212},{134,214},{136,216},{138,218},{140,2... | collective-permute-start | bytes 122888 | tf_op jit(solution)/shard_map/cond/branch_10_fun/ppermute | solution.py:37

commit v2 on v1

v2 whole, which is shorter than its diff:
```python
import functools

import jax
import jax.numpy as jnp
from jax import lax
from jax.experimental import pallas as pl
from jax.experimental.pallas import tpu as pltpu
from jax.sharding import PartitionSpec as P


HIGH = lax.Precision.HIGHEST
FINE = 4
LANES = 128
HEAD = 128


def dot(a, b):
    return jnp.dot(a, b, precision=HIGH, preferred_element_type=jnp.float32)


def fold(part):
    half = part.shape[0] // 2
    return jnp.concatenate([part[:half], part[half:]], axis=1)


def unfold(part):
    half = part.shape[1] // 2
    return jnp.concatenate([part[:, :half], part[:, half:]], axis=0)


def chunk_rows(n):
    tail = n - HEAD
    return max(n + n // 2, HEAD * 7 // 2), max(2 * n, tail * 7 // 2)


def mirrored_parts(ref, h):
    end = 2 * h + h // 2
    return ref[0:h], ref[h : 2 * h], unfold(ref[2 * h : end]), ref[end : end + h]


def put_mirrored(ref, h, parts):
    end = 2 * h + h // 2
    ref[0:h], ref[h : 2 * h], ref[2 * h : end], ref[end : end + h] = (
        parts[0],
        parts[1],
        fold(parts[2]),
        parts[3],
    )
    if end + h < ref.shape[0]:
        ref[end + h :] = jnp.zeros((ref.shape[0] - end - h, LANES), jnp.float32)


def forward_matrix(a_ref, b_ref, n):
    return jnp.concatenate([b_ref[0:n], b_ref[n : 2 * n], unfold(a_ref[n : n + n // 2])], axis=1)


def mirrored_all(a_ref, b_ref, n):
    top, low = mirrored_parts(a_ref, HEAD), mirrored_parts(b_ref, n - HEAD)
    return [jnp.concatenate(pair, axis=0) for pair in zip(top, low)]


def put_forward_a(ref, n, state, last):
    ref[0:n] = state
    ref[n : n + n // 2] = fold(last)


def put_forward_b(ref, n, first, second):
    ref[0:n] = first
    ref[n : 2 * n] = second
    if 2 * n < ref.shape[0]:
        ref[2 * n :] = jnp.zeros((ref.shape[0] - 2 * n, LANES), jnp.float32)


def first_kernel(
    mirrored_ref, inverse_hbm, residual_hbm, coupling_hbm, a_ref, b_ref, inverse, residual, coupling, sems
):
    n = coupling.shape[0]
    copies = [
        pltpu.make_async_copy(source, target, sems.at[i])
        for i, (source, target) in enumerate(
            [(inverse_hbm, inverse), (residual_hbm, residual), (coupling_hbm, coupling)]
        )
    ]
    for copy in copies:
        copy.start()
    for copy in copies:
        copy.wait()
    state = dot(inverse[...], residual[...])

    @pl.when(mirrored_ref[0] == 0)
    def _():
        put_forward_a(a_ref, n, state, coupling[:, 2 * LANES :])
        put_forward_b(b_ref, n, coupling[:, 0:LANES], coupling[:, LANES : 2 * LANES])

    @pl.when(mirrored_ref[0] != 0)
    def _():
        for ref, low, high in ((a_ref, 0, HEAD), (b_ref, HEAD, n)):
            rows = coupling[low:high]
            parts = (rows[:, 0:LANES], rows[:, LANES : 2 * LANES], rows[:, 2 * LANES :], state[low:high])
            put_mirrored(ref, high - low, parts)


def join_mirrored(n, h, a_ref, b_ref, got_ref, out_ref):
    got = mirrored_parts(got_ref, h)
    own = mirrored_all(a_ref, b_ref, n)
    both = dot(
        jnp.concatenate(got[:3], axis=1), jnp.concatenate([own[0], own[1], own[3], own[2]], axis=1)
    )
    state = got[3] + both[:, 2 * LANES : 3 * LANES]
    put_mirrored(
        out_ref, h, (both[:, 0:LANES], both[:, LANES : 2 * LANES], both[:, 3 * LANES :], state)
    )
    return state


def join_a_kernel(n, mirrored_ref, a_ref, b_ref, got_ref, out_ref, head_ref=None):
    @pl.when(mirrored_ref[0] == 0)
    def _():
        matrix = forward_matrix(a_ref, b_ref, n)
        both = dot(matrix, jnp.concatenate([got_ref[0:n], unfold(got_ref[n : n + n // 2])], axis=1))
        state = a_ref[0:n] + both[:, 0:LANES]
        put_forward_a(out_ref, n, state, both[:, LANES:])
        if head_ref is not None:
            head_ref[...] = state[0:HEAD]

    @pl.when(mirrored_ref[0] != 0)
    def _():
        state = join_mirrored(n, HEAD, a_ref, b_ref, got_ref, out_ref)
        if head_ref is not None:
            head_ref[...] = state


def join_b_kernel(n, mirrored_ref, a_ref, b_ref, got_ref, *refs):
    new_a_ref, out_ref, rest_ref = refs if len(refs) == 3 else (None, refs[0], None)

    @pl.when(mirrored_ref[0] == 0)
    def _():
        matrix = forward_matrix(a_ref, b_ref, n)
        both = dot(matrix, jnp.concatenate([got_ref[0:n], got_ref[n : 2 * n]], axis=1))
        put_forward_b(out_ref, n, both[:, 0:LANES], both[:, LANES:])
        if rest_ref is not None:
            rest_ref[...] = new_a_ref[HEAD:n]

    @pl.when(mirrored_ref[0] != 0)
    def _():
        state = join_mirrored(n, n - HEAD, a_ref, b_ref, got_ref, out_ref)
        if rest_ref is not None:
            rest_ref[...] = state


def close_kernel(mirrored_ref, a_ref, b_ref, got_ref, out_ref):
    n = out_ref.shape[0]
    got = got_ref[...]

    @pl.when(mirrored_ref[0] == 0)
    def _():
        out_ref[...] = a_ref[0:n] + dot(forward_matrix(a_ref, b_ref, n), got)

    @pl.when(mirrored_ref[0] != 0)
    def _():
        own = mirrored_all(a_ref, b_ref, n)
        out_ref[...] = own[3] + dot(jnp.concatenate(own[:3], axis=1), got)


VMEM = pl.BlockSpec(memory_space=pltpu.VMEM)
SMEM = pl.BlockSpec(memory_space=pltpu.SMEM)
HBM = pl.BlockSpec(memory_space=pltpu.HBM)


def call(kernel, specs, shapes, *operands, scratch=()):
    shapes = [jax.ShapeDtypeStruct(shape, jnp.float32) for shape in shapes]
    out = pl.pallas_call(
        kernel,
        out_shape=shapes,
        in_specs=specs,
        out_specs=[VMEM] * len(shapes),
        scratch_shapes=scratch,
        compiler_params=pltpu.CompilerParams(vmem_limit_bytes=12 << 20),
    )(*operands)
    return out[0] if len(shapes) == 1 else out


def sector_route(rows, sectors, step):
    return [
        (row * sectors + s, row * sectors + (s + step(row)) % sectors)
        for row in range(rows)
        if step(row) is not None
        for s in range(sectors)
    ]


def is_mirrored(row):
    return (row + 1) // 2 % 2 == 0


def hop(trace, shift, senders, sectors):
    def send(step, trace):
        route = [
            (row * sectors + s, (row + 1) * sectors + (s + step) % sectors)
            for row in senders
            for s in range(sectors)
        ]
        return lax.ppermute(trace, ("row", "sector"), route)

    return lax.switch(shift % FINE, [functools.partial(send, k) for k in range(FINE)], trace)


def turn(trace, shift, rows, sectors):
    def send(step, trace):
        if step == 0:
            return trace
        route = sector_route(rows, sectors, lambda row: step if row else None)
        return lax.ppermute(trace, ("row", "sector"), route)

    steps = [functools.partial(send, k) for k in range(0, sectors, FINE)]
    return lax.switch(shift // FINE, steps, trace)


def on_device(residual, block_inverse, cycle_coupling, outlet_flux, inlet_lift, mortar_shift):
    flux = outlet_flux[0, 0, 0]
    lift = inlet_lift[0, 0, 0]
    n = cycle_coupling.shape[-1]
    rows = lax.axis_size("row")
    row_index = lax.axis_index("row")
    sectors = lax.axis_size("sector")
    last = sectors.bit_length() - 2
    half = sectors // 2
    axes = ("row", "sector")
    mirror = is_mirrored(row_index)
    mirrored = jnp.reshape(mirror, (1,)).astype(jnp.int32)
    rows_a, rows_b = [(count, LANES) for count in chunk_rows(n)]

    def move(block, step):
        route = sector_route(rows, sectors, lambda row: -step if is_mirrored(row) else step)
        return lax.ppermute(block, axes, route)

    a, b = call(
        first_kernel,
        [SMEM, HBM, HBM, HBM],
        [rows_a, rows_b],
        mirrored,
        block_inverse[0, 0, 0],
        residual[0, 0, 0],
        cycle_coupling[0, 0],
        scratch=[
            pltpu.VMEM((n, n), jnp.float32),
            pltpu.VMEM((n, LANES), jnp.float32),
            pltpu.VMEM((n, n), jnp.float32),
            pltpu.SemaphoreType.DMA((3,)),
        ],
    )
    join_a = functools.partial(join_a_kernel, n)
    join_b = functools.partial(join_b_kernel, n)

    def step_a(level, *blocks):
        shapes = [rows_a] if level < last else [rows_a, (HEAD, LANES)]
        return call(join_a, [SMEM] + [VMEM] * 3, shapes, mirrored, *blocks)

    def step_b(level, *blocks):
        shapes = [rows_b] if level < last else [rows_b, (n - HEAD, LANES)]
        return call(join_b, [SMEM] + [VMEM] * len(blocks), shapes, mirrored, *blocks)

    got_a = move(a, 1)
    got_b = move(b, 1)
    for level in range(1, last):
        new_a = step_a(level, a, b, got_a)
        next_a = move(new_a, 2**level)
        got_b = lax.optimization_barrier((got_b, new_a))[0]
        new_b = step_b(level, a, b, got_b)
        if level == 1:
            early = lax.optimization_barrier((flux, new_b))[0]
            route = sector_route(rows, sectors, lambda row: None if row else 1 - half)
            early = lax.ppermute(early, axes, route)
        if level == 2:
            new_b, early = lax.optimization_barrier((new_b, early))
        next_b = move(new_b, 2**level)
        a, b, got_a, got_b = new_a, new_b, next_a, next_b
    new_a, top = step_a(last, a, b, got_a)
    got_b = lax.optimization_barrier((got_b, new_a))[0]
    new_b, low = step_b(last, a, b, got_b, new_a)
    window = jnp.concatenate([top, low], axis=0)
    got = lax.ppermute(window, axes, sector_route(rows, sectors, lambda row: half))
    state = call(close_kernel, [SMEM] + [VMEM] * 3, [(n, LANES)], mirrored, new_a, new_b, got)

    shifts = jnp.remainder(mortar_shift, sectors)
    gain = dot(flux, lift)
    base = dot(jnp.where(row_index == 0, early, flux), state)
    inlet = jnp.zeros_like(base)
    for section in range(1, rows):
        leaving = base + dot(gain, inlet) if section > 1 else base
        shift = shifts[section - 1]
        senders = [0] if section == 1 else range(1, rows - 1)
        if section == 1:
            shift = (shift + half - 1) % sectors
        moved = hop(leaving, shift, senders, sectors)
        if section == 1:
            going, moved = lax.optimization_barrier((state, moved))
            route = sector_route(rows, sectors, lambda row: half - 1 if is_mirrored(row) else None)
            homed = lax.ppermute(going, axes, route)
            moved = jnp.where(shift >= 0, moved, 0.0)
        moved = turn(moved, shift, rows, sectors)
        inlet = jnp.where(row_index == section, moved, inlet)
    state = jnp.where(mirror, homed, state)
    current = state + dot(lift, inlet)
    trace = dot(flux, state) + dot(gain, inlet)
    return (current[None, None, None], trace[None, None, None])


def solution(mesh):
    in_specs = (
        P("row", "sector", "band", None, None),
        P("row", "sector", "band", None, None),
        P("row", "sector", None, None),
        P("row", "sector", "band", None, None),
        P("row", "sector", "band", None, None),
        P(),
    )
    out_specs = (P("row", "sector", "band", None, None), P("row", "sector", "band", None, None))

    return jax.shard_map(
        on_device, mesh=mesh, in_specs=in_specs, out_specs=out_specs, check_vma=False
    )
```

time: 233 us -> 217 us (0.931); the launches traced: 235 us -> 216 us
  starting transfers between devices: 78.6 us -> 49.1 us
  Pallas kernels: 0 us -> 9.86 us
  matrix products: 12.9 us -> 3.1 us
  waiting for transfers between devices: 131 us -> 140 us
    ppermute x17 -> x19, starting transfers between devices: 78.6 us -> 49.1 us  [the longest x10 30.3 us: move(): return lax.ppermute(block, axes, route)]
    pallas_call x0 -> x12, Pallas kernels: none -> 9.86 us  [call(): pl.pallas_call(kernel, out_shape=shapes, in_specs=specs, out_specs=[VMEM]...]
    dot_general x18 -> x7, matrix products: 12.9 us -> 3.1 us  [dot(): return jnp.dot(a, b, precision=HIGH, preferred_element_type=jnp.float32)]
    ppermute x17 -> x19, waiting for transfers between devices: 131 us -> 140 us  [the longest x10 65.6 us: move(): return lax.ppermute(block, axes, route)]
  transfers between devices with their start and end apart: 17 -> 19, of which waited for: 14 -> 11; matrix products, arithmetic and copies ran while one was open for 4% -> 1% of each run, Pallas kernels for 0% -> 2%
where the time goes in v2:
time: 217 us; the launch traced here: 216 us
  waiting for transfers between devices  140 us (65%)
  starting transfers between devices  49.1 us (23%)
  Pallas kernels  9.86 us (5%)
  between operations  6.58 us (3%)
  local copies, waits for them, and re-layouts  4.89 us (2%)
  matrix products  3.1 us (1%)
    ppermute x10, waiting for transfers between devices, move(): return lax.ppermute(block, axes, route)  65.6 us
    ppermute x6, waiting for transfers between devices, send(): return lax.ppermute(trace, ('row', 'sector'), route)  64.5 us
    ppermute x10, starting transfers between devices, move(): return lax.ppermute(block, axes, route)  30.3 us
    ppermute x6, starting transfers between devices, send(): return lax.ppermute(trace, ('row', 'sector'), route)  10.8 us
    ppermute x1, waiting for transfers between devices, on_device(): lax.ppermute(window, axes, sector_route(rows, sectors, lambda row: half))  10.2 us
    pallas_call x12, Pallas kernels, call(): pl.pallas_call(kernel, out_shape=shapes, in_specs=specs, out_specs=[VMEM]...  9.86 us
    ppermute x1, starting transfers between devices, on_device(): lax.ppermute(window, axes, sector_route(rows, sectors, lambda row: half))  6.69 us
  transfers between devices with their start and end apart: 19, of which 11 were waited for; matrix products, arithmetic and copies ran while one was open for 1% of the time, Pallas kernels for 2%

profile of v2, /device:TPU:24, one launch (start us, length us, event | category | flops | bytes accessed | tf_op | source)
XLA Modules:
  0.0 215.6 jit_solution(4054263464631506877)
XLA Ops:
  0.7 1.1 copy-done.1
  1.7 1.0 copy-done.2
  2.8 0.9 copy-done.3
  3.7 1.5 shard_map.77
  5.2 3.4 %collective-permute-start.58 = (f32[672,128]{1,0:T(8,128)S(1)}, f32[672,128]{1,0:T(8,128)S(1)}, u32[]{:S(2)}, u32[]{:S(2)}) collective-permute-start(f32[672,128]{1,0:T(8,128)S(1)} %get-tuple-element.145.b_ref), channel_id=1, source_target_pairs={{0,126},{2,0},{4,2},{6,4},{8,6},{10,8},{12,10},{14,12},{16,14},{18... | collective-permute-start | bytes 1032200 | tf_op jit(solution)/shard_map/ppermute | solution.py:235
  8.6 3.4 %collective-permute-start.57 = (f32[480,128]{1,0:T(8,128)S(1)}, f32[480,128]{1,0:T(8,128)S(1)}, u32[]{:S(2)}, u32[]{:S(2)}) collective-permute-start(f32[480,128]{1,0:T(8,128)S(1)} %get-tuple-element.144.a_ref), channel_id=1, source_target_pairs={{0,126},{2,0},{4,2},{6,4},{8,6},{10,8},{12,10},{14,12},{16,14},{18... | collective-permute-start | bytes 737288 | tf_op jit(solution)/shard_map/ppermute | solution.py:235
  12.0 14.6 %collective-permute-done.57.got_ref = f32[480,128]{1,0:T(8,128)S(1)} collective-permute-done((f32[480,128]{1,0:T(8,128)S(1)}, f32[480,128]{1,0:T(8,128)S(1)}, u32[]{:S(2)}, u32[]{:S(2)}) %collective-permute-start.57) | collective-permute-done | bytes 245792 | tf_op jit(solution)/shard_map/ppermute | solution.py:235
  26.7 0.8 shard_map.78.a_ref
  28.2 1.9 collective-permute-start.60
  30.1 1.9 collective-permute-start.59
  32.8 10.9 %collective-permute-done.59.got_ref = f32[480,128]{1,0:T(8,128)S(1)} collective-permute-done((f32[480,128]{1,0:T(8,128)S(1)}, f32[480,128]{1,0:T(8,128)S(1)}, u32[]{:S(2)}, u32[]{:S(2)}) %collective-permute-start.59) | collective-permute-done | bytes 245792 | tf_op jit(solution)/shard_map/ppermute | solution.py:235
  43.7 0.8 shard_map.80.a_ref
  45.3 1.9 collective-permute-start.63
  47.2 1.9 collective-permute-start.62
  49.1 9.1 %collective-permute-done.62.got_ref = f32[480,128]{1,0:T(8,128)S(1)} collective-permute-done((f32[480,128]{1,0:T(8,128)S(1)}, f32[480,128]{1,0:T(8,128)S(1)}, u32[]{:S(2)}, u32[]{:S(2)}) %collective-permute-start.62) | collective-permute-done | bytes 245792 | tf_op jit(solution)/shard_map/ppermute | solution.py:235
  58.2 0.8 shard_map.82.a_ref
  59.8 1.9 collective-permute-start.65
  61.7 3.2 %collective-permute-start.64 = (f32[480,128]{1,0:T(8,128)S(1)}, f32[480,128]{1,0:T(8,128)S(1)}, u32[]{:S(2)}, u32[]{:S(2)}) collective-permute-start(f32[480,128]{1,0:T(8,128)S(1)} %shard_map.82.a_ref), channel_id=1, source_target_pairs={{0,112},{2,114},{4,116},{6,118},{8,120},{10,122},{12,124},{14,126}... | collective-permute-start | bytes 737288 | tf_op jit(solution)/shard_map/ppermute | solution.py:235
  64.9 15.1 %collective-permute-done.64.got_ref = f32[480,128]{1,0:T(8,128)S(1)} collective-permute-done((f32[480,128]{1,0:T(8,128)S(1)}, f32[480,128]{1,0:T(8,128)S(1)}, u32[]{:S(2)}, u32[]{:S(2)}) %collective-permute-start.64) | collective-permute-done | bytes 245792 | tf_op jit(solution)/shard_map/ppermute | solution.py:235
  80.0 0.8 shard_map.84.a_ref
  80.8 0.9 shard_map.85.b_ref
  81.7 1.9 collective-permute-start.67
  83.6 8.8 %collective-permute-start.66 = (f32[480,128]{1,0:T(8,128)S(1)}, f32[480,128]{1,0:T(8,128)S(1)}, u32[]{:S(2)}, u32[]{:S(2)}) collective-permute-start(f32[480,128]{1,0:T(8,128)S(1)} %shard_map.84.a_ref), channel_id=1, source_target_pairs={{0,96},{2,98},{4,100},{6,102},{8,104},{10,106},{12,108},{14,110},{... | collective-permute-start | bytes 737288 | tf_op jit(solution)/shard_map/ppermute | solution.py:235
  98.6 15.8 %collective-permute-done.66.got_ref = f32[480,128]{1,0:T(8,128)S(1)} collective-permute-done((f32[480,128]{1,0:T(8,128)S(1)}, f32[480,128]{1,0:T(8,128)S(1)}, u32[]{:S(2)}, u32[]{:S(2)}) %collective-permute-start.66) | collective-permute-done | bytes 245792 | tf_op jit(solution)/shard_map/ppermute | solution.py:235
  114.5 0.8 shard_map.86
  116.0 6.7 %collective-permute-start.68 = (f32[320,128]{1,0:T(8,128)S(1)}, f32[320,128]{1,0:T(8,128)S(1)}, u32[]{:S(2)}, u32[]{:S(2)}) collective-permute-start(f32[320,128]{1,0:T(8,128)S(1)} %pad_maximum_fusion), channel_id=1, source_target_pairs={{0,64},{2,66},{4,68},{6,70},{8,72},{10,74},{12,76},{14,78},{16,80}... | collective-permute-start | bytes 491528 | tf_op jit(solution)/shard_map/ppermute | solution.py:282
  123.0 10.2 %collective-permute-done.68.got_ref = f32[320,128]{1,0:T(8,128)S(1)} collective-permute-done((f32[320,128]{1,0:T(8,128)S(1)}, f32[320,128]{1,0:T(8,128)S(1)}, u32[]{:S(2)}, u32[]{:S(2)}) %collective-permute-start.68) | collective-permute-done | bytes 163872 | tf_op jit(solution)/shard_map/ppermute | solution.py:282
  134.1 1.3 conditional.6
  134.1 1.3 collective-permute-start.2
  135.4 0.8 broadcast_select_fusion.2
  136.2 10.7 %conditional.7 = (f32[80,128]{1,0:T(8,128)S(1)}) conditional(s32[]{:T(128)} %clamp.23, f32[80,128]{1,0:T(8,128)S(1)} %broadcast_select_fusion.2, f32[80,128]{1,0:T(8,128)S(1)} %broadcast_select_fusion.2, f32[80,128]{1,0:T(8,128)S(1)} %broadcast_select_fusion.2, f32[80,128]{1,0:T(8,128)S(1)} %broadcast_select_fusion.2, ...), branch_computations={%region_4.5_spmd, %region_5.6_spmd, %region_6.7_spmd, %region_7.8_... | conditional | bytes 245808 | solution.py:216
  136.2 1.9 collective-permute-start.14
  138.1 8.8 %collective-permute-done.14 = f32[80,128]{1,0:T(8,128)S(1)} collective-permute-done((f32[80,128]{1,0:T(8,128)S(1)}, f32[80,128]{1,0:T(8,128)S(1)}, u32[]{:S(2)}, u32[]{:S(2)}) %collective-permute-start.14) | collective-permute-done | bytes 40992 | tf_op jit(solution)/shard_map/cond/branch_11_fun/ppermute | solution.py:213
  147.1 31.7 %conditional.8 = (f32[80,128]{1,0:T(8,128)}) conditional(s32[]{:T(128)} %clamp.22, f32[80,128]{1,0:T(8,128)S(1)} %convolution_add_fusion.1, f32[80,128]{1,0:T(8,128)S(1)} %convolution_add_fusion.1, f32[80,128]{1,0:T(8,128)S(1)} %convolution_add_fusion.1, f32[80,128]{1,0:T(8,128)S(1)} %convolution_add_fusion.1), branch_computations={%region_20.21_spmd, %region_21.22_spmd, %region_22.23_spmd, %regio... | conditional | bytes 163888 | solution.py:205
  147.1 1.9 collective-permute-start.21
  149.0 29.7 %collective-permute-done.21 = f32[80,128]{1,0:T(8,128)} collective-permute-done((f32[80,128]{1,0:T(8,128)S(1)}, f32[80,128]{1,0:T(8,128)}, u32[]{:S(2)}, u32[]{:S(2)}) %collective-permute-start.21) | collective-permute-done | bytes 40992 | tf_op jit(solution)/shard_map/cond/branch_2_fun/ppermute | solution.py:203
  178.7 16.4 %conditional.9 = (f32[80,128]{1,0:T(8,128)}) conditional(s32[]{:T(128)} %clamp.21, f32[80,128]{1,0:T(8,128)} %get-tuple-element.165, f32[80,128]{1,0:T(8,128)} %get-tuple-element.165, f32[80,128]{1,0:T(8,128)} %get-tuple-element.165, f32[80,128]{1,0:T(8,128)} %get-tuple-element.165, ...), branch_computations={%region_24.25_spmd, %region_25.26_spmd, %region_26.27_spmd, %regio... | conditional | bytes 245808 | solution.py:216
  178.7 1.9 collective-permute-start.27
  180.6 13.8 %collective-permute-done.27 = f32[80,128]{1,0:T(8,128)S(1)} collective-permute-done((f32[80,128]{1,0:T(8,128)}, f32[80,128]{1,0:T(8,128)S(1)}, u32[]{:S(2)}, u32[]{:S(2)}) %collective-permute-start.27) | collective-permute-done | bytes 40992 | tf_op jit(solution)/shard_map/cond/branch_5_fun/ppermute | solution.py:213
  195.1 0.8 select_select_fusion
  196.7 6.9 %conditional.10 = (f32[80,128]{1,0:T(8,128)}) conditional(s32[]{:T(128)} %clamp.20, f32[80,128]{1,0:T(8,128)S(1)} %convolution_add_fusion, f32[80,128]{1,0:T(8,128)S(1)} %convolution_add_fusion, f32[80,128]{1,0:T(8,128)S(1)} %convolution_add_fusion, f32[80,128]{1,0:T(8,128)S(1)} %convolution_add_fusion), branch_computations={%region_40.41_spmd, %region_41.42_spmd, %region_42.43_spmd, %regio... | conditional | bytes 163888 | solution.py:205
  196.8 1.9 collective-permute-start.38
  198.7 5.0 %collective-permute-done.38 = f32[80,128]{1,0:T(8,128)} collective-permute-done((f32[80,128]{1,0:T(8,128)S(1)}, f32[80,128]{1,0:T(8,128)}, u32[]{:S(2)}, u32[]{:S(2)}) %collective-permute-start.38) | collective-permute-done | bytes 40992 | tf_op jit(solution)/shard_map/cond/branch_0_fun/ppermute | solution.py:203
  203.7 9.7 %conditional.11 = (f32[80,128]{1,0:T(8,128)}) conditional(s32[]{:T(128)} %clamp.19, f32[80,128]{1,0:T(8,128)} %get-tuple-element.167, f32[80,128]{1,0:T(8,128)} %get-tuple-element.167, f32[80,128]{1,0:T(8,128)} %get-tuple-element.167, f32[80,128]{1,0:T(8,128)} %get-tuple-element.167, ...), branch_computations={%region_44.45_spmd, %region_45.46_spmd, %region_46.47_spmd, %regio... | conditional | bytes 245808 | solution.py:216
  203.7 1.9 collective-permute-start.44
  205.6 7.2 %collective-permute-done.44 = f32[80,128]{1,0:T(8,128)S(1)} collective-permute-done((f32[80,128]{1,0:T(8,128)}, f32[80,128]{1,0:T(8,128)S(1)}, u32[]{:S(2)}, u32[]{:S(2)}) %collective-permute-start.44) | collective-permute-done | bytes 40992 | tf_op jit(solution)/shard_map/cond/branch_3_fun/ppermute | solution.py:213
  213.6 1.1 fusion.1
  214.7 0.9 fusion.3
  (35 shorter events, 7.8 us)
Async XLA Ops:
  0.6 122.1 %copy-start = (f32[1,1,1,320,80]{3,4,2,1,0:T(8,128)S(1)}, f32[1,1,1,320,80]{3,4,2,1,0:T(8,128)}, u32[]{:S(2)}) copy-start(f32[1,1,1,320,80]{3,4,2,1,0:T(8,128)} %param.70) | copy-start | bytes 307204
  0.7 1.1 copy-start.1
  1.7 1.0 copy-start.2
  2.8 0.9 copy-start.3
  5.2 22.3 %collective-permute-start.58 = (f32[672,128]{1,0:T(8,128)S(1)}, f32[672,128]{1,0:T(8,128)S(1)}, u32[]{:S(2)}, u32[]{:S(2)}) collective-permute-start(f32[672,128]{1,0:T(8,128)S(1)} %get-tuple-element.145.b_ref), channel_id=1, source_target_pairs={{0,126},{2,0},{4,2},{6,4},{8,6},{10,8},{12,10},{14,12},{16,14},{18... | collective-permute-start | bytes 1032200 | tf_op jit(solution)/shard_map/ppermute | solution.py:235
  8.6 18.0 %collective-permute-start.57 = (f32[480,128]{1,0:T(8,128)S(1)}, f32[480,128]{1,0:T(8,128)S(1)}, u32[]{:S(2)}, u32[]{:S(2)}) collective-permute-start(f32[480,128]{1,0:T(8,128)S(1)} %get-tuple-element.144.a_ref), channel_id=1, source_target_pairs={{0,126},{2,0},{4,2},{6,4},{8,6},{10,8},{12,10},{14,12},{16,14},{18... | collective-permute-start | bytes 737288 | tf_op jit(solution)/shard_map/ppermute | solution.py:235
  27.5 4.6 %copy-start.4 = (f32[1,1,1,80,320]{4,3,2,1,0:T(8,128)S(1)}, f32[1,1,1,80,320]{4,3,2,1,0:T(8,128)}, u32[]{:S(2)}) copy-start(f32[1,1,1,80,320]{4,3,2,1,0:T(8,128)} %param.69) | copy-start | bytes 307204
  28.2 16.3 %collective-permute-start.60 = (f32[672,128]{1,0:T(8,128)S(1)}, f32[672,128]{1,0:T(8,128)S(1)}, u32[]{:S(2)}, u32[]{:S(2)}) collective-permute-start(f32[672,128]{1,0:T(8,128)S(1)} %shard_map.79.b_ref), channel_id=1, source_target_pairs={{0,124},{2,126},{4,0},{6,2},{8,4},{10,6},{12,8},{14,10},{16,12},{1... | collective-permute-start | bytes 1032200 | tf_op jit(solution)/shard_map/ppermute | solution.py:235
  30.1 13.6 %collective-permute-start.59 = (f32[480,128]{1,0:T(8,128)S(1)}, f32[480,128]{1,0:T(8,128)S(1)}, u32[]{:S(2)}, u32[]{:S(2)}) collective-permute-start(f32[480,128]{1,0:T(8,128)S(1)} %shard_map.78.a_ref), channel_id=1, source_target_pairs={{0,124},{2,126},{4,0},{6,2},{8,4},{10,6},{12,8},{14,10},{16,12},{1... | collective-permute-start | bytes 737288 | tf_op jit(solution)/shard_map/ppermute | solution.py:235
  32.1 13.2 %collective-permute-start.61 = (f32[80,320]{1,0:T(8,128)S(1)}, f32[80,320]{1,0:T(8,128)S(1)}, u32[]{:S(2)}, u32[]{:S(2)}) collective-permute-start(f32[80,320]{1,0:T(8,128)S(1)} %bitcast.45), channel_id=1, source_target_pairs={{0,66},{2,68},{4,70},{6,72},{8,74},{10,76},{12,78},{14,80},{16,82}... | collective-permute-start | bytes 307208 | tf_op jit(solution)/shard_map/ppermute | solution.py:273
  45.3 13.8 %collective-permute-start.63 = (f32[672,128]{1,0:T(8,128)S(1)}, f32[672,128]{1,0:T(8,128)S(1)}, u32[]{:S(2)}, u32[]{:S(2)}) collective-permute-start(f32[672,128]{1,0:T(8,128)S(1)} %shard_map.81.b_ref), channel_id=1, source_target_pairs={{0,120},{2,122},{4,124},{6,126},{8,0},{10,2},{12,4},{14,6},{16,8},... | collective-permute-start | bytes 1032200 | tf_op jit(solution)/shard_map/ppermute | solution.py:235
  47.2 11.1 %collective-permute-start.62 = (f32[480,128]{1,0:T(8,128)S(1)}, f32[480,128]{1,0:T(8,128)S(1)}, u32[]{:S(2)}, u32[]{:S(2)}) collective-permute-start(f32[480,128]{1,0:T(8,128)S(1)} %shard_map.80.a_ref), channel_id=1, source_target_pairs={{0,120},{2,122},{4,124},{6,126},{8,0},{10,2},{12,4},{14,6},{16,8},... | collective-permute-start | bytes 737288 | tf_op jit(solution)/shard_map/ppermute | solution.py:235
  59.8 21.0 %collective-permute-start.65 = (f32[672,128]{1,0:T(8,128)S(1)}, f32[672,128]{1,0:T(8,128)S(1)}, u32[]{:S(2)}, u32[]{:S(2)}) collective-permute-start(f32[672,128]{1,0:T(8,128)S(1)} %shard_map.83.b_ref), channel_id=1, source_target_pairs={{0,112},{2,114},{4,116},{6,118},{8,120},{10,122},{12,124},{14,126}... | collective-permute-start | bytes 1032200 | tf_op jit(solution)/shard_map/ppermute | solution.py:235
  61.7 18.3 %collective-permute-start.64 = (f32[480,128]{1,0:T(8,128)S(1)}, f32[480,128]{1,0:T(8,128)S(1)}, u32[]{:S(2)}, u32[]{:S(2)}) collective-permute-start(f32[480,128]{1,0:T(8,128)S(1)} %shard_map.82.a_ref), channel_id=1, source_target_pairs={{0,112},{2,114},{4,116},{6,118},{8,120},{10,122},{12,124},{14,126}... | collective-permute-start | bytes 737288 | tf_op jit(solution)/shard_map/ppermute | solution.py:235
  81.7 10.7 %copy-start.5 = (s32[3]{0:T(128)S(1)}, s32[3]{0:T(128)}, u32[]{:S(2)}) copy-start(s32[3]{0:T(128)} %param.71) | copy-start | bytes 40
  81.7 33.6 %collective-permute-start.67 = (f32[672,128]{1,0:T(8,128)S(1)}, f32[672,128]{1,0:T(8,128)S(1)}, u32[]{:S(2)}, u32[]{:S(2)}) collective-permute-start(f32[672,128]{1,0:T(8,128)S(1)} %shard_map.85.b_ref), channel_id=1, source_target_pairs={{0,96},{2,98},{4,100},{6,102},{8,104},{10,106},{12,108},{14,110},{... | collective-permute-start | bytes 1032200 | tf_op jit(solution)/shard_map/ppermute | solution.py:235
  83.6 30.8 %collective-permute-start.66 = (f32[480,128]{1,0:T(8,128)S(1)}, f32[480,128]{1,0:T(8,128)S(1)}, u32[]{:S(2)}, u32[]{:S(2)}) collective-permute-start(f32[480,128]{1,0:T(8,128)S(1)} %shard_map.84.a_ref), channel_id=1, source_target_pairs={{0,96},{2,98},{4,100},{6,102},{8,104},{10,106},{12,108},{14,110},{... | collective-permute-start | bytes 737288 | tf_op jit(solution)/shard_map/ppermute | solution.py:235
  116.0 17.2 %collective-permute-start.68 = (f32[320,128]{1,0:T(8,128)S(1)}, f32[320,128]{1,0:T(8,128)S(1)}, u32[]{:S(2)}, u32[]{:S(2)}) collective-permute-start(f32[320,128]{1,0:T(8,128)S(1)} %pad_maximum_fusion), channel_id=1, source_target_pairs={{0,64},{2,66},{4,68},{6,70},{8,72},{10,74},{12,76},{14,78},{16,80}... | collective-permute-start | bytes 491528 | tf_op jit(solution)/shard_map/ppermute | solution.py:282
  134.1 1.3 collective-permute-start.2
  136.2 10.7 %collective-permute-start.14 = (f32[80,128]{1,0:T(8,128)S(1)}, f32[80,128]{1,0:T(8,128)S(1)}, u32[]{:S(2)}, u32[]{:S(2)}) collective-permute-start(f32[80,128]{1,0:T(8,128)S(1)} %param.15), channel_id=1, source_target_pairs={{128,216},{130,218},{132,220},{134,222},{136,224},{138,226},{140,2... | collective-permute-start | bytes 122888 | tf_op jit(solution)/shard_map/cond/branch_11_fun/ppermute | solution.py:213
  147.1 31.6 %collective-permute-start.21 = (f32[80,128]{1,0:T(8,128)S(1)}, f32[80,128]{1,0:T(8,128)}, u32[]{:S(2)}, u32[]{:S(2)}) collective-permute-start(f32[80,128]{1,0:T(8,128)S(1)} %param.22), channel_id=1, source_target_pairs={{128,260},{130,262},{132,264},{134,266},{136,268},{138,270},{140,2... | collective-permute-start | bytes 122888 | tf_op jit(solution)/shard_map/cond/branch_2_fun/ppermute | solution.py:203
  178.7 15.8 %collective-permute-start.27 = (f32[80,128]{1,0:T(8,128)}, f32[80,128]{1,0:T(8,128)S(1)}, u32[]{:S(2)}, u32[]{:S(2)}) collective-permute-start(f32[80,128]{1,0:T(8,128)} %param.29), channel_id=1, source_target_pairs={{128,168},{130,170},{132,172},{134,174},{136,176},{138,178},{140,1... | collective-permute-start | bytes 122888 | tf_op jit(solution)/shard_map/cond/branch_5_fun/ppermute | solution.py:213
  196.1 17.5 %collective-permute-start.69 = (f32[320,128]{1,0:T(8,128)S(1)}, f32[320,128]{1,0:T(8,128)S(1)}, u32[]{:S(2)}, u32[]{:S(2)}) collective-permute-start(f32[320,128]{1,0:T(8,128)S(1)} %shard_map.88), channel_id=1, source_target_pairs={{0,62},{2,64},{4,66},{6,68},{8,70},{10,72},{12,74},{14,76},{16,78}... | collective-permute-start | bytes 491528 | tf_op jit(solution)/shard_map/ppermute | solution.py:299
  196.8 6.9 %collective-permute-start.38 = (f32[80,128]{1,0:T(8,128)S(1)}, f32[80,128]{1,0:T(8,128)}, u32[]{:S(2)}, u32[]{:S(2)}) collective-permute-start(f32[80,128]{1,0:T(8,128)S(1)} %param.40), channel_id=1, source_target_pairs={{128,256},{130,258},{132,260},{134,262},{136,264},{138,266},{140,2... | collective-permute-start | bytes 122888 | tf_op jit(solution)/shard_map/cond/branch_0_fun/ppermute | solution.py:203
  203.7 9.1 %collective-permute-start.44 = (f32[80,128]{1,0:T(8,128)}, f32[80,128]{1,0:T(8,128)S(1)}, u32[]{:S(2)}, u32[]{:S(2)}) collective-permute-start(f32[80,128]{1,0:T(8,128)} %param.47), channel_id=1, source_target_pairs={{128,152},{130,154},{132,156},{134,158},{136,160},{138,162},{140,1... | collective-permute-start | bytes 122888 | tf_op jit(solution)/shard_map/cond/branch_3_fun/ppermute | solution.py:213

commit v3 on v2

--- a/solution.py
+++ b/solution.py
@@ -239,9 +239,10 @@
         [SMEM, HBM, HBM, HBM],
         [rows_a, rows_b],
         mirrored,
-        block_inverse[0, 0, 0],
-        residual[0, 0, 0],
-        cycle_coupling[0, 0],
+        *[
+            pltpu.with_memory_space_constraint(block, pltpu.HBM)
+            for block in (block_inverse[0, 0, 0], residual[0, 0, 0], cycle_coupling[0, 0])
+        ],
         scratch=[
             pltpu.VMEM((n, n), jnp.float32),
             pltpu.VMEM((n, LANES), jnp.float32),
@@ -262,17 +263,14 @@
 
     got_a = move(a, 1)
     got_b = move(b, 1)
+    early = lax.ppermute(
+        flux, axes, sector_route(rows, sectors, lambda row: None if row else 1 - half)
+    )
     for level in range(1, last):
         new_a = step_a(level, a, b, got_a)
         next_a = move(new_a, 2**level)
         got_b = lax.optimization_barrier((got_b, new_a))[0]
         new_b = step_b(level, a, b, got_b)
-        if level == 1:
-            early = lax.optimization_barrier((flux, new_b))[0]
-            route = sector_route(rows, sectors, lambda row: None if row else 1 - half)
-            early = lax.ppermute(early, axes, route)
-        if level == 2:
-            new_b, early = lax.optimization_barrier((new_b, early))
         next_b = move(new_b, 2**level)
         a, b, got_a, got_b = new_a, new_b, next_a, next_b
     new_a, top = step_a(last, a, b, got_a)

time: 217 us -> 205 us (0.945); the launches traced: 216 us -> 201 us
  waiting for transfers between devices: 140 us -> 128 us
  local copies, waits for them, and re-layouts: 4.89 us -> 1.87 us
    ppermute x6, waiting for transfers between devices: 64.5 us -> 52.7 us  [send(): return lax.ppermute(trace, ('row', 'sector'), route)]
    ppermute x1, waiting for transfers between devices: 10.2 us -> 4.22 us  [on_device(): lax.ppermute(window, axes, sector_route(rows, sectors, lambda row: half))]
    ppermute x10, waiting for transfers between devices: 65.6 us -> 71.5 us  [move(): return lax.ppermute(block, axes, route)]
    unnamed x12 -> x6, local copies, waits for them, and re-layouts: 3.02 us -> 0.02 us
  transfers between devices with their start and end apart: 19 -> 19, of which waited for: 11 -> 11; matrix products, arithmetic and copies ran while one was open for 1% -> 1% of each run, Pallas kernels for 2% -> 3%
where the time goes in v3:
time: 205 us; the launch traced here: 201 us
  waiting for transfers between devices  128 us (62%)
  starting transfers between devices  49.2 us (24%)
  Pallas kernels  10.3 us (5%)
  between operations  6.65 us (3%)
  matrix products  3.1 us (2%)
    ppermute x10, waiting for transfers between devices, move(): return lax.ppermute(block, axes, route)  71.5 us
    ppermute x6, waiting for transfers between devices, send(): return lax.ppermute(trace, ('row', 'sector'), route)  52.7 us
    ppermute x10, starting transfers between devices, move(): return lax.ppermute(block, axes, route)  30.3 us
    ppermute x6, starting transfers between devices, send(): return lax.ppermute(trace, ('row', 'sector'), route)  10.8 us
    pallas_call x12, Pallas kernels, call(): pl.pallas_call(kernel, out_shape=shapes, in_specs=specs, out_specs=[VMEM]...  10.3 us
    ppermute x1, starting transfers between devices, on_device(): lax.ppermute(window, axes, sector_route(rows, sectors, lambda row: half))  6.71 us
    ppermute x1, waiting for transfers between devices, on_device(): lax.ppermute(window, axes, sector_route(rows, sectors, lambda row: half))  4.22 us
  transfers between devices with their start and end apart: 19, of which 11 were waited for; matrix products, arithmetic and copies ran while one was open for 1% of the time, Pallas kernels for 3%

profile of v3, /device:TPU:24, one launch (start us, length us, event | category | flops | bytes accessed | tf_op | source)
XLA Modules:
  0.0 201.2 jit_solution(13325404757117232139)
XLA Ops:
  0.7 2.0 shard_map.77
  2.7 3.4 %collective-permute-start.58 = (f32[672,128]{1,0:T(8,128)S(1)}, f32[672,128]{1,0:T(8,128)S(1)}, u32[]{:S(2)}, u32[]{:S(2)}) collective-permute-start(f32[672,128]{1,0:T(8,128)S(1)} %get-tuple-element.142.b_ref), channel_id=1, source_target_pairs={{0,126},{2,0},{4,2},{6,4},{8,6},{10,8},{12,10},{14,12},{16,14},{18... | collective-permute-start | bytes 1032200 | tf_op jit(solution)/shard_map/ppermute | solution.py:235
  6.1 3.4 %collective-permute-start.57 = (f32[480,128]{1,0:T(8,128)S(1)}, f32[480,128]{1,0:T(8,128)S(1)}, u32[]{:S(2)}, u32[]{:S(2)}) collective-permute-start(f32[480,128]{1,0:T(8,128)S(1)} %get-tuple-element.141.a_ref), channel_id=1, source_target_pairs={{0,126},{2,0},{4,2},{6,4},{8,6},{10,8},{12,10},{14,12},{16,14},{18... | collective-permute-start | bytes 737288 | tf_op jit(solution)/shard_map/ppermute | solution.py:235
  9.5 14.6 %collective-permute-done.57.got_ref = f32[480,128]{1,0:T(8,128)S(1)} collective-permute-done((f32[480,128]{1,0:T(8,128)S(1)}, f32[480,128]{1,0:T(8,128)S(1)}, u32[]{:S(2)}, u32[]{:S(2)}) %collective-permute-start.57) | collective-permute-done | bytes 245792 | tf_op jit(solution)/shard_map/ppermute | solution.py:235
  24.1 0.8 shard_map.78.a_ref
  25.6 1.9 collective-permute-start.60
  27.6 1.9 collective-permute-start.59
  29.5 11.6 %collective-permute-done.59.got_ref = f32[480,128]{1,0:T(8,128)S(1)} collective-permute-done((f32[480,128]{1,0:T(8,128)S(1)}, f32[480,128]{1,0:T(8,128)S(1)}, u32[]{:S(2)}, u32[]{:S(2)}) %collective-permute-start.59) | collective-permute-done | bytes 245792 | tf_op jit(solution)/shard_map/ppermute | solution.py:235
  41.1 0.8 shard_map.80.a_ref
  42.0 0.7 shard_map.81.b_ref
  42.7 1.9 collective-permute-start.62
  44.6 1.9 collective-permute-start.61
  46.5 9.1 %collective-permute-done.61.got_ref = f32[480,128]{1,0:T(8,128)S(1)} collective-permute-done((f32[480,128]{1,0:T(8,128)S(1)}, f32[480,128]{1,0:T(8,128)S(1)}, u32[]{:S(2)}, u32[]{:S(2)}) %collective-permute-start.61) | collective-permute-done | bytes 245792 | tf_op jit(solution)/shard_map/ppermute | solution.py:235
  55.7 0.8 shard_map.82.a_ref
  56.5 0.7 shard_map.83.b_ref
  57.2 1.9 collective-permute-start.64
  59.1 3.2 %collective-permute-start.63 = (f32[480,128]{1,0:T(8,128)S(1)}, f32[480,128]{1,0:T(8,128)S(1)}, u32[]{:S(2)}, u32[]{:S(2)}) collective-permute-start(f32[480,128]{1,0:T(8,128)S(1)} %shard_map.82.a_ref), channel_id=1, source_target_pairs={{0,112},{2,114},{4,116},{6,118},{8,120},{10,122},{12,124},{14,126}... | collective-permute-start | bytes 737288 | tf_op jit(solution)/shard_map/ppermute | solution.py:235
  62.3 15.1 %collective-permute-done.63.got_ref = f32[480,128]{1,0:T(8,128)S(1)} collective-permute-done((f32[480,128]{1,0:T(8,128)S(1)}, f32[480,128]{1,0:T(8,128)S(1)}, u32[]{:S(2)}, u32[]{:S(2)}) %collective-permute-start.63) | collective-permute-done | bytes 245792 | tf_op jit(solution)/shard_map/ppermute | solution.py:235
  77.4 0.8 shard_map.84.a_ref
  78.2 0.9 shard_map.85.b_ref
  79.1 1.9 collective-permute-start.66
  81.1 8.8 %collective-permute-start.65 = (f32[480,128]{1,0:T(8,128)S(1)}, f32[480,128]{1,0:T(8,128)S(1)}, u32[]{:S(2)}, u32[]{:S(2)}) collective-permute-start(f32[480,128]{1,0:T(8,128)S(1)} %shard_map.84.a_ref), channel_id=1, source_target_pairs={{0,96},{2,98},{4,100},{6,102},{8,104},{10,106},{12,108},{14,110},{... | collective-permute-start | bytes 737288 | tf_op jit(solution)/shard_map/ppermute | solution.py:235
  90.8 21.0 %collective-permute-done.65.got_ref = f32[480,128]{1,0:T(8,128)S(1)} collective-permute-done((f32[480,128]{1,0:T(8,128)S(1)}, f32[480,128]{1,0:T(8,128)S(1)}, u32[]{:S(2)}, u32[]{:S(2)}) %collective-permute-start.65) | collective-permute-done | bytes 245792 | tf_op jit(solution)/shard_map/ppermute | solution.py:235
  111.8 0.8 shard_map.86
  112.6 0.7 shard_map.87
  113.4 6.7 %collective-permute-start.67 = (f32[320,128]{1,0:T(8,128)S(1)}, f32[320,128]{1,0:T(8,128)S(1)}, u32[]{:S(2)}, u32[]{:S(2)}) collective-permute-start(f32[320,128]{1,0:T(8,128)S(1)} %pad_maximum_fusion), channel_id=1, source_target_pairs={{0,64},{2,66},{4,68},{6,70},{8,72},{10,74},{12,76},{14,78},{16,80}... | collective-permute-start | bytes 491528 | tf_op jit(solution)/shard_map/ppermute | solution.py:280
  126.4 4.2 %collective-permute-done.67.got_ref = f32[320,128]{1,0:T(8,128)S(1)} collective-permute-done((f32[320,128]{1,0:T(8,128)S(1)}, f32[320,128]{1,0:T(8,128)S(1)}, u32[]{:S(2)}, u32[]{:S(2)}) %collective-permute-start.67) | collective-permute-done | bytes 163872 | tf_op jit(solution)/shard_map/ppermute | solution.py:280
  131.4 1.3 conditional.6
  131.5 1.3 collective-permute-start.2
  132.7 0.8 broadcast_select_fusion.2
  133.5 10.7 %conditional.7 = (f32[80,128]{1,0:T(8,128)S(1)}) conditional(s32[]{:T(128)} %clamp.23, f32[80,128]{1,0:T(8,128)S(1)} %broadcast_select_fusion.2, f32[80,128]{1,0:T(8,128)S(1)} %broadcast_select_fusion.2, f32[80,128]{1,0:T(8,128)S(1)} %broadcast_select_fusion.2, f32[80,128]{1,0:T(8,128)S(1)} %broadcast_select_fusion.2, ...), branch_computations={%region_4.5_spmd, %region_5.6_spmd, %region_6.7_spmd, %region_7.8_... | conditional | bytes 245808 | solution.py:216
  133.5 1.9 collective-permute-start.14
  135.4 8.8 %collective-permute-done.14 = f32[80,128]{1,0:T(8,128)S(1)} collective-permute-done((f32[80,128]{1,0:T(8,128)S(1)}, f32[80,128]{1,0:T(8,128)S(1)}, u32[]{:S(2)}, u32[]{:S(2)}) %collective-permute-start.14) | collective-permute-done | bytes 40992 | tf_op jit(solution)/shard_map/cond/branch_11_fun/ppermute | solution.py:213
  144.4 22.6 %conditional.8 = (f32[80,128]{1,0:T(8,128)}) conditional(s32[]{:T(128)} %clamp.22, f32[80,128]{1,0:T(8,128)S(1)} %convolution_add_fusion.1, f32[80,128]{1,0:T(8,128)S(1)} %convolution_add_fusion.1, f32[80,128]{1,0:T(8,128)S(1)} %convolution_add_fusion.1, f32[80,128]{1,0:T(8,128)S(1)} %convolution_add_fusion.1), branch_computations={%region_20.21_spmd, %region_21.22_spmd, %region_22.23_spmd, %regio... | conditional | bytes 163888 | solution.py:205
  144.5 1.9 collective-permute-start.21
  146.4 20.7 %collective-permute-done.21 = f32[80,128]{1,0:T(8,128)} collective-permute-done((f32[80,128]{1,0:T(8,128)S(1)}, f32[80,128]{1,0:T(8,128)}, u32[]{:S(2)}, u32[]{:S(2)}) %collective-permute-start.21) | collective-permute-done | bytes 40992 | tf_op jit(solution)/shard_map/cond/branch_2_fun/ppermute | solution.py:203
  167.1 13.6 %conditional.9 = (f32[80,128]{1,0:T(8,128)}) conditional(s32[]{:T(128)} %clamp.21, f32[80,128]{1,0:T(8,128)} %get-tuple-element.159, f32[80,128]{1,0:T(8,128)} %get-tuple-element.159, f32[80,128]{1,0:T(8,128)} %get-tuple-element.159, f32[80,128]{1,0:T(8,128)} %get-tuple-element.159, ...), branch_computations={%region_24.25_spmd, %region_25.26_spmd, %region_26.27_spmd, %regio... | conditional | bytes 245808 | solution.py:216
  167.1 1.9 collective-permute-start.27
  169.0 11.0 %collective-permute-done.27 = f32[80,128]{1,0:T(8,128)S(1)} collective-permute-done((f32[80,128]{1,0:T(8,128)}, f32[80,128]{1,0:T(8,128)S(1)}, u32[]{:S(2)}, u32[]{:S(2)}) %collective-permute-start.27) | collective-permute-done | bytes 40992 | tf_op jit(solution)/shard_map/cond/branch_5_fun/ppermute | solution.py:213
  180.7 0.8 select_select_fusion
  182.3 6.9 %conditional.10 = (f32[80,128]{1,0:T(8,128)}) conditional(s32[]{:T(128)} %clamp.20, f32[80,128]{1,0:T(8,128)S(1)} %convolution_add_fusion, f32[80,128]{1,0:T(8,128)S(1)} %convolution_add_fusion, f32[80,128]{1,0:T(8,128)S(1)} %convolution_add_fusion, f32[80,128]{1,0:T(8,128)S(1)} %convolution_add_fusion), branch_computations={%region_40.41_spmd, %region_41.42_spmd, %region_42.43_spmd, %regio... | conditional | bytes 163888 | solution.py:205
  182.3 1.9 collective-permute-start.38
  184.3 5.0 %collective-permute-done.38 = f32[80,128]{1,0:T(8,128)} collective-permute-done((f32[80,128]{1,0:T(8,128)S(1)}, f32[80,128]{1,0:T(8,128)}, u32[]{:S(2)}, u32[]{:S(2)}) %collective-permute-start.38) | collective-permute-done | bytes 40992 | tf_op jit(solution)/shard_map/cond/branch_0_fun/ppermute | solution.py:203
  189.3 9.7 %conditional.11 = (f32[80,128]{1,0:T(8,128)}) conditional(s32[]{:T(128)} %clamp.19, f32[80,128]{1,0:T(8,128)} %get-tuple-element.161, f32[80,128]{1,0:T(8,128)} %get-tuple-element.161, f32[80,128]{1,0:T(8,128)} %get-tuple-element.161, f32[80,128]{1,0:T(8,128)} %get-tuple-element.161, ...), branch_computations={%region_44.45_spmd, %region_45.46_spmd, %region_46.47_spmd, %regio... | conditional | bytes 245808 | solution.py:216
  189.3 1.9 collective-permute-start.44
  191.2 7.2 %collective-permute-done.44 = f32[80,128]{1,0:T(8,128)S(1)} collective-permute-done((f32[80,128]{1,0:T(8,128)}, f32[80,128]{1,0:T(8,128)S(1)}, u32[]{:S(2)}, u32[]{:S(2)}) %collective-permute-start.44) | collective-permute-done | bytes 40992 | tf_op jit(solution)/shard_map/cond/branch_3_fun/ppermute | solution.py:213
  199.2 1.1 fusion.1
  200.3 0.9 fusion.3
  (29 shorter events, 5.6 us)
Async XLA Ops:
  0.6 89.9 %copy-start = (f32[1,1,1,320,80]{3,4,2,1,0:T(8,128)S(1)}, f32[1,1,1,320,80]{3,4,2,1,0:T(8,128)}, u32[]{:S(2)}) copy-start(f32[1,1,1,320,80]{3,4,2,1,0:T(8,128)} %param.70) | copy-start | bytes 307204
  2.7 22.3 %collective-permute-start.58 = (f32[672,128]{1,0:T(8,128)S(1)}, f32[672,128]{1,0:T(8,128)S(1)}, u32[]{:S(2)}, u32[]{:S(2)}) collective-permute-start(f32[672,128]{1,0:T(8,128)S(1)} %get-tuple-element.142.b_ref), channel_id=1, source_target_pairs={{0,126},{2,0},{4,2},{6,4},{8,6},{10,8},{12,10},{14,12},{16,14},{18... | collective-permute-start | bytes 1032200 | tf_op jit(solution)/shard_map/ppermute | solution.py:235
  6.1 18.0 %collective-permute-start.57 = (f32[480,128]{1,0:T(8,128)S(1)}, f32[480,128]{1,0:T(8,128)S(1)}, u32[]{:S(2)}, u32[]{:S(2)}) collective-permute-start(f32[480,128]{1,0:T(8,128)S(1)} %get-tuple-element.141.a_ref), channel_id=1, source_target_pairs={{0,126},{2,0},{4,2},{6,4},{8,6},{10,8},{12,10},{14,12},{16,14},{18... | collective-permute-start | bytes 737288 | tf_op jit(solution)/shard_map/ppermute | solution.py:235
  25.6 16.3 %collective-permute-start.60 = (f32[672,128]{1,0:T(8,128)S(1)}, f32[672,128]{1,0:T(8,128)S(1)}, u32[]{:S(2)}, u32[]{:S(2)}) collective-permute-start(f32[672,128]{1,0:T(8,128)S(1)} %shard_map.79.b_ref), channel_id=1, source_target_pairs={{0,124},{2,126},{4,0},{6,2},{8,4},{10,6},{12,8},{14,10},{16,12},{1... | collective-permute-start | bytes 1032200 | tf_op jit(solution)/shard_map/ppermute | solution.py:235
  27.6 13.6 %collective-permute-start.59 = (f32[480,128]{1,0:T(8,128)S(1)}, f32[480,128]{1,0:T(8,128)S(1)}, u32[]{:S(2)}, u32[]{:S(2)}) collective-permute-start(f32[480,128]{1,0:T(8,128)S(1)} %shard_map.78.a_ref), channel_id=1, source_target_pairs={{0,124},{2,126},{4,0},{6,2},{8,4},{10,6},{12,8},{14,10},{16,12},{1... | collective-permute-start | bytes 737288 | tf_op jit(solution)/shard_map/ppermute | solution.py:235
  42.7 13.8 %collective-permute-start.62 = (f32[672,128]{1,0:T(8,128)S(1)}, f32[672,128]{1,0:T(8,128)S(1)}, u32[]{:S(2)}, u32[]{:S(2)}) collective-permute-start(f32[672,128]{1,0:T(8,128)S(1)} %shard_map.81.b_ref), channel_id=1, source_target_pairs={{0,120},{2,122},{4,124},{6,126},{8,0},{10,2},{12,4},{14,6},{16,8},... | collective-permute-start | bytes 1032200 | tf_op jit(solution)/shard_map/ppermute | solution.py:235
  44.6 11.1 %collective-permute-start.61 = (f32[480,128]{1,0:T(8,128)S(1)}, f32[480,128]{1,0:T(8,128)S(1)}, u32[]{:S(2)}, u32[]{:S(2)}) collective-permute-start(f32[480,128]{1,0:T(8,128)S(1)} %shard_map.80.a_ref), channel_id=1, source_target_pairs={{0,120},{2,122},{4,124},{6,126},{8,0},{10,2},{12,4},{14,6},{16,8},... | collective-permute-start | bytes 737288 | tf_op jit(solution)/shard_map/ppermute | solution.py:235
  57.2 21.0 %collective-permute-start.64 = (f32[672,128]{1,0:T(8,128)S(1)}, f32[672,128]{1,0:T(8,128)S(1)}, u32[]{:S(2)}, u32[]{:S(2)}) collective-permute-start(f32[672,128]{1,0:T(8,128)S(1)} %shard_map.83.b_ref), channel_id=1, source_target_pairs={{0,112},{2,114},{4,116},{6,118},{8,120},{10,122},{12,124},{14,126}... | collective-permute-start | bytes 1032200 | tf_op jit(solution)/shard_map/ppermute | solution.py:235
  59.1 18.3 %collective-permute-start.63 = (f32[480,128]{1,0:T(8,128)S(1)}, f32[480,128]{1,0:T(8,128)S(1)}, u32[]{:S(2)}, u32[]{:S(2)}) collective-permute-start(f32[480,128]{1,0:T(8,128)S(1)} %shard_map.82.a_ref), channel_id=1, source_target_pairs={{0,112},{2,114},{4,116},{6,118},{8,120},{10,122},{12,124},{14,126}... | collective-permute-start | bytes 737288 | tf_op jit(solution)/shard_map/ppermute | solution.py:235
  78.2 11.6 %copy-start.1 = (f32[1,1,1,80,320]{4,3,2,1,0:T(8,128)S(1)}, f32[1,1,1,80,320]{4,3,2,1,0:T(8,128)}, u32[]{:S(2)}) copy-start(f32[1,1,1,80,320]{4,3,2,1,0:T(8,128)} %param.69) | copy-start | bytes 307204
  79.1 33.5 %collective-permute-start.66 = (f32[672,128]{1,0:T(8,128)S(1)}, f32[672,128]{1,0:T(8,128)S(1)}, u32[]{:S(2)}, u32[]{:S(2)}) collective-permute-start(f32[672,128]{1,0:T(8,128)S(1)} %shard_map.85.b_ref), channel_id=1, source_target_pairs={{0,96},{2,98},{4,100},{6,102},{8,104},{10,106},{12,108},{14,110},{... | collective-permute-start | bytes 1032200 | tf_op jit(solution)/shard_map/ppermute | solution.py:235
  81.1 30.7 %collective-permute-start.65 = (f32[480,128]{1,0:T(8,128)S(1)}, f32[480,128]{1,0:T(8,128)S(1)}, u32[]{:S(2)}, u32[]{:S(2)}) collective-permute-start(f32[480,128]{1,0:T(8,128)S(1)} %shard_map.84.a_ref), channel_id=1, source_target_pairs={{0,96},{2,98},{4,100},{6,102},{8,104},{10,106},{12,108},{14,110},{... | collective-permute-start | bytes 737288 | tf_op jit(solution)/shard_map/ppermute | solution.py:235
  89.8 41.3 %collective-permute-start.68 = (f32[80,320]{1,0:T(8,128)S(1)}, f32[80,320]{1,0:T(8,128)S(1)}, u32[]{:S(2)}, u32[]{:S(2)}) collective-permute-start(f32[80,320]{1,0:T(8,128)S(1)} %bitcast.42), channel_id=1, source_target_pairs={{0,66},{2,68},{4,70},{6,72},{8,74},{10,76},{12,78},{14,80},{16,82}... | collective-permute-start | bytes 307208 | tf_op jit(solution)/shard_map/ppermute | solution.py:266
  113.3 6.8 %copy-start.2 = (s32[3]{0:T(128)S(1)}, s32[3]{0:T(128)}, u32[]{:S(2)}) copy-start(s32[3]{0:T(128)} %param.71) | copy-start | bytes 40
  113.4 17.2 %collective-permute-start.67 = (f32[320,128]{1,0:T(8,128)S(1)}, f32[320,128]{1,0:T(8,128)S(1)}, u32[]{:S(2)}, u32[]{:S(2)}) collective-permute-start(f32[320,128]{1,0:T(8,128)S(1)} %pad_maximum_fusion), channel_id=1, source_target_pairs={{0,64},{2,66},{4,68},{6,70},{8,72},{10,74},{12,76},{14,78},{16,80}... | collective-permute-start | bytes 491528 | tf_op jit(solution)/shard_map/ppermute | solution.py:280
  131.5 1.3 collective-permute-start.2
  133.5 10.7 %collective-permute-start.14 = (f32[80,128]{1,0:T(8,128)S(1)}, f32[80,128]{1,0:T(8,128)S(1)}, u32[]{:S(2)}, u32[]{:S(2)}) collective-permute-start(f32[80,128]{1,0:T(8,128)S(1)} %param.15), channel_id=1, source_target_pairs={{128,216},{130,218},{132,220},{134,222},{136,224},{138,226},{140,2... | collective-permute-start | bytes 122888 | tf_op jit(solution)/shard_map/cond/branch_11_fun/ppermute | solution.py:213
  144.5 22.6 %collective-permute-start.21 = (f32[80,128]{1,0:T(8,128)S(1)}, f32[80,128]{1,0:T(8,128)}, u32[]{:S(2)}, u32[]{:S(2)}) collective-permute-start(f32[80,128]{1,0:T(8,128)S(1)} %param.22), channel_id=1, source_target_pairs={{128,260},{130,262},{132,264},{134,266},{136,268},{138,270},{140,2... | collective-permute-start | bytes 122888 | tf_op jit(solution)/shard_map/cond/branch_2_fun/ppermute | solution.py:203
  167.1 13.0 %collective-permute-start.27 = (f32[80,128]{1,0:T(8,128)}, f32[80,128]{1,0:T(8,128)S(1)}, u32[]{:S(2)}, u32[]{:S(2)}) collective-permute-start(f32[80,128]{1,0:T(8,128)} %param.29), channel_id=1, source_target_pairs={{128,168},{130,170},{132,172},{134,174},{136,176},{138,178},{140,1... | collective-permute-start | bytes 122888 | tf_op jit(solution)/shard_map/cond/branch_5_fun/ppermute | solution.py:213
  181.6 17.5 %collective-permute-start.69 = (f32[320,128]{1,0:T(8,128)S(1)}, f32[320,128]{1,0:T(8,128)S(1)}, u32[]{:S(2)}, u32[]{:S(2)}) collective-permute-start(f32[320,128]{1,0:T(8,128)S(1)} %shard_map.88), channel_id=1, source_target_pairs={{0,62},{2,64},{4,66},{6,68},{8,70},{10,72},{12,74},{14,76},{16,78}... | collective-permute-start | bytes 491528 | tf_op jit(solution)/shard_map/ppermute | solution.py:297
  182.3 6.9 %collective-permute-start.38 = (f32[80,128]{1,0:T(8,128)S(1)}, f32[80,128]{1,0:T(8,128)}, u32[]{:S(2)}, u32[]{:S(2)}) collective-permute-start(f32[80,128]{1,0:T(8,128)S(1)} %param.40), channel_id=1, source_target_pairs={{128,256},{130,258},{132,260},{134,262},{136,264},{138,266},{140,2... | collective-permute-start | bytes 122888 | tf_op jit(solution)/shard_map/cond/branch_0_fun/ppermute | solution.py:203
  189.3 9.1 %collective-permute-start.44 = (f32[80,128]{1,0:T(8,128)}, f32[80,128]{1,0:T(8,128)S(1)}, u32[]{:S(2)}, u32[]{:S(2)}) collective-permute-start(f32[80,128]{1,0:T(8,128)} %param.47), channel_id=1, source_target_pairs={{128,152},{130,154},{132,156},{134,158},{136,160},{138,162},{140,1... | collective-permute-start | bytes 122888 | tf_op jit(solution)/shard_map/cond/branch_3_fun/ppermute | solution.py:213

commit v4 on v3

--- a/solution.py
+++ b/solution.py
@@ -113,53 +113,99 @@
     return state
 
 
-def join_a_kernel(n, mirrored_ref, a_ref, b_ref, got_ref, out_ref, head_ref=None):
+def join_a_kernel(n, mirrored_ref, a_ref, b_ref, got_ref, out_ref):
     @pl.when(mirrored_ref[0] == 0)
     def _():
         matrix = forward_matrix(a_ref, b_ref, n)
         both = dot(matrix, jnp.concatenate([got_ref[0:n], unfold(got_ref[n : n + n // 2])], axis=1))
-        state = a_ref[0:n] + both[:, 0:LANES]
-        put_forward_a(out_ref, n, state, both[:, LANES:])
-        if head_ref is not None:
-            head_ref[...] = state[0:HEAD]
-
-    @pl.when(mirrored_ref[0] != 0)
-    def _():
-        state = join_mirrored(n, HEAD, a_ref, b_ref, got_ref, out_ref)
-        if head_ref is not None:
-            head_ref[...] = state
-
-
-def join_b_kernel(n, mirrored_ref, a_ref, b_ref, got_ref, *refs):
-    new_a_ref, out_ref, rest_ref = refs if len(refs) == 3 else (None, refs[0], None)
-
+        put_forward_a(out_ref, n, a_ref[0:n] + both[:, 0:LANES], both[:, LANES:])
+
+    @pl.when(mirrored_ref[0] != 0)
+    def _():
+        join_mirrored(n, HEAD, a_ref, b_ref, got_ref, out_ref)
+
+
+def join_b_kernel(n, mirrored_ref, a_ref, b_ref, got_ref, out_ref):
     @pl.when(mirrored_ref[0] == 0)
     def _():
         matrix = forward_matrix(a_ref, b_ref, n)
         both = dot(matrix, jnp.concatenate([got_ref[0:n], got_ref[n : 2 * n]], axis=1))
         put_forward_b(out_ref, n, both[:, 0:LANES], both[:, LANES:])
-        if rest_ref is not None:
-            rest_ref[...] = new_a_ref[HEAD:n]
-
-    @pl.when(mirrored_ref[0] != 0)
-    def _():
-        state = join_mirrored(n, n - HEAD, a_ref, b_ref, got_ref, out_ref)
-        if rest_ref is not None:
-            rest_ref[...] = state
-
-
-def close_kernel(mirrored_ref, a_ref, b_ref, got_ref, out_ref):
+
+    @pl.when(mirrored_ref[0] != 0)
+    def _():
+        join_mirrored(n, n - HEAD, a_ref, b_ref, got_ref, out_ref)
+
+
+def split_kernel(n, mirrored_ref, band_ref, a_ref, b_ref, got_ref, new_a_ref, m_ref, s_ref, half_ref):
+    m = n + n // 2
+
+    @pl.when(mirrored_ref[0] == 0)
+    def _():
+        matrix = forward_matrix(a_ref, b_ref, n)
+        both = dot(matrix, jnp.concatenate([got_ref[0:n], got_ref[n : 2 * n]], axis=1))
+        m_ref[0:n] = both[:, 0:LANES]
+        m_ref[n : 2 * n] = both[:, LANES:]
+        m_ref[2 * n :] = new_a_ref[n:m]
+        s_ref[...] = new_a_ref[0:n]
+
+    @pl.when(mirrored_ref[0] != 0)
+    def _():
+        got = mirrored_parts(got_ref, n - HEAD)
+        own = mirrored_all(a_ref, b_ref, n)
+        both = dot(
+            jnp.concatenate(got[:3], axis=1), jnp.concatenate([own[0], own[1], own[3], own[2]], axis=1)
+        )
+        top = mirrored_parts(new_a_ref, HEAD)
+        m_ref[0:HEAD] = top[0]
+        m_ref[HEAD:n] = both[:, 0:LANES]
+        m_ref[n : n + HEAD] = top[1]
+        m_ref[n + HEAD : 2 * n] = both[:, LANES : 2 * LANES]
+        m_ref[2 * n :] = fold(jnp.concatenate([top[2], both[:, 3 * LANES :]], axis=0))
+        s_ref[0:HEAD] = top[3]
+        s_ref[HEAD:n] = got[3] + both[:, 2 * LANES : 3 * LANES]
+
+    count = half_ref.shape[0]
+    half_ref[...] = m_ref[pl.ds(pl.multiple_of(band_ref[0] * count, 8), count)]
+
+
+def whole(ref, n):
+    return jnp.concatenate([ref[0:n], ref[n : 2 * n], unfold(ref[2 * n :])], axis=1)
+
+
+def put_halves(band_ref, mine_ref, other_ref, both_ref):
+    count = mine_ref.shape[0]
+    both_ref[pl.ds(pl.multiple_of(band_ref[0] * count, 8), count)] = mine_ref[...]
+    both_ref[pl.ds(pl.multiple_of((1 - band_ref[0]) * count, 8), count)] = other_ref[...]
+
+
+def state_kernel(mirrored_ref, band_ref, m_ref, s_ref, mine_ref, other_ref, got_ref, out_ref, gotm_ref):
+    n = s_ref.shape[0]
+    put_halves(band_ref, mine_ref, other_ref, gotm_ref)
+
+    @pl.when(mirrored_ref[0] == 0)
+    def _():
+        out_ref[...] = s_ref[...] + dot(whole(m_ref, n), got_ref[...])
+
+    @pl.when(mirrored_ref[0] != 0)
+    def _():
+        out_ref[...] = got_ref[...] + dot(whole(gotm_ref, n), s_ref[...])
+
+
+def square_kernel(mirrored_ref, m_ref, gotm_ref, out_ref):
     n = out_ref.shape[0]
-    got = got_ref[...]
-
-    @pl.when(mirrored_ref[0] == 0)
-    def _():
-        out_ref[...] = a_ref[0:n] + dot(forward_matrix(a_ref, b_ref, n), got)
-
-    @pl.when(mirrored_ref[0] != 0)
-    def _():
-        own = mirrored_all(a_ref, b_ref, n)
-        out_ref[...] = own[3] + dot(jnp.concatenate(own[:3], axis=1), got)
+
+    @pl.when(mirrored_ref[0] == 0)
+    def _():
+        out_ref[...] = dot(whole(m_ref, n), whole(gotm_ref, n))
+
+    @pl.when(mirrored_ref[0] != 0)
+    def _():
+        out_ref[...] = dot(whole(gotm_ref, n), whole(m_ref, n))
+
+
+def close_kernel(m_ref, s_ref, got_ref, out_ref):
+    out_ref[...] = s_ref[...] + dot(m_ref[...], got_ref[...])
 
 
 VMEM = pl.BlockSpec(memory_space=pltpu.VMEM)
@@ -202,18 +248,19 @@
         ]
         return lax.ppermute(trace, ("row", "sector"), route)
 
-    return lax.switch(shift % FINE, [functools.partial(send, k) for k in range(FINE)], trace)
+    return lax.switch(shift & (FINE - 1), [functools.partial(send, k) for k in range(FINE)], trace)
 
 
 def turn(trace, shift, rows, sectors):
     def send(step, trace):
         if step == 0:
             return trace
-        route = sector_route(rows, sectors, lambda row: step if row else None)
+        first = 0 if step == sectors // 2 else 1
+        route = sector_route(rows, sectors, lambda row: step if row >= first else None)
         return lax.ppermute(trace, ("row", "sector"), route)
 
     steps = [functools.partial(send, k) for k in range(0, sectors, FINE)]
-    return lax.switch(shift // FINE, steps, trace)
+    return lax.switch(shift >> 2, steps, trace)
 
 
 def on_device(residual, block_inverse, cycle_coupling, outlet_flux, inlet_lift, mortar_shift):
@@ -253,34 +300,57 @@
     join_a = functools.partial(join_a_kernel, n)
     join_b = functools.partial(join_b_kernel, n)
 
-    def step_a(level, *blocks):
-        shapes = [rows_a] if level < last else [rows_a, (HEAD, LANES)]
-        return call(join_a, [SMEM] + [VMEM] * 3, shapes, mirrored, *blocks)
-
-    def step_b(level, *blocks):
-        shapes = [rows_b] if level < last else [rows_b, (n - HEAD, LANES)]
-        return call(join_b, [SMEM] + [VMEM] * len(blocks), shapes, mirrored, *blocks)
+    def step(kernel, shapes, *blocks):
+        return call(kernel, [SMEM] + [VMEM] * len(blocks), shapes, mirrored, *blocks)
 
     got_a = move(a, 1)
     got_b = move(b, 1)
     early = lax.ppermute(
         flux, axes, sector_route(rows, sectors, lambda row: None if row else 1 - half)
     )
-    for level in range(1, last):
-        new_a = step_a(level, a, b, got_a)
+    for level in range(1, last - 1):
+        new_a = step(join_a, [rows_a], a, b, got_a)
         next_a = move(new_a, 2**level)
         got_b = lax.optimization_barrier((got_b, new_a))[0]
-        new_b = step_b(level, a, b, got_b)
+        new_b = step(join_b, [rows_b], a, b, got_b)
         next_b = move(new_b, 2**level)
         a, b, got_a, got_b = new_a, new_b, next_a, next_b
-    new_a, top = step_a(last, a, b, got_a)
+
+    new_a = step(join_a, [rows_a], a, b, got_a)
     got_b = lax.optimization_barrier((got_b, new_a))[0]
-    new_b, low = step_b(last, a, b, got_b, new_a)
-    window = jnp.concatenate([top, low], axis=0)
-    got = lax.ppermute(window, axes, sector_route(rows, sectors, lambda row: half))
-    state = call(close_kernel, [SMEM] + [VMEM] * 3, [(n, LANES)], mirrored, new_a, new_b, got)
-
-    shifts = jnp.remainder(mortar_shift, sectors)
+    count = n + n // 4
+    band = jnp.reshape(lax.axis_index("band"), (1,)).astype(jnp.int32)
+    matrix, state, mine = call(
+        functools.partial(split_kernel, n),
+        [SMEM] * 2 + [VMEM] * 4,
+        [(2 * count, LANES), (n, LANES), (count, LANES)],
+        mirrored,
+        band,
+        a,
+        b,
+        got_b,
+        new_a,
+    )
+    got_mine = move(mine, half // 2)
+    got = move(state, half // 2)
+    got_other = lax.ppermute(got_mine, "band", [(0, 1), (1, 0)])
+    state, got_matrix = call(
+        state_kernel,
+        [SMEM] * 2 + [VMEM] * 5,
+        [(n, LANES), (2 * count, LANES)],
+        mirrored,
+        band,
+        matrix,
+        state,
+        got_mine,
+        got_other,
+        got,
+    )
+    got = lax.ppermute(state, axes, sector_route(rows, sectors, lambda row: half))
+    matrix = step(square_kernel, [(n, n)], matrix, got_matrix)
+    state = call(close_kernel, [VMEM] * 3, [(n, LANES)], matrix, state, got)
+
+    shifts = mortar_shift & (sectors - 1)
     gain = dot(flux, lift)
     base = dot(jnp.where(row_index == 0, early, flux), state)
     inlet = jnp.zeros_like(base)
@@ -289,7 +359,7 @@
         shift = shifts[section - 1]
         senders = [0] if section == 1 else range(1, rows - 1)
         if section == 1:
-            shift = (shift + half - 1) % sectors
+            shift = (shift + half - 1) & (sectors - 1)
         moved = hop(leaving, shift, senders, sectors)
         if section == 1:
             going, moved = lax.optimization_barrier((state, moved))

time: 205 us -> 200 us (0.976); the launches traced: 201 us -> 199 us
  between operations: 6.65 us -> 4.24 us
    ppermute x1 -> x2, waiting for transfers between devices: 4.22 us -> 16.6 us  [the longest x1 11.9 us: on_device(): lax.ppermute(state, axes, sector_route(rows, sectors, lambda row: half))]
    ppermute x10, waiting for transfers between devices: 71.5 us -> 60.2 us  [move(): return lax.ppermute(block, axes, route)]
    ppermute x1 -> x2, starting transfers between devices: 6.71 us -> 5.08 us  [the longest x1 2.64 us: on_device(): got_other = lax.ppermute(got_mine, 'band', [(0, 1), (1, 0)])]
  transfers between devices with their start and end apart: 19 -> 20, of which waited for: 11 -> 12; matrix products, arithmetic and copies ran while one was open for 1% -> 1% of each run, Pallas kernels for 3% -> 3%
where the time goes in v4:
time: 200 us; the launch traced here: 199 us
  waiting for transfers between devices  130 us (65%)
  starting transfers between devices  47.5 us (24%)
  Pallas kernels  10.5 us (5%)
  between operations  4.24 us (2%)
  matrix products  3.09 us (2%)
    ppermute x10, waiting for transfers between devices, move(): return lax.ppermute(block, axes, route)  60.2 us
    ppermute x6, waiting for transfers between devices, send(): return lax.ppermute(trace, ('row', 'sector'), route)  53.7 us
    ppermute x10, starting transfers between devices, move(): return lax.ppermute(block, axes, route)  30.3 us
    ppermute x1, waiting for transfers between devices, on_device(): lax.ppermute(state, axes, sector_route(rows, sectors, lambda row: half))  11.9 us
    ppermute x6, starting transfers between devices, send(): return lax.ppermute(trace, ('row', 'sector'), route)  10.8 us
    pallas_call x12, Pallas kernels, call(): pl.pallas_call(kernel, out_shape=shapes, in_specs=specs, out_specs=[VMEM]...  10.5 us
    ppermute x1, waiting for transfers between devices, on_device(): got_other = lax.ppermute(got_mine, 'band', [(0, 1), (1, 0)])  4.69 us
  transfers between devices with their start and end apart: 20, of which 12 were waited for; matrix products, arithmetic and copies ran while one was open for 1% of the time, Pallas kernels for 3%

profile of v4, /device:TPU:24, one launch (start us, length us, event | category | flops | bytes accessed | tf_op | source)
XLA Modules:
  0.0 199.5 jit_solution(5617091469270275098)
XLA Ops:
  0.7 2.0 shard_map.77
  2.7 3.4 %collective-permute-start.58 = (f32[672,128]{1,0:T(8,128)S(1)}, f32[672,128]{1,0:T(8,128)S(1)}, u32[]{:S(2)}, u32[]{:S(2)}) collective-permute-start(f32[672,128]{1,0:T(8,128)S(1)} %get-tuple-element.142.b_ref), channel_id=1, source_target_pairs={{0,126},{2,0},{4,2},{6,4},{8,6},{10,8},{12,10},{14,12},{16,14},{18... | collective-permute-start | bytes 1032200 | tf_op jit(solution)/shard_map/ppermute | solution.py:282
  6.1 3.4 %collective-permute-start.57 = (f32[480,128]{1,0:T(8,128)S(1)}, f32[480,128]{1,0:T(8,128)S(1)}, u32[]{:S(2)}, u32[]{:S(2)}) collective-permute-start(f32[480,128]{1,0:T(8,128)S(1)} %get-tuple-element.141.a_ref), channel_id=1, source_target_pairs={{0,126},{2,0},{4,2},{6,4},{8,6},{10,8},{12,10},{14,12},{16,14},{18... | collective-permute-start | bytes 737288 | tf_op jit(solution)/shard_map/ppermute | solution.py:282
  9.5 14.6 %collective-permute-done.57.got_ref = f32[480,128]{1,0:T(8,128)S(1)} collective-permute-done((f32[480,128]{1,0:T(8,128)S(1)}, f32[480,128]{1,0:T(8,128)S(1)}, u32[]{:S(2)}, u32[]{:S(2)}) %collective-permute-start.57) | collective-permute-done | bytes 245792 | tf_op jit(solution)/shard_map/ppermute | solution.py:282
  24.1 0.8 shard_map.78.a_ref
  25.7 1.9 collective-permute-start.60
  27.6 1.9 collective-permute-start.59
  29.5 11.6 %collective-permute-done.59.got_ref = f32[480,128]{1,0:T(8,128)S(1)} collective-permute-done((f32[480,128]{1,0:T(8,128)S(1)}, f32[480,128]{1,0:T(8,128)S(1)}, u32[]{:S(2)}, u32[]{:S(2)}) %collective-permute-start.59) | collective-permute-done | bytes 245792 | tf_op jit(solution)/shard_map/ppermute | solution.py:282
  41.1 0.8 shard_map.80.a_ref
  42.7 1.9 collective-permute-start.62
  44.6 1.9 collective-permute-start.61
  46.5 9.1 %collective-permute-done.61.got_ref = f32[480,128]{1,0:T(8,128)S(1)} collective-permute-done((f32[480,128]{1,0:T(8,128)S(1)}, f32[480,128]{1,0:T(8,128)S(1)}, u32[]{:S(2)}, u32[]{:S(2)}) %collective-permute-start.61) | collective-permute-done | bytes 245792 | tf_op jit(solution)/shard_map/ppermute | solution.py:282
  55.7 0.8 shard_map.82.a_ref
  56.5 0.7 shard_map.83.b_ref
  57.2 1.9 collective-permute-start.63
  59.1 3.2 %collective-permute-start.64 = (f32[480,128]{1,0:T(8,128)S(1)}, f32[480,128]{1,0:T(8,128)S(1)}, u32[]{:S(2)}, u32[]{:S(2)}) collective-permute-start(f32[480,128]{1,0:T(8,128)S(1)} %shard_map.82.a_ref), channel_id=1, source_target_pairs={{0,112},{2,114},{4,116},{6,118},{8,120},{10,122},{12,124},{14,126}... | collective-permute-start | bytes 737288 | tf_op jit(solution)/shard_map/ppermute | solution.py:282
  62.3 15.1 %collective-permute-done.64.got_ref = f32[480,128]{1,0:T(8,128)S(1)} collective-permute-done((f32[480,128]{1,0:T(8,128)S(1)}, f32[480,128]{1,0:T(8,128)S(1)}, u32[]{:S(2)}, u32[]{:S(2)}) %collective-permute-start.64) | collective-permute-done | bytes 245792 | tf_op jit(solution)/shard_map/ppermute | solution.py:282
  77.4 0.8 shard_map.84.new_a_ref
  78.2 0.9 shard_map.85
  79.2 1.9 collective-permute-start.65
  81.8 8.8 %collective-permute-start.67 = (f32[320,128]{1,0:T(8,128)S(1)}, f32[320,128]{1,0:T(8,128)S(1)}, u32[]{:S(2)}, u32[]{:S(2)}) collective-permute-start(f32[320,128]{1,0:T(8,128)S(1)} %get-tuple-element.148.s_ref), channel_id=1, source_target_pairs={{0,96},{2,98},{4,100},{6,102},{8,104},{10,106},{12,108},{14,110},{... | collective-permute-start | bytes 491528 | tf_op jit(solution)/shard_map/ppermute | solution.py:282
  90.5 9.7 %collective-permute-done.65.mine_ref = f32[400,128]{1,0:T(8,128)S(1)} collective-permute-done((f32[400,128]{1,0:T(8,128)S(1)}, f32[400,128]{1,0:T(8,128)S(1)}, u32[]{:S(2)}, u32[]{:S(2)}) %collective-permute-start.65) | collective-permute-done | bytes 204832 | tf_op jit(solution)/shard_map/ppermute | solution.py:282
  100.2 2.6 %collective-permute-start.66 = (f32[400,128]{1,0:T(8,128)S(1)}, f32[400,128]{1,0:T(8,128)S(1)}, u32[]{:S(2)}, u32[]{:S(2)}) collective-permute-start(f32[400,128]{1,0:T(8,128)S(1)} %collective-permute-done.65.mine_ref), channel_id=1, source_target_pairs={{0,1},{1,0},{2,3},{3,2},{4,5},{5,4},{6,7},{7,6},{8,9},{9,8},{10,11... | collective-permute-start | bytes 614408 | tf_op jit(solution)/shard_map/ppermute | solution.py:336
  103.2 4.7 %collective-permute-done.66.other_ref = f32[400,128]{1,0:T(8,128)S(1)} collective-permute-done((f32[400,128]{1,0:T(8,128)S(1)}, f32[400,128]{1,0:T(8,128)S(1)}, u32[]{:S(2)}, u32[]{:S(2)}) %collective-permute-start.66) | collective-permute-done | bytes 204832 | tf_op jit(solution)/shard_map/ppermute | solution.py:336
  108.5 2.4 %collective-permute-start.68 = (f32[320,128]{1,0:T(8,128)S(1)}, f32[320,128]{1,0:T(8,128)S(1)}, u32[]{:S(2)}, u32[]{:S(2)}) collective-permute-start(f32[320,128]{1,0:T(8,128)S(1)} %get-tuple-element.151.s_ref), channel_id=1, source_target_pairs={{0,64},{2,66},{4,68},{6,70},{8,72},{10,74},{12,76},{14,78},{16,80}... | collective-permute-start | bytes 491528 | tf_op jit(solution)/shard_map/ppermute | solution.py:349
  114.8 1.1 shard_map.87.m_ref
  115.9 11.9 %collective-permute-done.68.got_ref = f32[320,128]{1,0:T(8,128)S(1)} collective-permute-done((f32[320,128]{1,0:T(8,128)S(1)}, f32[320,128]{1,0:T(8,128)S(1)}, u32[]{:S(2)}, u32[]{:S(2)}) %collective-permute-start.68) | collective-permute-done | bytes 163872 | tf_op jit(solution)/shard_map/ppermute | solution.py:349
  128.7 1.3 conditional.6
  128.7 1.3 collective-permute-start.2
  130.0 0.8 broadcast_select_fusion.2
  130.8 10.7 %conditional.7 = (f32[80,128]{1,0:T(8,128)S(1)}) conditional(s32[]{:T(128)} %bitcast.12, f32[80,128]{1,0:T(8,128)S(1)} %broadcast_select_fusion.2, f32[80,128]{1,0:T(8,128)S(1)} %broadcast_select_fusion.2, f32[80,128]{1,0:T(8,128)S(1)} %broadcast_select_fusion.2, f32[80,128]{1,0:T(8,128)S(1)} %broadcast_select_fusion.2, ...), branch_computations={%region_4.5_spmd, %region_5.6_spmd, %region_6.7_spmd, %region_7.8_... | conditional | bytes 245808 | solution.py:263
  130.8 1.9 collective-permute-start.14
  132.7 8.8 %collective-permute-done.14 = f32[80,128]{1,0:T(8,128)S(1)} collective-permute-done((f32[80,128]{1,0:T(8,128)S(1)}, f32[80,128]{1,0:T(8,128)S(1)}, u32[]{:S(2)}, u32[]{:S(2)}) %collective-permute-start.14) | collective-permute-done | bytes 40992 | tf_op jit(solution)/shard_map/cond/branch_11_fun/ppermute | solution.py:260
  141.7 23.7 %conditional.8 = (f32[80,128]{1,0:T(8,128)}) conditional(s32[]{:T(128)} %bitcast.11, f32[80,128]{1,0:T(8,128)S(1)} %convolution_add_fusion.1, f32[80,128]{1,0:T(8,128)S(1)} %convolution_add_fusion.1, f32[80,128]{1,0:T(8,128)S(1)} %convolution_add_fusion.1, f32[80,128]{1,0:T(8,128)S(1)} %convolution_add_fusion.1), branch_computations={%region_20.21_spmd, %region_21.22_spmd, %region_22.23_spmd, %regio... | conditional | bytes 163888 | solution.py:251
  141.7 1.9 collective-permute-start.21
  143.6 21.7 %collective-permute-done.21 = f32[80,128]{1,0:T(8,128)} collective-permute-done((f32[80,128]{1,0:T(8,128)S(1)}, f32[80,128]{1,0:T(8,128)}, u32[]{:S(2)}, u32[]{:S(2)}) %collective-permute-start.21) | collective-permute-done | bytes 40992 | tf_op jit(solution)/shard_map/cond/branch_2_fun/ppermute | solution.py:249
  165.3 12.7 %conditional.9 = (f32[80,128]{1,0:T(8,128)}) conditional(s32[]{:T(128)} %bitcast.10, f32[80,128]{1,0:T(8,128)} %get-tuple-element.159, f32[80,128]{1,0:T(8,128)} %get-tuple-element.159, f32[80,128]{1,0:T(8,128)} %get-tuple-element.159, f32[80,128]{1,0:T(8,128)} %get-tuple-element.159, ...), branch_computations={%region_24.25_spmd, %region_25.26_spmd, %region_26.27_spmd, %regio... | conditional | bytes 245808 | solution.py:263
  165.3 1.9 collective-permute-start.27
  167.2 10.2 %collective-permute-done.27 = f32[80,128]{1,0:T(8,128)S(1)} collective-permute-done((f32[80,128]{1,0:T(8,128)}, f32[80,128]{1,0:T(8,128)S(1)}, u32[]{:S(2)}, u32[]{:S(2)}) %collective-permute-start.27) | collective-permute-done | bytes 40992 | tf_op jit(solution)/shard_map/cond/branch_5_fun/ppermute | solution.py:260
  178.1 0.8 select_select_fusion
  179.7 6.9 %conditional.10 = (f32[80,128]{1,0:T(8,128)}) conditional(s32[]{:T(128)} %bitcast.8, f32[80,128]{1,0:T(8,128)S(1)} %convolution_add_fusion, f32[80,128]{1,0:T(8,128)S(1)} %convolution_add_fusion, f32[80,128]{1,0:T(8,128)S(1)} %convolution_add_fusion, f32[80,128]{1,0:T(8,128)S(1)} %convolution_add_fusion), branch_computations={%region_40.41_spmd, %region_41.42_spmd, %region_42.43_spmd, %regio... | conditional | bytes 163888 | solution.py:251
  179.7 1.9 collective-permute-start.38
  181.6 5.0 %collective-permute-done.38 = f32[80,128]{1,0:T(8,128)} collective-permute-done((f32[80,128]{1,0:T(8,128)S(1)}, f32[80,128]{1,0:T(8,128)}, u32[]{:S(2)}, u32[]{:S(2)}) %collective-permute-start.38) | collective-permute-done | bytes 40992 | tf_op jit(solution)/shard_map/cond/branch_0_fun/ppermute | solution.py:249
  186.7 10.6 %conditional.11 = (f32[80,128]{1,0:T(8,128)}) conditional(s32[]{:T(128)} %bitcast.7, f32[80,128]{1,0:T(8,128)} %get-tuple-element.161, f32[80,128]{1,0:T(8,128)} %get-tuple-element.161, f32[80,128]{1,0:T(8,128)} %get-tuple-element.161, f32[80,128]{1,0:T(8,128)} %get-tuple-element.161, ...), branch_computations={%region_44.45_spmd, %region_45.46_spmd, %region_46.47_spmd, %regio... | conditional | bytes 245808 | solution.py:263
  186.7 1.9 collective-permute-start.44
  188.6 8.1 %collective-permute-done.44 = f32[80,128]{1,0:T(8,128)S(1)} collective-permute-done((f32[80,128]{1,0:T(8,128)}, f32[80,128]{1,0:T(8,128)S(1)}, u32[]{:S(2)}, u32[]{:S(2)}) %collective-permute-start.44) | collective-permute-done | bytes 40992 | tf_op jit(solution)/shard_map/cond/branch_3_fun/ppermute | solution.py:260
  197.4 1.1 fusion.1
  198.6 0.9 fusion.3
  (30 shorter events, 7.0 us)
Async XLA Ops:
  0.6 102.2 %copy-start = (f32[1,1,1,320,80]{3,4,2,1,0:T(8,128)S(1)}, f32[1,1,1,320,80]{3,4,2,1,0:T(8,128)}, u32[]{:S(2)}) copy-start(f32[1,1,1,320,80]{3,4,2,1,0:T(8,128)} %param.70) | copy-start | bytes 307204
  2.7 22.3 %collective-permute-start.58 = (f32[672,128]{1,0:T(8,128)S(1)}, f32[672,128]{1,0:T(8,128)S(1)}, u32[]{:S(2)}, u32[]{:S(2)}) collective-permute-start(f32[672,128]{1,0:T(8,128)S(1)} %get-tuple-element.142.b_ref), channel_id=1, source_target_pairs={{0,126},{2,0},{4,2},{6,4},{8,6},{10,8},{12,10},{14,12},{16,14},{18... | collective-permute-start | bytes 1032200 | tf_op jit(solution)/shard_map/ppermute | solution.py:282
  6.1 18.0 %collective-permute-start.57 = (f32[480,128]{1,0:T(8,128)S(1)}, f32[480,128]{1,0:T(8,128)S(1)}, u32[]{:S(2)}, u32[]{:S(2)}) collective-permute-start(f32[480,128]{1,0:T(8,128)S(1)} %get-tuple-element.141.a_ref), channel_id=1, source_target_pairs={{0,126},{2,0},{4,2},{6,4},{8,6},{10,8},{12,10},{14,12},{16,14},{18... | collective-permute-start | bytes 737288 | tf_op jit(solution)/shard_map/ppermute | solution.py:282
  25.7 16.3 %collective-permute-start.60 = (f32[672,128]{1,0:T(8,128)S(1)}, f32[672,128]{1,0:T(8,128)S(1)}, u32[]{:S(2)}, u32[]{:S(2)}) collective-permute-start(f32[672,128]{1,0:T(8,128)S(1)} %shard_map.79.b_ref), channel_id=1, source_target_pairs={{0,124},{2,126},{4,0},{6,2},{8,4},{10,6},{12,8},{14,10},{16,12},{1... | collective-permute-start | bytes 1032200 | tf_op jit(solution)/shard_map/ppermute | solution.py:282
  27.6 13.6 %collective-permute-start.59 = (f32[480,128]{1,0:T(8,128)S(1)}, f32[480,128]{1,0:T(8,128)S(1)}, u32[]{:S(2)}, u32[]{:S(2)}) collective-permute-start(f32[480,128]{1,0:T(8,128)S(1)} %shard_map.78.a_ref), channel_id=1, source_target_pairs={{0,124},{2,126},{4,0},{6,2},{8,4},{10,6},{12,8},{14,10},{16,12},{1... | collective-permute-start | bytes 737288 | tf_op jit(solution)/shard_map/ppermute | solution.py:282
  42.7 13.8 %collective-permute-start.62 = (f32[672,128]{1,0:T(8,128)S(1)}, f32[672,128]{1,0:T(8,128)S(1)}, u32[]{:S(2)}, u32[]{:S(2)}) collective-permute-start(f32[672,128]{1,0:T(8,128)S(1)} %shard_map.81.b_ref), channel_id=1, source_target_pairs={{0,120},{2,122},{4,124},{6,126},{8,0},{10,2},{12,4},{14,6},{16,8},... | collective-permute-start | bytes 1032200 | tf_op jit(solution)/shard_map/ppermute | solution.py:282
  44.6 11.1 %collective-permute-start.61 = (f32[480,128]{1,0:T(8,128)S(1)}, f32[480,128]{1,0:T(8,128)S(1)}, u32[]{:S(2)}, u32[]{:S(2)}) collective-permute-start(f32[480,128]{1,0:T(8,128)S(1)} %shard_map.80.a_ref), channel_id=1, source_target_pairs={{0,120},{2,122},{4,124},{6,126},{8,0},{10,2},{12,4},{14,6},{16,8},... | collective-permute-start | bytes 737288 | tf_op jit(solution)/shard_map/ppermute | solution.py:282
  57.2 21.0 %collective-permute-start.63 = (f32[672,128]{1,0:T(8,128)S(1)}, f32[672,128]{1,0:T(8,128)S(1)}, u32[]{:S(2)}, u32[]{:S(2)}) collective-permute-start(f32[672,128]{1,0:T(8,128)S(1)} %shard_map.83.b_ref), channel_id=1, source_target_pairs={{0,112},{2,114},{4,116},{6,118},{8,120},{10,122},{12,124},{14,126}... | collective-permute-start | bytes 1032200 | tf_op jit(solution)/shard_map/ppermute | solution.py:282
  59.1 18.3 %collective-permute-start.64 = (f32[480,128]{1,0:T(8,128)S(1)}, f32[480,128]{1,0:T(8,128)S(1)}, u32[]{:S(2)}, u32[]{:S(2)}) collective-permute-start(f32[480,128]{1,0:T(8,128)S(1)} %shard_map.82.a_ref), channel_id=1, source_target_pairs={{0,112},{2,114},{4,116},{6,118},{8,120},{10,122},{12,124},{14,126}... | collective-permute-start | bytes 737288 | tf_op jit(solution)/shard_map/ppermute | solution.py:282
  78.2 2.9 %copy-start.1 = (f32[1,1,1,80,320]{4,3,2,1,0:T(8,128)S(1)}, f32[1,1,1,80,320]{4,3,2,1,0:T(8,128)}, u32[]{:S(2)}) copy-start(f32[1,1,1,80,320]{4,3,2,1,0:T(8,128)} %param.69) | copy-start | bytes 307204
  79.2 21.1 %collective-permute-start.65 = (f32[400,128]{1,0:T(8,128)S(1)}, f32[400,128]{1,0:T(8,128)S(1)}, u32[]{:S(2)}, u32[]{:S(2)}) collective-permute-start(f32[400,128]{1,0:T(8,128)S(1)} %get-tuple-element.149), channel_id=1, source_target_pairs={{0,96},{2,98},{4,100},{6,102},{8,104},{10,106},{12,108},{14,110},{... | collective-permute-start | bytes 614408 | tf_op jit(solution)/shard_map/ppermute | solution.py:282
  81.1 47.3 %collective-permute-start.69 = (f32[80,320]{1,0:T(8,128)S(1)}, f32[80,320]{1,0:T(8,128)S(1)}, u32[]{:S(2)}, u32[]{:S(2)}) collective-permute-start(f32[80,320]{1,0:T(8,128)S(1)} %bitcast.47), channel_id=1, source_target_pairs={{0,66},{2,68},{4,70},{6,72},{8,74},{10,76},{12,78},{14,80},{16,82}... | collective-permute-start | bytes 307208 | tf_op jit(solution)/shard_map/ppermute | solution.py:308
  81.8 21.4 %collective-permute-start.67 = (f32[320,128]{1,0:T(8,128)S(1)}, f32[320,128]{1,0:T(8,128)S(1)}, u32[]{:S(2)}, u32[]{:S(2)}) collective-permute-start(f32[320,128]{1,0:T(8,128)S(1)} %get-tuple-element.148.s_ref), channel_id=1, source_target_pairs={{0,96},{2,98},{4,100},{6,102},{8,104},{10,106},{12,108},{14,110},{... | collective-permute-start | bytes 491528 | tf_op jit(solution)/shard_map/ppermute | solution.py:282
  100.2 7.6 %collective-permute-start.66 = (f32[400,128]{1,0:T(8,128)S(1)}, f32[400,128]{1,0:T(8,128)S(1)}, u32[]{:S(2)}, u32[]{:S(2)}) collective-permute-start(f32[400,128]{1,0:T(8,128)S(1)} %collective-permute-done.65.mine_ref), channel_id=1, source_target_pairs={{0,1},{1,0},{2,3},{3,2},{4,5},{5,4},{6,7},{7,6},{8,9},{9,8},{10,11... | collective-permute-start | bytes 614408 | tf_op jit(solution)/shard_map/ppermute | solution.py:336
  108.5 2.5 %copy-start.2 = (s32[3]{0:T(128)S(1)}, s32[3]{0:T(128)}, u32[]{:S(2)}) copy-start(s32[3]{0:T(128)} %param.71) | copy-start | bytes 40
  108.5 19.4 %collective-permute-start.68 = (f32[320,128]{1,0:T(8,128)S(1)}, f32[320,128]{1,0:T(8,128)S(1)}, u32[]{:S(2)}, u32[]{:S(2)}) collective-permute-start(f32[320,128]{1,0:T(8,128)S(1)} %get-tuple-element.151.s_ref), channel_id=1, source_target_pairs={{0,64},{2,66},{4,68},{6,70},{8,72},{10,74},{12,76},{14,78},{16,80}... | collective-permute-start | bytes 491528 | tf_op jit(solution)/shard_map/ppermute | solution.py:349
  128.7 1.3 collective-permute-start.2
  130.8 10.7 %collective-permute-start.14 = (f32[80,128]{1,0:T(8,128)S(1)}, f32[80,128]{1,0:T(8,128)S(1)}, u32[]{:S(2)}, u32[]{:S(2)}) collective-permute-start(f32[80,128]{1,0:T(8,128)S(1)} %param.15), channel_id=1, source_target_pairs={{128,216},{130,218},{132,220},{134,222},{136,224},{138,226},{140,2... | collective-permute-start | bytes 122888 | tf_op jit(solution)/shard_map/cond/branch_11_fun/ppermute | solution.py:260
  141.7 23.6 %collective-permute-start.21 = (f32[80,128]{1,0:T(8,128)S(1)}, f32[80,128]{1,0:T(8,128)}, u32[]{:S(2)}, u32[]{:S(2)}) collective-permute-start(f32[80,128]{1,0:T(8,128)S(1)} %param.22), channel_id=1, source_target_pairs={{128,260},{130,262},{132,264},{134,266},{136,268},{138,270},{140,2... | collective-permute-start | bytes 122888 | tf_op jit(solution)/shard_map/cond/branch_2_fun/ppermute | solution.py:249
  165.3 12.1 %collective-permute-start.27 = (f32[80,128]{1,0:T(8,128)}, f32[80,128]{1,0:T(8,128)S(1)}, u32[]{:S(2)}, u32[]{:S(2)}) collective-permute-start(f32[80,128]{1,0:T(8,128)} %param.29), channel_id=1, source_target_pairs={{128,168},{130,170},{132,172},{134,174},{136,176},{138,178},{140,1... | collective-permute-start | bytes 122888 | tf_op jit(solution)/shard_map/cond/branch_5_fun/ppermute | solution.py:260
  179.0 18.4 %collective-permute-start.70 = (f32[320,128]{1,0:T(8,128)S(1)}, f32[320,128]{1,0:T(8,128)S(1)}, u32[]{:S(2)}, u32[]{:S(2)}) collective-permute-start(f32[320,128]{1,0:T(8,128)S(1)} %shard_map.88), channel_id=1, source_target_pairs={{0,62},{2,64},{4,66},{6,68},{8,70},{10,72},{12,74},{14,76},{16,78}... | collective-permute-start | bytes 491528 | tf_op jit(solution)/shard_map/ppermute | solution.py:367
  179.7 6.9 %collective-permute-start.38 = (f32[80,128]{1,0:T(8,128)S(1)}, f32[80,128]{1,0:T(8,128)}, u32[]{:S(2)}, u32[]{:S(2)}) collective-permute-start(f32[80,128]{1,0:T(8,128)S(1)} %param.40), channel_id=1, source_target_pairs={{128,256},{130,258},{132,260},{134,262},{136,264},{138,266},{140,2... | collective-permute-start | bytes 122888 | tf_op jit(solution)/shard_map/cond/branch_0_fun/ppermute | solution.py:249
  186.7 10.0 %collective-permute-start.44 = (f32[80,128]{1,0:T(8,128)}, f32[80,128]{1,0:T(8,128)S(1)}, u32[]{:S(2)}, u32[]{:S(2)}) collective-permute-start(f32[80,128]{1,0:T(8,128)} %param.47), channel_id=1, source_target_pairs={{128,152},{130,154},{132,156},{134,158},{136,160},{138,162},{140,1... | collective-permute-start | bytes 122888 | tf_op jit(solution)/shard_map/cond/branch_3_fun/ppermute | solution.py:260

commit v5 on v4

--- a/solution.py
+++ b/solution.py
@@ -31,6 +31,11 @@
 def chunk_rows(n):
     tail = n - HEAD
     return max(n + n // 2, HEAD * 7 // 2), max(2 * n, tail * 7 // 2)
+
+
+def chunks(ref, n):
+    count = chunk_rows(n)[0]
+    return ref.at[0:count], ref.at[count:]
 
 
 def mirrored_parts(ref, h):
@@ -72,9 +77,10 @@
 
 
 def first_kernel(
-    mirrored_ref, inverse_hbm, residual_hbm, coupling_hbm, a_ref, b_ref, inverse, residual, coupling, sems
+    mirrored_ref, inverse_hbm, residual_hbm, coupling_hbm, both_ref, inverse, residual, coupling, sems
 ):
     n = coupling.shape[0]
+    a_ref, b_ref = chunks(both_ref, n)
     copies = [
         pltpu.make_async_copy(source, target, sems.at[i])
         for i, (source, target) in enumerate(
@@ -135,6 +141,14 @@
     @pl.when(mirrored_ref[0] != 0)
     def _():
         join_mirrored(n, n - HEAD, a_ref, b_ref, got_ref, out_ref)
+
+
+def first_join_a_kernel(n, mirrored_ref, both_ref, got_ref, out_ref):
+    join_a_kernel(n, mirrored_ref, *chunks(both_ref, n), chunks(got_ref, n)[0], out_ref)
+
+
+def first_join_b_kernel(n, mirrored_ref, both_ref, got_ref, out_ref):
+    join_b_kernel(n, mirrored_ref, *chunks(both_ref, n), chunks(got_ref, n)[1], out_ref)
 
 
 def split_kernel(n, mirrored_ref, band_ref, a_ref, b_ref, got_ref, new_a_ref, m_ref, s_ref, half_ref):
@@ -179,17 +193,13 @@
     both_ref[pl.ds(pl.multiple_of((1 - band_ref[0]) * count, 8), count)] = other_ref[...]
 
 
-def state_kernel(mirrored_ref, band_ref, m_ref, s_ref, mine_ref, other_ref, got_ref, out_ref, gotm_ref):
-    n = s_ref.shape[0]
+def forward_kernel(m_ref, s_ref, got_ref, out_ref):
+    out_ref[...] = s_ref[...] + dot(whole(m_ref, s_ref.shape[0]), got_ref[...])
+
+
+def mirrored_kernel(band_ref, s_ref, mine_ref, other_ref, got_ref, out_ref, gotm_ref):
     put_halves(band_ref, mine_ref, other_ref, gotm_ref)
-
-    @pl.when(mirrored_ref[0] == 0)
-    def _():
-        out_ref[...] = s_ref[...] + dot(whole(m_ref, n), got_ref[...])
-
-    @pl.when(mirrored_ref[0] != 0)
-    def _():
-        out_ref[...] = got_ref[...] + dot(whole(gotm_ref, n), s_ref[...])
+    out_ref[...] = got_ref[...] + dot(whole(gotm_ref, s_ref.shape[0]), s_ref[...])
 
 
 def square_kernel(mirrored_ref, m_ref, gotm_ref, out_ref):
@@ -236,7 +246,7 @@
 
 
 def is_mirrored(row):
-    return (row + 1) // 2 % 2 == 0
+    return row % 2 == 1
 
 
 def hop(trace, shift, senders, sectors):
@@ -255,8 +265,7 @@
     def send(step, trace):
         if step == 0:
             return trace
-        first = 0 if step == sectors // 2 else 1
-        route = sector_route(rows, sectors, lambda row: step if row >= first else None)
+        route = sector_route(rows, sectors, lambda row: None if is_mirrored(row) else step)
         return lax.ppermute(trace, ("row", "sector"), route)
 
     steps = [functools.partial(send, k) for k in range(0, sectors, FINE)]
@@ -281,10 +290,10 @@
         route = sector_route(rows, sectors, lambda row: -step if is_mirrored(row) else step)
         return lax.ppermute(block, axes, route)
 
-    a, b = call(
+    start = call(
         first_kernel,
         [SMEM, HBM, HBM, HBM],
-        [rows_a, rows_b],
+        [(rows_a[0] + rows_b[0], LANES)],
         mirrored,
         *[
             pltpu.with_memory_space_constraint(block, pltpu.HBM)
@@ -303,12 +312,18 @@
     def step(kernel, shapes, *blocks):
         return call(kernel, [SMEM] + [VMEM] * len(blocks), shapes, mirrored, *blocks)
 
-    got_a = move(a, 1)
-    got_b = move(b, 1)
+    got = move(start, 1)
+    gain = dot(flux, lift)
     early = lax.ppermute(
-        flux, axes, sector_route(rows, sectors, lambda row: None if row else 1 - half)
-    )
-    for level in range(1, last - 1):
+        jnp.concatenate([flux, gain], axis=1),
+        axes,
+        sector_route(rows, sectors, lambda row: 1 - half if row == 1 else None),
+    )
+    a = step(functools.partial(first_join_a_kernel, n), [rows_a], start, got)
+    got_a = move(a, 2)
+    b = step(functools.partial(first_join_b_kernel, n), [rows_b], start, got)
+    got_b = move(b, 2)
+    for level in range(2, last - 1):
         new_a = step(join_a, [rows_a], a, b, got_a)
         next_a = move(new_a, 2**level)
         got_b = lax.optimization_barrier((got_b, new_a))[0]
@@ -331,44 +346,56 @@
         got_b,
         new_a,
     )
+    got = move(state, half // 2)
     got_mine = move(mine, half // 2)
-    got = move(state, half // 2)
+    ahead = call(forward_kernel, [VMEM] * 3, [(n, LANES)], matrix, state, got)
+    route = sector_route(rows, sectors, lambda row: None if is_mirrored(row) else half)
+    got_ahead = lax.ppermute(ahead, axes, route)
     got_other = lax.ppermute(got_mine, "band", [(0, 1), (1, 0)])
-    state, got_matrix = call(
-        state_kernel,
-        [SMEM] * 2 + [VMEM] * 5,
+    behind, got_matrix = call(
+        mirrored_kernel,
+        [SMEM] + [VMEM] * 4,
         [(n, LANES), (2 * count, LANES)],
-        mirrored,
         band,
-        matrix,
         state,
         got_mine,
         got_other,
         got,
     )
-    got = lax.ppermute(state, axes, sector_route(rows, sectors, lambda row: half))
+    route = sector_route(rows, sectors, lambda row: half if is_mirrored(row) else None)
+    got_behind = lax.ppermute(behind, axes, route)
     matrix = step(square_kernel, [(n, n)], matrix, got_matrix)
-    state = call(close_kernel, [VMEM] * 3, [(n, LANES)], matrix, state, got)
-
-    shifts = mortar_shift & (sectors - 1)
-    gain = dot(flux, lift)
-    base = dot(jnp.where(row_index == 0, early, flux), state)
-    inlet = jnp.zeros_like(base)
-    for section in range(1, rows):
-        leaving = base + dot(gain, inlet) if section > 1 else base
-        shift = shifts[section - 1]
-        senders = [0] if section == 1 else range(1, rows - 1)
-        if section == 1:
-            shift = (shift + half - 1) & (sectors - 1)
-        moved = hop(leaving, shift, senders, sectors)
-        if section == 1:
-            going, moved = lax.optimization_barrier((state, moved))
+
+    mask = sectors - 1
+    state = call(close_kernel, [VMEM] * 3, [(n, LANES)], matrix, ahead, got_ahead)
+    shift = (mortar_shift[0] - (half - 1)) & mask
+    moved = hop(turn(dot(flux, state), shift, rows, sectors), shift, [0], sectors)
+    inlet = jnp.where(row_index == 1, moved, 0.0)
+
+    got_behind = lax.optimization_barrier((got_behind, inlet))[0]
+    closed = call(close_kernel, [VMEM] * 3, [(n, LANES)], matrix, behind, got_behind)
+    state = jnp.where(mirror, closed, state)
+    base = dot(jnp.where(row_index == 1, early[:, :n], flux), state)
+    local = jnp.where(row_index == 1, early[:, n:], gain)
+    for section in range(2, rows):
+        leaving = base + dot(local, inlet)
+        shift = mortar_shift[section - 1]
+        if section == 2:
+            shift = shift + (half - 1)
+        shift = shift & mask
+        if is_mirrored(section):
+            leaving = turn(leaving, shift, rows, sectors)
+        moved = hop(leaving, shift, range(1, rows - 1), sectors)
+        if section == 2:
+            going, moved = lax.optimization_barrier((jnp.concatenate([state, inlet], axis=0), moved))
             route = sector_route(rows, sectors, lambda row: half - 1 if is_mirrored(row) else None)
             homed = lax.ppermute(going, axes, route)
             moved = jnp.where(shift >= 0, moved, 0.0)
-        moved = turn(moved, shift, rows, sectors)
+        if not is_mirrored(section):
+            moved = turn(moved, shift, rows, sectors)
         inlet = jnp.where(row_index == section, moved, inlet)
-    state = jnp.where(mirror, homed, state)
+    state = jnp.where(mirror, homed[:n], state)
+    inlet = jnp.where(row_index == 1, homed[n:], inlet)
     current = state + dot(lift, inlet)
     trace = dot(flux, state) + dot(gain, inlet)
     return (current[None, None, None], trace[None, None, None])

time: 200 us -> 184 us (0.920)
  waiting for transfers between devices: 130 us -> 104 us
  starting transfers between devices: 47.5 us -> 58.9 us
    ppermute x6, waiting for transfers between devices: 53.7 us -> 35.7 us  [send(): return lax.ppermute(trace, ('row', 'sector'), route)]
    ppermute x2 -> x3, waiting for transfers between devices: 11.9 us -> 1.78 us  [the longest x1 1.78 us: on_device(): got_ahead = lax.ppermute(ahead, axes, route)]
    ppermute x6, starting transfers between devices: 10.8 us -> 20.8 us  [send(): return lax.ppermute(trace, ('row', 'sector'), route)]
    ppermute x10 -> x9, waiting for transfers between devices: 60.2 us -> 64.8 us  [move(): return lax.ppermute(block, axes, route)]
    ppermute x2 -> x3, starting transfers between devices: 3.11 us -> 7.61 us  [the longest x1 6.27 us: on_device(): got_ahead = lax.ppermute(ahead, axes, route)]
    ppermute x1, waiting for transfers between devices: 4.69 us -> 1.58 us  [on_device(): got_other = lax.ppermute(got_mine, 'band', [(0, 1), (1, 0)])]
    ppermute x10 -> x9, starting transfers between devices: 30.3 us -> 27.2 us  [move(): return lax.ppermute(block, axes, route)]
    pallas_call x12 -> x14, Pallas kernels: 10.5 us -> 11.6 us  [call(): pl.pallas_call(kernel, out_shape=shapes, in_specs=specs, out_specs=[VMEM]...]
  transfers between devices with their start and end apart: 20 -> 20, of which waited for: 12 -> 12; matrix products, arithmetic and copies ran while one was open for 1% -> 1% of each run, Pallas kernels for 3% -> 4%
where the time goes in v5:
time: 184 us; the launch traced here: 183 us
  waiting for transfers between devices  104 us (57%)
  starting transfers between devices  58.9 us (32%)
  Pallas kernels  11.6 us (6%)
  matrix products  3.49 us (2%)
  between operations  2.98 us (2%)
    ppermute x9, waiting for transfers between devices, move(): return lax.ppermute(block, axes, route)  64.8 us
    ppermute x6, waiting for transfers between devices, send(): return lax.ppermute(trace, ('row', 'sector'), route)  35.7 us
    ppermute x9, starting transfers between devices, move(): return lax.ppermute(block, axes, route)  27.2 us
    ppermute x6, starting transfers between devices, send(): return lax.ppermute(trace, ('row', 'sector'), route)  20.8 us
    pallas_call x14, Pallas kernels, call(): pl.pallas_call(kernel, out_shape=shapes, in_specs=specs, out_specs=[VMEM]...  11.6 us
    ppermute x1, starting transfers between devices, on_device(): got_ahead = lax.ppermute(ahead, axes, route)  6.27 us
  transfers between devices with their start and end apart: 20, of which 12 were waited for; matrix products, arithmetic and copies ran while one was open for 1% of the time, Pallas kernels for 4%

profile of v5, /device:TPU:24, one launch (start us, length us, event | category | flops | bytes accessed | tf_op | source)
XLA Modules:
  0.0 182.7 jit_solution(10221220593120514637)
XLA Ops:
  0.7 2.0 %shard_map.77.both_ref = f32[1152,128]{1,0:T(8,128)S(1)} custom-call(s32[1]{0:T(128)} %bitcast.mirrored_ref, f32[320,320]{1,0:T(8,128)} %bitcast.52, f32[320,128]{1,0:T(8,128)} %bitcast.54, f32[320,320]{1,0:T(8,128)} %bitcast.53), custom_call_target="tpu_custom_call" | custom-call | tf_op jit(solution)/shard_map/pallas_call | solution.py:228
  2.6 3.4 %collective-permute-start.57 = (f32[1152,128]{1,0:T(8,128)S(1)}, f32[1152,128]{1,0:T(8,128)S(1)}, u32[]{:S(2)}, u32[]{:S(2)}) collective-permute-start(f32[1152,128]{1,0:T(8,128)S(1)} %shard_map.77.both_ref), channel_id=1, source_target_pairs={{0,2},{2,4},{4,6},{6,8},{8,10},{10,12},{12,14},{14,16},{16,18},{18... | collective-permute-start | bytes 1769480 | tf_op jit(solution)/shard_map/ppermute | solution.py:291
  6.1 18.0 %collective-permute-done.57.got_ref = f32[1152,128]{1,0:T(8,128)S(1)} collective-permute-done((f32[1152,128]{1,0:T(8,128)S(1)}, f32[1152,128]{1,0:T(8,128)S(1)}, u32[]{:S(2)}, u32[]{:S(2)}) %collective-permute-start.57) | collective-permute-done | bytes 589856 | tf_op jit(solution)/shard_map/ppermute | solution.py:291
  24.1 0.7 shard_map.79.b_ref
  24.8 1.9 %collective-permute-start.59 = (f32[672,128]{1,0:T(8,128)S(1)}, f32[672,128]{1,0:T(8,128)S(1)}, u32[]{:S(2)}, u32[]{:S(2)}) collective-permute-start(f32[672,128]{1,0:T(8,128)S(1)} %shard_map.79.b_ref), channel_id=1, source_target_pairs={{0,4},{2,6},{4,8},{6,10},{8,12},{10,14},{12,16},{14,18},{16,20},{1... | collective-permute-start | bytes 1032200 | tf_op jit(solution)/shard_map/ppermute | solution.py:291
  26.7 0.8 shard_map.78.a_ref
  27.6 1.9 %collective-permute-start.58 = (f32[480,128]{1,0:T(8,128)S(1)}, f32[480,128]{1,0:T(8,128)S(1)}, u32[]{:S(2)}, u32[]{:S(2)}) collective-permute-start(f32[480,128]{1,0:T(8,128)S(1)} %shard_map.78.a_ref), channel_id=1, source_target_pairs={{0,4},{2,6},{4,8},{6,10},{8,12},{10,14},{12,16},{14,18},{16,20},{1... | collective-permute-start | bytes 737288 | tf_op jit(solution)/shard_map/ppermute | solution.py:291
  29.5 10.8 %collective-permute-done.58.got_ref = f32[480,128]{1,0:T(8,128)S(1)} collective-permute-done((f32[480,128]{1,0:T(8,128)S(1)}, f32[480,128]{1,0:T(8,128)S(1)}, u32[]{:S(2)}, u32[]{:S(2)}) %collective-permute-start.58) | collective-permute-done | bytes 245792 | tf_op jit(solution)/shard_map/ppermute | solution.py:291
  40.3 0.8 shard_map.80.a_ref
  41.1 0.7 shard_map.81.b_ref
  41.8 1.9 %collective-permute-start.61 = (f32[672,128]{1,0:T(8,128)S(1)}, f32[672,128]{1,0:T(8,128)S(1)}, u32[]{:S(2)}, u32[]{:S(2)}) collective-permute-start(f32[672,128]{1,0:T(8,128)S(1)} %shard_map.81.b_ref), channel_id=1, source_target_pairs={{0,8},{2,10},{4,12},{6,14},{8,16},{10,18},{12,20},{14,22},{16,24},... | collective-permute-start | bytes 1032200 | tf_op jit(solution)/shard_map/ppermute | solution.py:291
  43.8 1.9 %collective-permute-start.60 = (f32[480,128]{1,0:T(8,128)S(1)}, f32[480,128]{1,0:T(8,128)S(1)}, u32[]{:S(2)}, u32[]{:S(2)}) collective-permute-start(f32[480,128]{1,0:T(8,128)S(1)} %shard_map.80.a_ref), channel_id=1, source_target_pairs={{0,8},{2,10},{4,12},{6,14},{8,16},{10,18},{12,20},{14,22},{16,24},... | collective-permute-start | bytes 737288 | tf_op jit(solution)/shard_map/ppermute | solution.py:291
  45.7 9.1 %collective-permute-done.60.got_ref = f32[480,128]{1,0:T(8,128)S(1)} collective-permute-done((f32[480,128]{1,0:T(8,128)S(1)}, f32[480,128]{1,0:T(8,128)S(1)}, u32[]{:S(2)}, u32[]{:S(2)}) %collective-permute-start.60) | collective-permute-done | bytes 245792 | tf_op jit(solution)/shard_map/ppermute | solution.py:291
  54.8 0.8 shard_map.82.a_ref
  55.7 0.7 shard_map.83.b_ref
  56.4 1.9 %collective-permute-start.62 = (f32[672,128]{1,0:T(8,128)S(1)}, f32[672,128]{1,0:T(8,128)S(1)}, u32[]{:S(2)}, u32[]{:S(2)}) collective-permute-start(f32[672,128]{1,0:T(8,128)S(1)} %shard_map.83.b_ref), channel_id=1, source_target_pairs={{0,16},{2,18},{4,20},{6,22},{8,24},{10,26},{12,28},{14,30},{16,32}... | collective-permute-start | bytes 1032200 | tf_op jit(solution)/shard_map/ppermute | solution.py:291
  58.3 3.3 %collective-permute-start.63 = (f32[480,128]{1,0:T(8,128)S(1)}, f32[480,128]{1,0:T(8,128)S(1)}, u32[]{:S(2)}, u32[]{:S(2)}) collective-permute-start(f32[480,128]{1,0:T(8,128)S(1)} %shard_map.82.a_ref), channel_id=1, source_target_pairs={{0,16},{2,18},{4,20},{6,22},{8,24},{10,26},{12,28},{14,30},{16,32}... | collective-permute-start | bytes 737288 | tf_op jit(solution)/shard_map/ppermute | solution.py:291
  61.6 15.0 %collective-permute-done.63.got_ref = f32[480,128]{1,0:T(8,128)S(1)} collective-permute-done((f32[480,128]{1,0:T(8,128)S(1)}, f32[480,128]{1,0:T(8,128)S(1)}, u32[]{:S(2)}, u32[]{:S(2)}) %collective-permute-start.63) | collective-permute-done | bytes 245792 | tf_op jit(solution)/shard_map/ppermute | solution.py:291
  76.6 0.8 shard_map.84.new_a_ref
  77.4 0.9 shard_map.85
  78.3 1.9 %collective-permute-start.64 = (f32[400,128]{1,0:T(8,128)S(1)}, f32[400,128]{1,0:T(8,128)S(1)}, u32[]{:S(2)}, u32[]{:S(2)}) collective-permute-start(f32[400,128]{1,0:T(8,128)S(1)} %get-tuple-element.144), channel_id=1, source_target_pairs={{0,32},{2,34},{4,36},{6,38},{8,40},{10,42},{12,44},{14,46},{16,48}... | collective-permute-start | bytes 614408 | tf_op jit(solution)/shard_map/ppermute | solution.py:291
  80.2 9.0 %collective-permute-start.66 = (f32[320,128]{1,0:T(8,128)S(1)}, f32[320,128]{1,0:T(8,128)S(1)}, u32[]{:S(2)}, u32[]{:S(2)}) collective-permute-start(f32[320,128]{1,0:T(8,128)S(1)} %get-tuple-element.143.s_ref), channel_id=1, source_target_pairs={{0,32},{2,34},{4,36},{6,38},{8,40},{10,42},{12,44},{14,46},{16,48}... | collective-permute-start | bytes 491528 | tf_op jit(solution)/shard_map/ppermute | solution.py:291
  89.5 11.9 %collective-permute-done.66.got_ref = f32[320,128]{1,0:T(8,128)S(1)} collective-permute-done((f32[320,128]{1,0:T(8,128)S(1)}, f32[320,128]{1,0:T(8,128)S(1)}, u32[]{:S(2)}, u32[]{:S(2)}) %collective-permute-start.66) | collective-permute-done | bytes 163872 | tf_op jit(solution)/shard_map/ppermute | solution.py:291
  102.0 6.3 %collective-permute-start.68 = (f32[320,128]{1,0:T(8,128)S(1)}, f32[320,128]{1,0:T(8,128)S(1)}, u32[]{:S(2)}, u32[]{:S(2)}) collective-permute-start(f32[320,128]{1,0:T(8,128)S(1)} %shard_map.88.s_ref), channel_id=1, source_target_pairs={{0,64},{2,66},{4,68},{6,70},{8,72},{10,74},{12,76},{14,78},{16,80}... | collective-permute-start | bytes 491528 | tf_op jit(solution)/shard_map/ppermute | solution.py:353
  108.3 2.7 %collective-permute-start.65 = (f32[400,128]{1,0:T(8,128)S(1)}, f32[400,128]{1,0:T(8,128)S(1)}, u32[]{:S(2)}, u32[]{:S(2)}) collective-permute-start(f32[400,128]{1,0:T(8,128)S(1)} %collective-permute-done.64.mine_ref), channel_id=1, source_target_pairs={{0,1},{1,0},{2,3},{3,2},{4,5},{5,4},{6,7},{7,6},{8,9},{9,8},{10,11... | collective-permute-start | bytes 614408 | tf_op jit(solution)/shard_map/ppermute | solution.py:354
  114.3 1.6 collective-permute-done.65.other_ref
  116.5 1.1 shard_map.87.m_ref
  117.6 1.8 collective-permute-done.68.got_ref
  120.9 13.5 %conditional.6 = (f32[80,128]{1,0:T(8,128)S(1)}) conditional(s32[]{:T(128)} %bitcast.6, f32[80,128]{1,0:T(8,128)S(1)} %convolution_bitcast_fusion.2, f32[80,128]{1,0:T(8,128)S(1)} %convolution_bitcast_fusion.2, f32[80,128]{1,0:T(8,128)S(1)} %convolution_bitcast_fusion.2, ...), branch_computations={%region_0.1_spmd, %region_1.2_spmd, %region_2.3_spmd, %region_3.4_... | conditional | bytes 245808 | solution.py:272
  121.0 11.8 %collective-permute-start.11 = (f32[80,128]{1,0:T(8,128)S(1)}, f32[80,128]{1,0:T(8,128)S(1)}, u32[]{:S(2)}, u32[]{:S(2)}) collective-permute-start(f32[80,128]{1,0:T(8,128)S(1)} %param.12), channel_id=1, source_target_pairs={{0,96},{2,98},{4,100},{6,102},{8,104},{10,106},{12,108},{14,110},{... | collective-permute-start | bytes 122888 | tf_op jit(solution)/shard_map/cond/branch_12_fun/ppermute | solution.py:269
  132.8 1.7 collective-permute-done.11
  134.5 1.3 conditional.7
  134.5 1.3 collective-permute-start.15
  136.9 18.2 %conditional.8 = (f32[80,128]{1,0:T(8,128)}) conditional(s32[]{:T(128)} %bitcast.9, f32[80,128]{1,0:T(8,128)S(1)} %convolution_add_fusion.1, f32[80,128]{1,0:T(8,128)S(1)} %convolution_add_fusion.1, f32[80,128]{1,0:T(8,128)S(1)} %convolution_add_fusion.1, f32[80,128]{1,0:T(8,128)S(1)} %convolution_add_fusion.1), branch_computations={%region_20.21_spmd, %region_21.22_spmd, %region_22.23_spmd, %regio... | conditional | bytes 163888 | solution.py:261
  136.9 1.9 %collective-permute-start.20 = (f32[80,128]{1,0:T(8,128)S(1)}, f32[80,128]{1,0:T(8,128)}, u32[]{:S(2)}, u32[]{:S(2)}) collective-permute-start(f32[80,128]{1,0:T(8,128)S(1)} %param.21), channel_id=1, source_target_pairs={{128,258},{130,260},{132,262},{134,264},{136,266},{138,268},{140,2... | collective-permute-start | bytes 122888 | tf_op jit(solution)/shard_map/cond/branch_1_fun/ppermute | solution.py:259
  138.9 16.3 %collective-permute-done.20 = f32[80,128]{1,0:T(8,128)} collective-permute-done((f32[80,128]{1,0:T(8,128)S(1)}, f32[80,128]{1,0:T(8,128)}, u32[]{:S(2)}, u32[]{:S(2)}) %collective-permute-start.20) | collective-permute-done | bytes 40992 | tf_op jit(solution)/shard_map/cond/branch_1_fun/ppermute | solution.py:259
  155.8 0.8 broadcast_select_fusion.1
  156.6 7.7 %conditional.9 = (f32[80,128]{1,0:T(8,128)S(1)}) conditional(s32[]{:T(128)} %bitcast.13, f32[80,128]{1,0:T(8,128)S(1)} %broadcast_select_fusion.1, f32[80,128]{1,0:T(8,128)S(1)} %broadcast_select_fusion.1, f32[80,128]{1,0:T(8,128)S(1)} %broadcast_select_fusion.1, f32[80,128]{1,0:T(8,128)S(1)} %broadcast_select_fusion.1, ...), branch_computations={%region_24.25_spmd, %region_25.26_spmd, %region_26.27_spmd, %regio... | conditional | bytes 245808 | solution.py:272
  156.6 1.9 %collective-permute-start.35 = (f32[80,128]{1,0:T(8,128)S(1)}, f32[80,128]{1,0:T(8,128)S(1)}, u32[]{:S(2)}, u32[]{:S(2)}) collective-permute-start(f32[80,128]{1,0:T(8,128)S(1)} %param.37), channel_id=1, source_target_pairs={{0,104},{2,106},{4,108},{6,110},{8,112},{10,114},{12,116},{14,118}... | collective-permute-start | bytes 122888 | tf_op jit(solution)/shard_map/cond/branch_13_fun/ppermute | solution.py:269
  158.6 5.8 %collective-permute-done.35 = f32[80,128]{1,0:T(8,128)S(1)} collective-permute-done((f32[80,128]{1,0:T(8,128)S(1)}, f32[80,128]{1,0:T(8,128)S(1)}, u32[]{:S(2)}, u32[]{:S(2)}) %collective-permute-start.35) | collective-permute-done | bytes 40992 | tf_op jit(solution)/shard_map/cond/branch_13_fun/ppermute | solution.py:269
  164.6 9.0 %conditional.10 = (f32[80,128]{1,0:T(8,128)S(1)}) conditional(s32[]{:T(128)} %bitcast.12, f32[80,128]{1,0:T(8,128)S(1)} %convolution_add_fusion, f32[80,128]{1,0:T(8,128)S(1)} %convolution_add_fusion, f32[80,128]{1,0:T(8,128)S(1)} %convolution_add_fusion, f32[80,128]{1,0:T(8,128)S(1)} %convolution_add_fusion, ...), branch_computations={%region_40.41_spmd, %region_41.42_spmd, %region_42.43_spmd, %regio... | conditional | bytes 245808 | solution.py:272
  164.6 1.9 %collective-permute-start.40 = (f32[80,128]{1,0:T(8,128)S(1)}, f32[80,128]{1,0:T(8,128)S(1)}, u32[]{:S(2)}, u32[]{:S(2)}) collective-permute-start(f32[80,128]{1,0:T(8,128)S(1)} %param.43), channel_id=1, source_target_pairs={{0,24},{2,26},{4,28},{6,30},{8,32},{10,34},{12,36},{14,38},{16,40}... | collective-permute-start | bytes 122888 | tf_op jit(solution)/shard_map/cond/branch_3_fun/ppermute | solution.py:269
  166.5 7.0 %collective-permute-done.40 = f32[80,128]{1,0:T(8,128)S(1)} collective-permute-done((f32[80,128]{1,0:T(8,128)S(1)}, f32[80,128]{1,0:T(8,128)S(1)}, u32[]{:S(2)}, u32[]{:S(2)}) %collective-permute-start.40) | collective-permute-done | bytes 40992 | tf_op jit(solution)/shard_map/cond/branch_3_fun/ppermute | solution.py:269
  173.5 6.9 %conditional.11 = (f32[80,128]{1,0:T(8,128)}) conditional(s32[]{:T(128)} %bitcast.11, f32[80,128]{1,0:T(8,128)S(1)} %get-tuple-element.157, f32[80,128]{1,0:T(8,128)S(1)} %get-tuple-element.157, f32[80,128]{1,0:T(8,128)S(1)} %get-tuple-element.157, f32[80,128]{1,0:T(8,128)S(1)} %get-tuple-element.157), branch_computations={%region_56.57_spmd, %region_57.58_spmd, %region_58.59_spmd, %regio... | conditional | bytes 163888 | solution.py:261
  173.5 1.9 %collective-permute-start.53 = (f32[80,128]{1,0:T(8,128)S(1)}, f32[80,128]{1,0:T(8,128)}, u32[]{:S(2)}, u32[]{:S(2)}) collective-permute-start(f32[80,128]{1,0:T(8,128)S(1)} %param.56), channel_id=1, source_target_pairs={{128,256},{130,258},{132,260},{134,262},{136,264},{138,266},{140,2... | collective-permute-start | bytes 122888 | tf_op jit(solution)/shard_map/cond/branch_0_fun/ppermute | solution.py:259
  175.4 5.0 %collective-permute-done.53 = f32[80,128]{1,0:T(8,128)} collective-permute-done((f32[80,128]{1,0:T(8,128)S(1)}, f32[80,128]{1,0:T(8,128)}, u32[]{:S(2)}, u32[]{:S(2)}) %collective-permute-start.53) | collective-permute-done | bytes 40992 | tf_op jit(solution)/shard_map/cond/branch_0_fun/ppermute | solution.py:259
  180.6 1.1 fusion.1
  181.8 0.9 fusion.3
  (36 shorter events, 6.7 us)
Async XLA Ops:
  0.6 88.6 %copy-start = (f32[1,1,1,320,80]{3,4,2,1,0:T(8,128)S(1)}, f32[1,1,1,320,80]{3,4,2,1,0:T(8,128)}, u32[]{:S(2)}) copy-start(f32[1,1,1,320,80]{3,4,2,1,0:T(8,128)} %param.70) | copy-start | bytes 307204
  2.6 21.5 %collective-permute-start.57 = (f32[1152,128]{1,0:T(8,128)S(1)}, f32[1152,128]{1,0:T(8,128)S(1)}, u32[]{:S(2)}, u32[]{:S(2)}) collective-permute-start(f32[1152,128]{1,0:T(8,128)S(1)} %shard_map.77.both_ref), channel_id=1, source_target_pairs={{0,2},{2,4},{4,6},{6,8},{8,10},{10,12},{12,14},{14,16},{16,18},{18... | collective-permute-start | bytes 1769480 | tf_op jit(solution)/shard_map/ppermute | solution.py:291
  24.8 16.3 %collective-permute-start.59 = (f32[672,128]{1,0:T(8,128)S(1)}, f32[672,128]{1,0:T(8,128)S(1)}, u32[]{:S(2)}, u32[]{:S(2)}) collective-permute-start(f32[672,128]{1,0:T(8,128)S(1)} %shard_map.79.b_ref), channel_id=1, source_target_pairs={{0,4},{2,6},{4,8},{6,10},{8,12},{10,14},{12,16},{14,18},{16,20},{1... | collective-permute-start | bytes 1032200 | tf_op jit(solution)/shard_map/ppermute | solution.py:291
  27.6 12.7 %collective-permute-start.58 = (f32[480,128]{1,0:T(8,128)S(1)}, f32[480,128]{1,0:T(8,128)S(1)}, u32[]{:S(2)}, u32[]{:S(2)}) collective-permute-start(f32[480,128]{1,0:T(8,128)S(1)} %shard_map.78.a_ref), channel_id=1, source_target_pairs={{0,4},{2,6},{4,8},{6,10},{8,12},{10,14},{12,16},{14,18},{16,20},{1... | collective-permute-start | bytes 737288 | tf_op jit(solution)/shard_map/ppermute | solution.py:291
  41.8 13.8 %collective-permute-start.61 = (f32[672,128]{1,0:T(8,128)S(1)}, f32[672,128]{1,0:T(8,128)S(1)}, u32[]{:S(2)}, u32[]{:S(2)}) collective-permute-start(f32[672,128]{1,0:T(8,128)S(1)} %shard_map.81.b_ref), channel_id=1, source_target_pairs={{0,8},{2,10},{4,12},{6,14},{8,16},{10,18},{12,20},{14,22},{16,24},... | collective-permute-start | bytes 1032200 | tf_op jit(solution)/shard_map/ppermute | solution.py:291
  43.8 11.1 %collective-permute-start.60 = (f32[480,128]{1,0:T(8,128)S(1)}, f32[480,128]{1,0:T(8,128)S(1)}, u32[]{:S(2)}, u32[]{:S(2)}) collective-permute-start(f32[480,128]{1,0:T(8,128)S(1)} %shard_map.80.a_ref), channel_id=1, source_target_pairs={{0,8},{2,10},{4,12},{6,14},{8,16},{10,18},{12,20},{14,22},{16,24},... | collective-permute-start | bytes 737288 | tf_op jit(solution)/shard_map/ppermute | solution.py:291
  56.4 21.0 %collective-permute-start.62 = (f32[672,128]{1,0:T(8,128)S(1)}, f32[672,128]{1,0:T(8,128)S(1)}, u32[]{:S(2)}, u32[]{:S(2)}) collective-permute-start(f32[672,128]{1,0:T(8,128)S(1)} %shard_map.83.b_ref), channel_id=1, source_target_pairs={{0,16},{2,18},{4,20},{6,22},{8,24},{10,26},{12,28},{14,30},{16,32}... | collective-permute-start | bytes 1032200 | tf_op jit(solution)/shard_map/ppermute | solution.py:291
  58.3 18.3 %collective-permute-start.63 = (f32[480,128]{1,0:T(8,128)S(1)}, f32[480,128]{1,0:T(8,128)S(1)}, u32[]{:S(2)}, u32[]{:S(2)}) collective-permute-start(f32[480,128]{1,0:T(8,128)S(1)} %shard_map.82.a_ref), channel_id=1, source_target_pairs={{0,16},{2,18},{4,20},{6,22},{8,24},{10,26},{12,28},{14,30},{16,32}... | collective-permute-start | bytes 737288 | tf_op jit(solution)/shard_map/ppermute | solution.py:291
  77.4 11.8 %copy-start.1 = (f32[1,1,1,80,320]{4,3,2,1,0:T(8,128)S(1)}, f32[1,1,1,80,320]{4,3,2,1,0:T(8,128)}, u32[]{:S(2)}) copy-start(f32[1,1,1,80,320]{4,3,2,1,0:T(8,128)} %param.69) | copy-start | bytes 307204
  78.3 29.9 %collective-permute-start.64 = (f32[400,128]{1,0:T(8,128)S(1)}, f32[400,128]{1,0:T(8,128)S(1)}, u32[]{:S(2)}, u32[]{:S(2)}) collective-permute-start(f32[400,128]{1,0:T(8,128)S(1)} %get-tuple-element.144), channel_id=1, source_target_pairs={{0,32},{2,34},{4,36},{6,38},{8,40},{10,42},{12,44},{14,46},{16,48}... | collective-permute-start | bytes 614408 | tf_op jit(solution)/shard_map/ppermute | solution.py:291
  80.2 21.2 %collective-permute-start.66 = (f32[320,128]{1,0:T(8,128)S(1)}, f32[320,128]{1,0:T(8,128)S(1)}, u32[]{:S(2)}, u32[]{:S(2)}) collective-permute-start(f32[320,128]{1,0:T(8,128)S(1)} %get-tuple-element.143.s_ref), channel_id=1, source_target_pairs={{0,32},{2,34},{4,36},{6,38},{8,40},{10,42},{12,44},{14,46},{16,48}... | collective-permute-start | bytes 491528 | tf_op jit(solution)/shard_map/ppermute | solution.py:291
  102.0 17.4 %collective-permute-start.68 = (f32[320,128]{1,0:T(8,128)S(1)}, f32[320,128]{1,0:T(8,128)S(1)}, u32[]{:S(2)}, u32[]{:S(2)}) collective-permute-start(f32[320,128]{1,0:T(8,128)S(1)} %shard_map.88.s_ref), channel_id=1, source_target_pairs={{0,64},{2,66},{4,68},{6,70},{8,72},{10,74},{12,76},{14,78},{16,80}... | collective-permute-start | bytes 491528 | tf_op jit(solution)/shard_map/ppermute | solution.py:353
  108.3 7.7 %collective-permute-start.65 = (f32[400,128]{1,0:T(8,128)S(1)}, f32[400,128]{1,0:T(8,128)S(1)}, u32[]{:S(2)}, u32[]{:S(2)}) collective-permute-start(f32[400,128]{1,0:T(8,128)S(1)} %collective-permute-done.64.mine_ref), channel_id=1, source_target_pairs={{0,1},{1,0},{2,3},{3,2},{4,5},{5,4},{6,7},{7,6},{8,9},{9,8},{10,11... | collective-permute-start | bytes 614408 | tf_op jit(solution)/shard_map/ppermute | solution.py:354
  111.0 0.7 copy-start.2
  111.0 25.4 %collective-permute-start.69 = (f32[80,400]{1,0:T(8,128)S(1)}, f32[80,400]{1,0:T(8,128)S(1)}, u32[]{:S(2)}, u32[]{:S(2)}) collective-permute-start(f32[80,400]{1,0:T(8,128)S(1)} %pad_maximum_fusion.1), channel_id=1, source_target_pairs={{128,194},{130,196},{132,198},{134,200},{136,202},{138,204},{140,2... | collective-permute-start | bytes 384008 | tf_op jit(solution)/shard_map/ppermute | solution.py:317
  120.2 15.5 %collective-permute-start.67 = (f32[320,128]{1,0:T(8,128)S(1)}, f32[320,128]{1,0:T(8,128)S(1)}, u32[]{:S(2)}, u32[]{:S(2)}) collective-permute-start(f32[320,128]{1,0:T(8,128)S(1)} %get-tuple-element.146.s_ref), channel_id=1, source_target_pairs={{128,192},{130,194},{132,196},{134,198},{136,200},{138,202},{140,2... | collective-permute-start | bytes 491528 | tf_op jit(solution)/shard_map/ppermute | solution.py:366
  121.0 13.5 %collective-permute-start.11 = (f32[80,128]{1,0:T(8,128)S(1)}, f32[80,128]{1,0:T(8,128)S(1)}, u32[]{:S(2)}, u32[]{:S(2)}) collective-permute-start(f32[80,128]{1,0:T(8,128)S(1)} %param.12), channel_id=1, source_target_pairs={{0,96},{2,98},{4,100},{6,102},{8,104},{10,106},{12,108},{14,110},{... | collective-permute-start | bytes 122888 | tf_op jit(solution)/shard_map/cond/branch_12_fun/ppermute | solution.py:269
  134.5 1.3 collective-permute-start.15
  136.9 18.2 %collective-permute-start.20 = (f32[80,128]{1,0:T(8,128)S(1)}, f32[80,128]{1,0:T(8,128)}, u32[]{:S(2)}, u32[]{:S(2)}) collective-permute-start(f32[80,128]{1,0:T(8,128)S(1)} %param.21), channel_id=1, source_target_pairs={{128,258},{130,260},{132,262},{134,264},{136,266},{138,268},{140,2... | collective-permute-start | bytes 122888 | tf_op jit(solution)/shard_map/cond/branch_1_fun/ppermute | solution.py:259
  155.2 25.3 %collective-permute-start.70 = (f32[400,128]{1,0:T(8,128)S(1)}, f32[400,128]{1,0:T(8,128)S(1)}, u32[]{:S(2)}, u32[]{:S(2)}) collective-permute-start(f32[400,128]{1,0:T(8,128)S(1)} %pad_maximum_fusion), channel_id=1, source_target_pairs={{128,190},{130,192},{132,194},{134,196},{136,198},{138,200},{140,2... | collective-permute-start | bytes 614408 | tf_op jit(solution)/shard_map/ppermute | solution.py:392
  156.6 7.7 %collective-permute-start.35 = (f32[80,128]{1,0:T(8,128)S(1)}, f32[80,128]{1,0:T(8,128)S(1)}, u32[]{:S(2)}, u32[]{:S(2)}) collective-permute-start(f32[80,128]{1,0:T(8,128)S(1)} %param.37), channel_id=1, source_target_pairs={{0,104},{2,106},{4,108},{6,110},{8,112},{10,114},{12,116},{14,118}... | collective-permute-start | bytes 122888 | tf_op jit(solution)/shard_map/cond/branch_13_fun/ppermute | solution.py:269
  164.6 8.9 %collective-permute-start.40 = (f32[80,128]{1,0:T(8,128)S(1)}, f32[80,128]{1,0:T(8,128)S(1)}, u32[]{:S(2)}, u32[]{:S(2)}) collective-permute-start(f32[80,128]{1,0:T(8,128)S(1)} %param.43), channel_id=1, source_target_pairs={{0,24},{2,26},{4,28},{6,30},{8,32},{10,34},{12,36},{14,38},{16,40}... | collective-permute-start | bytes 122888 | tf_op jit(solution)/shard_map/cond/branch_3_fun/ppermute | solution.py:269
  173.5 6.9 %collective-permute-start.53 = (f32[80,128]{1,0:T(8,128)S(1)}, f32[80,128]{1,0:T(8,128)}, u32[]{:S(2)}, u32[]{:S(2)}) collective-permute-start(f32[80,128]{1,0:T(8,128)S(1)} %param.56), channel_id=1, source_target_pairs={{128,256},{130,258},{132,260},{134,262},{136,264},{138,266},{140,2... | collective-permute-start | bytes 122888 | tf_op jit(solution)/shard_map/cond/branch_0_fun/ppermute | solution.py:259

commit v6 on v5

--- a/solution.py
+++ b/solution.py
@@ -14,7 +14,19 @@
 HEAD = 128
 
 
-def dot(a, b):
+def dot(a, b, contract=(1, 0)):
+    dims = (((contract[0],), (contract[1],)), ((), ()))
+
+    def product(x, y):
+        return lax.dot_general(x, y, dims, preferred_element_type=jnp.float32)
+
+    a_high, b_high = a.astype(jnp.bfloat16), b.astype(jnp.bfloat16)
+    a_low = (a - a_high.astype(jnp.float32)).astype(jnp.bfloat16)
+    b_low = (b - b_high.astype(jnp.float32)).astype(jnp.bfloat16)
+    return product(a_high, b_high) + (product(a_high, b_low) + product(a_low, b_high))
+
+
+def exact_dot(a, b):
     return jnp.dot(a, b, precision=HIGH, preferred_element_type=jnp.float32)
 
 
@@ -218,6 +230,59 @@
     out_ref[...] = s_ref[...] + dot(m_ref[...], got_ref[...])
 
 
+def second_kernel(
+    row_ref, m_ref, s_ref, got_ref, ready_ref, moved_ref, early_ref, flux_ref, gain_ref, going_ref, base_ref, out_ref
+):
+    n = ready_ref.shape[0]
+    mirror = row_ref[0] % 2 == 1
+
+    @pl.when(mirror)
+    def _():
+        going_ref[0:n] = s_ref[...] + dot(m_ref[...], got_ref[...])
+
+    @pl.when(jnp.logical_not(mirror))
+    def _():
+        going_ref[0:n] = ready_ref[...]
+
+    @pl.when(row_ref[0] == 1)
+    def _():
+        going_ref[n:] = moved_ref[...]
+        base = dot(early_ref[:, 0:n], going_ref[0:n])
+        base_ref[...] = base
+        out_ref[...] = base + dot(early_ref[:, n:], moved_ref[...])
+
+    @pl.when(row_ref[0] != 1)
+    def _():
+        going_ref[n:] = jnp.zeros_like(moved_ref)
+        base = dot(flux_ref[...], going_ref[0:n])
+        base_ref[...] = base
+        out_ref[...] = base
+
+
+def last_kernel(
+    row_ref, going_ref, homed_ref, second_ref, third_ref, lift_ref, flux_ref, gain_ref, state_ref, trace_ref, all_ref
+):
+    n = state_ref.shape[1]
+    row = row_ref[0]
+
+    @pl.when(row % 2 == 1)
+    def _():
+        all_ref[...] = homed_ref[...]
+
+    @pl.when(row % 2 == 0)
+    def _():
+        all_ref[...] = going_ref[...]
+
+    for section, moved_ref in ((2, second_ref), (3, third_ref)):
+
+        @pl.when(row == section)
+        def _(moved_ref=moved_ref):
+            all_ref[n:] = moved_ref[...]
+
+    state_ref[0] = all_ref[0:n] + dot(lift_ref[...], all_ref[n:], (0, 0))
+    trace_ref[0] = dot(flux_ref[...], all_ref[0:n]) + dot(gain_ref[...], all_ref[n:])
+
+
 VMEM = pl.BlockSpec(memory_space=pltpu.VMEM)
 SMEM = pl.BlockSpec(memory_space=pltpu.SMEM)
 HBM = pl.BlockSpec(memory_space=pltpu.HBM)
@@ -313,7 +378,7 @@
         return call(kernel, [SMEM] + [VMEM] * len(blocks), shapes, mirrored, *blocks)
 
     got = move(start, 1)
-    gain = dot(flux, lift)
+    gain = exact_dot(flux, lift)
     early = lax.ppermute(
         jnp.concatenate([flux, gain], axis=1),
         axes,
@@ -369,36 +434,48 @@
     mask = sectors - 1
     state = call(close_kernel, [VMEM] * 3, [(n, LANES)], matrix, ahead, got_ahead)
     shift = (mortar_shift[0] - (half - 1)) & mask
-    moved = hop(turn(dot(flux, state), shift, rows, sectors), shift, [0], sectors)
-    inlet = jnp.where(row_index == 1, moved, 0.0)
-
-    got_behind = lax.optimization_barrier((got_behind, inlet))[0]
-    closed = call(close_kernel, [VMEM] * 3, [(n, LANES)], matrix, behind, got_behind)
-    state = jnp.where(mirror, closed, state)
-    base = dot(jnp.where(row_index == 1, early[:, :n], flux), state)
-    local = jnp.where(row_index == 1, early[:, n:], gain)
-    for section in range(2, rows):
-        leaving = base + dot(local, inlet)
-        shift = mortar_shift[section - 1]
-        if section == 2:
-            shift = shift + (half - 1)
-        shift = shift & mask
-        if is_mirrored(section):
-            leaving = turn(leaving, shift, rows, sectors)
-        moved = hop(leaving, shift, range(1, rows - 1), sectors)
-        if section == 2:
-            going, moved = lax.optimization_barrier((jnp.concatenate([state, inlet], axis=0), moved))
-            route = sector_route(rows, sectors, lambda row: half - 1 if is_mirrored(row) else None)
-            homed = lax.ppermute(going, axes, route)
-            moved = jnp.where(shift >= 0, moved, 0.0)
-        if not is_mirrored(section):
-            moved = turn(moved, shift, rows, sectors)
-        inlet = jnp.where(row_index == section, moved, inlet)
-    state = jnp.where(mirror, homed[:n], state)
-    inlet = jnp.where(row_index == 1, homed[n:], inlet)
-    current = state + dot(lift, inlet)
-    trace = dot(flux, state) + dot(gain, inlet)
-    return (current[None, None, None], trace[None, None, None])
+    moved = hop(turn(exact_dot(flux, state), shift, rows, sectors), shift, [0], sectors)
+
+    row = jnp.reshape(row_index, (1,)).astype(jnp.int32)
+    face = (flux.shape[0], LANES)
+    going, base, leaving = call(
+        second_kernel,
+        [SMEM] + [VMEM] * 8,
+        [(n + face[0], LANES), face, face],
+        row,
+        matrix,
+        behind,
+        got_behind,
+        state,
+        moved,
+        early,
+        flux,
+        gain,
+    )
+    shift = (mortar_shift[1] + (half - 1)) & mask
+    moved = hop(leaving, shift, range(1, rows - 1), sectors)
+    going, moved = lax.optimization_barrier((going, moved))
+    route = sector_route(rows, sectors, lambda row: half - 1 if is_mirrored(row) else None)
+    homed = lax.ppermute(going, axes, route)
+    moved = jnp.where(shift >= 0, moved, 0.0)
+    second = turn(moved, shift, rows, sectors)
+    shift = mortar_shift[2] & mask
+    leaving = turn(base + exact_dot(gain, second), shift, rows, sectors)
+    third = hop(leaving, shift, range(1, rows - 1), sectors)
+    return call(
+        last_kernel,
+        [SMEM] + [VMEM] * 7,
+        [(1, n, LANES), (1,) + face],
+        row,
+        going,
+        homed,
+        second,
+        third,
+        lift.T,
+        flux,
+        gain,
+        scratch=[pltpu.VMEM((n + face[0], LANES), jnp.float32)],
+    )
 
 
 def solution(mesh):
@@ -412,6 +489,9 @@
     )
     out_specs = (P("row", "sector", "band", None, None), P("row", "sector", "band", None, None))
 
+    def layer(*operands):
+        return tuple(block[None, None] for block in on_device(*operands))
+
     return jax.shard_map(
-        on_device, mesh=mesh, in_specs=in_specs, out_specs=out_specs, check_vma=False
-    )
+        layer, mesh=mesh, in_specs=in_specs, out_specs=out_specs, check_vma=False
+    )

time: 184 us -> 185 us (level)
  waiting for transfers between devices: 104 us -> 111 us
  matrix products: 3.49 us -> 0.72 us
    ppermute x6, waiting for transfers between devices: 35.7 us -> 42.2 us  [send(): return lax.ppermute(trace, ('row', 'sector'), route)]
    dot_general x8 -> x3, matrix products: 3.49 us -> 0.72 us  [exact_dot(): return jnp.dot(a, b, precision=HIGH, preferred_element_type=jnp.float32)]
    pallas_call x14 -> x15, Pallas kernels: 11.6 us -> 10.2 us  [call(): pl.pallas_call(kernel, out_shape=shapes, in_specs=specs, out_specs=[VMEM]...]
  transfers between devices with their start and end apart: 20 -> 20, of which waited for: 12 -> 12; matrix products, arithmetic and copies ran while one was open for 1% -> 1% of each run, Pallas kernels for 4% -> 2%
where the time goes in v6:
time: 185 us; the launch traced here: 183 us
  waiting for transfers between devices  111 us (60%)
  starting transfers between devices  57.1 us (31%)
  Pallas kernels  10.2 us (6%)
  between operations  2.86 us (2%)
    ppermute x9, waiting for transfers between devices, move(): return lax.ppermute(block, axes, route)  65.1 us
    ppermute x6, waiting for transfers between devices, send(): return lax.ppermute(trace, ('row', 'sector'), route)  42.2 us
    ppermute x9, starting transfers between devices, move(): return lax.ppermute(block, axes, route)  27.2 us
    ppermute x6, starting transfers between devices, send(): return lax.ppermute(trace, ('row', 'sector'), route)  19 us
    pallas_call x15, Pallas kernels, call(): pl.pallas_call(kernel, out_shape=shapes, in_specs=specs, out_specs=[VMEM]...  10.2 us
    ppermute x1, starting transfers between devices, on_device(): got_ahead = lax.ppermute(ahead, axes, route)  6.26 us
  transfers between devices with their start and end apart: 20, of which 12 were waited for; matrix products, arithmetic and copies ran while one was open for 1% of the time, Pallas kernels for 2%

profile of v6, /device:TPU:24, one launch (start us, length us, event | category | flops | bytes accessed | tf_op | source)
XLA Modules:
  0.0 183.4 jit_solution(16234321858899408226)
XLA Ops:
  0.6 1.7 shard_map.77.both_ref
  2.4 3.4 %collective-permute-start.57 = (f32[1152,128]{1,0:T(8,128)S(1)}, f32[1152,128]{1,0:T(8,128)S(1)}, u32[]{:S(2)}, u32[]{:S(2)}) collective-permute-start(f32[1152,128]{1,0:T(8,128)S(1)} %shard_map.77.both_ref), channel_id=1, source_target_pairs={{0,2},{2,4},{4,6},{6,8},{8,10},{10,12},{12,14},{14,16},{16,18},{18... | collective-permute-start | bytes 1769480 | tf_op jit(solution)/shard_map/ppermute | solution.py:356
  5.8 18.0 %collective-permute-done.57.got_ref = f32[1152,128]{1,0:T(8,128)S(1)} collective-permute-done((f32[1152,128]{1,0:T(8,128)S(1)}, f32[1152,128]{1,0:T(8,128)S(1)}, u32[]{:S(2)}, u32[]{:S(2)}) %collective-permute-start.57) | collective-permute-done | bytes 589856 | tf_op jit(solution)/shard_map/ppermute | solution.py:356
  24.2 1.9 %collective-permute-start.59 = (f32[672,128]{1,0:T(8,128)S(1)}, f32[672,128]{1,0:T(8,128)S(1)}, u32[]{:S(2)}, u32[]{:S(2)}) collective-permute-start(f32[672,128]{1,0:T(8,128)S(1)} %shard_map.79.b_ref), channel_id=1, source_target_pairs={{0,4},{2,6},{4,8},{6,10},{8,12},{10,14},{12,16},{14,18},{16,20},{1... | collective-permute-start | bytes 1032200 | tf_op jit(solution)/shard_map/ppermute | solution.py:356
  26.2 0.6 shard_map.78.a_ref
  26.7 1.9 %collective-permute-start.58 = (f32[480,128]{1,0:T(8,128)S(1)}, f32[480,128]{1,0:T(8,128)S(1)}, u32[]{:S(2)}, u32[]{:S(2)}) collective-permute-start(f32[480,128]{1,0:T(8,128)S(1)} %shard_map.78.a_ref), channel_id=1, source_target_pairs={{0,4},{2,6},{4,8},{6,10},{8,12},{10,14},{12,16},{14,18},{16,20},{1... | collective-permute-start | bytes 737288 | tf_op jit(solution)/shard_map/ppermute | solution.py:356
  28.7 11.1 %collective-permute-done.58.got_ref = f32[480,128]{1,0:T(8,128)S(1)} collective-permute-done((f32[480,128]{1,0:T(8,128)S(1)}, f32[480,128]{1,0:T(8,128)S(1)}, u32[]{:S(2)}, u32[]{:S(2)}) %collective-permute-start.58) | collective-permute-done | bytes 245792 | tf_op jit(solution)/shard_map/ppermute | solution.py:356
  39.7 0.6 shard_map.80.a_ref
  40.7 1.9 %collective-permute-start.61 = (f32[672,128]{1,0:T(8,128)S(1)}, f32[672,128]{1,0:T(8,128)S(1)}, u32[]{:S(2)}, u32[]{:S(2)}) collective-permute-start(f32[672,128]{1,0:T(8,128)S(1)} %shard_map.81.b_ref), channel_id=1, source_target_pairs={{0,8},{2,10},{4,12},{6,14},{8,16},{10,18},{12,20},{14,22},{16,24},... | collective-permute-start | bytes 1032200 | tf_op jit(solution)/shard_map/ppermute | solution.py:356
  42.7 1.9 %collective-permute-start.60 = (f32[480,128]{1,0:T(8,128)S(1)}, f32[480,128]{1,0:T(8,128)S(1)}, u32[]{:S(2)}, u32[]{:S(2)}) collective-permute-start(f32[480,128]{1,0:T(8,128)S(1)} %shard_map.80.a_ref), channel_id=1, source_target_pairs={{0,8},{2,10},{4,12},{6,14},{8,16},{10,18},{12,20},{14,22},{16,24},... | collective-permute-start | bytes 737288 | tf_op jit(solution)/shard_map/ppermute | solution.py:356
  44.6 9.1 %collective-permute-done.60.got_ref = f32[480,128]{1,0:T(8,128)S(1)} collective-permute-done((f32[480,128]{1,0:T(8,128)S(1)}, f32[480,128]{1,0:T(8,128)S(1)}, u32[]{:S(2)}, u32[]{:S(2)}) %collective-permute-start.60) | collective-permute-done | bytes 245792 | tf_op jit(solution)/shard_map/ppermute | solution.py:356
  53.7 0.6 shard_map.82.a_ref
  54.7 1.9 %collective-permute-start.62 = (f32[672,128]{1,0:T(8,128)S(1)}, f32[672,128]{1,0:T(8,128)S(1)}, u32[]{:S(2)}, u32[]{:S(2)}) collective-permute-start(f32[672,128]{1,0:T(8,128)S(1)} %shard_map.83.b_ref), channel_id=1, source_target_pairs={{0,16},{2,18},{4,20},{6,22},{8,24},{10,26},{12,28},{14,30},{16,32}... | collective-permute-start | bytes 1032200 | tf_op jit(solution)/shard_map/ppermute | solution.py:356
  56.6 3.3 %collective-permute-start.63 = (f32[480,128]{1,0:T(8,128)S(1)}, f32[480,128]{1,0:T(8,128)S(1)}, u32[]{:S(2)}, u32[]{:S(2)}) collective-permute-start(f32[480,128]{1,0:T(8,128)S(1)} %shard_map.82.a_ref), channel_id=1, source_target_pairs={{0,16},{2,18},{4,20},{6,22},{8,24},{10,26},{12,28},{14,30},{16,32}... | collective-permute-start | bytes 737288 | tf_op jit(solution)/shard_map/ppermute | solution.py:356
  60.0 15.0 %collective-permute-done.63.got_ref = f32[480,128]{1,0:T(8,128)S(1)} collective-permute-done((f32[480,128]{1,0:T(8,128)S(1)}, f32[480,128]{1,0:T(8,128)S(1)}, u32[]{:S(2)}, u32[]{:S(2)}) %collective-permute-start.63) | collective-permute-done | bytes 245792 | tf_op jit(solution)/shard_map/ppermute | solution.py:356
  74.9 0.6 shard_map.84.new_a_ref
  76.0 1.9 %collective-permute-start.64 = (f32[400,128]{1,0:T(8,128)S(1)}, f32[400,128]{1,0:T(8,128)S(1)}, u32[]{:S(2)}, u32[]{:S(2)}) collective-permute-start(f32[400,128]{1,0:T(8,128)S(1)} %get-tuple-element.148), channel_id=1, source_target_pairs={{0,32},{2,34},{4,36},{6,38},{8,40},{10,42},{12,44},{14,46},{16,48}... | collective-permute-start | bytes 614408 | tf_op jit(solution)/shard_map/ppermute | solution.py:356
  77.9 9.0 %collective-permute-start.66 = (f32[320,128]{1,0:T(8,128)S(1)}, f32[320,128]{1,0:T(8,128)S(1)}, u32[]{:S(2)}, u32[]{:S(2)}) collective-permute-start(f32[320,128]{1,0:T(8,128)S(1)} %get-tuple-element.147.s_ref), channel_id=1, source_target_pairs={{0,32},{2,34},{4,36},{6,38},{8,40},{10,42},{12,44},{14,46},{16,48}... | collective-permute-start | bytes 491528 | tf_op jit(solution)/shard_map/ppermute | solution.py:356
  87.2 11.9 %collective-permute-done.66.got_ref = f32[320,128]{1,0:T(8,128)S(1)} collective-permute-done((f32[320,128]{1,0:T(8,128)S(1)}, f32[320,128]{1,0:T(8,128)S(1)}, u32[]{:S(2)}, u32[]{:S(2)}) %collective-permute-start.66) | collective-permute-done | bytes 163872 | tf_op jit(solution)/shard_map/ppermute | solution.py:356
  99.4 6.3 %collective-permute-start.68 = (f32[320,128]{1,0:T(8,128)S(1)}, f32[320,128]{1,0:T(8,128)S(1)}, u32[]{:S(2)}, u32[]{:S(2)}) collective-permute-start(f32[320,128]{1,0:T(8,128)S(1)} %shard_map.88.s_ref), channel_id=1, source_target_pairs={{0,64},{2,66},{4,68},{6,70},{8,72},{10,74},{12,76},{14,78},{16,80}... | collective-permute-start | bytes 491528 | tf_op jit(solution)/shard_map/ppermute | solution.py:418
  105.7 2.7 %collective-permute-start.65 = (f32[400,128]{1,0:T(8,128)S(1)}, f32[400,128]{1,0:T(8,128)S(1)}, u32[]{:S(2)}, u32[]{:S(2)}) collective-permute-start(f32[400,128]{1,0:T(8,128)S(1)} %collective-permute-done.64.mine_ref), channel_id=1, source_target_pairs={{0,1},{1,0},{2,3},{3,2},{4,5},{5,4},{6,7},{7,6},{8,9},{9,8},{10,11... | collective-permute-start | bytes 614408 | tf_op jit(solution)/shard_map/ppermute | solution.py:419
  108.5 0.7 collective-permute-start.69
  109.2 0.7 fusion.4
  111.7 1.7 collective-permute-done.65.other_ref
  113.8 0.6 shard_map.87.m_ref
  114.4 0.7 collective-permute-start.67
  115.1 1.8 collective-permute-done.68.got_ref
  117.5 11.8 %conditional.6 = (f32[80,128]{1,0:T(8,128)S(1)}) conditional(s32[]{:T(128)} %bitcast.7, f32[80,128]{1,0:T(8,128)S(1)} %convolution_bitcast_fusion, f32[80,128]{1,0:T(8,128)S(1)} %convolution_bitcast_fusion, f32[80,128]{1,0:T(8,128)S(1)} %convolution_bitcast_fusion, ...), branch_computations={%region_0.1_spmd, %region_1.2_spmd, %region_2.3_spmd, %region_3.4_... | conditional | bytes 245808 | solution.py:337
  117.5 10.1 %collective-permute-start.11 = (f32[80,128]{1,0:T(8,128)S(1)}, f32[80,128]{1,0:T(8,128)S(1)}, u32[]{:S(2)}, u32[]{:S(2)}) collective-permute-start(f32[80,128]{1,0:T(8,128)S(1)} %param.12), channel_id=1, source_target_pairs={{0,96},{2,98},{4,100},{6,102},{8,104},{10,106},{12,108},{14,110},{... | collective-permute-start | bytes 122888 | tf_op jit(solution)/shard_map/cond/branch_12_fun/ppermute | solution.py:334
  127.6 1.7 collective-permute-done.11
  129.3 1.3 conditional.7
  129.3 1.3 collective-permute-start.15
  130.6 1.0 shard_map.90
  131.6 24.8 %conditional.8 = (f32[80,128]{1,0:T(8,128)}) conditional(s32[]{:T(128)} %bitcast.11, f32[80,128]{1,0:T(8,128)S(1)} %get-tuple-element.152, f32[80,128]{1,0:T(8,128)S(1)} %get-tuple-element.152, f32[80,128]{1,0:T(8,128)S(1)} %get-tuple-element.152, f32[80,128]{1,0:T(8,128)S(1)} %get-tuple-element.152), branch_computations={%region_20.21_spmd, %region_21.22_spmd, %region_22.23_spmd, %regio... | conditional | bytes 163888 | solution.py:326
  131.6 1.9 %collective-permute-start.20 = (f32[80,128]{1,0:T(8,128)S(1)}, f32[80,128]{1,0:T(8,128)}, u32[]{:S(2)}, u32[]{:S(2)}) collective-permute-start(f32[80,128]{1,0:T(8,128)S(1)} %param.21), channel_id=1, source_target_pairs={{128,258},{130,260},{132,262},{134,264},{136,266},{138,268},{140,2... | collective-permute-start | bytes 122888 | tf_op jit(solution)/shard_map/cond/branch_1_fun/ppermute | solution.py:324
  133.5 22.8 %collective-permute-done.20 = f32[80,128]{1,0:T(8,128)} collective-permute-done((f32[80,128]{1,0:T(8,128)S(1)}, f32[80,128]{1,0:T(8,128)}, u32[]{:S(2)}, u32[]{:S(2)}) %collective-permute-start.20) | collective-permute-done | bytes 40992 | tf_op jit(solution)/shard_map/cond/branch_1_fun/ppermute | solution.py:324
  156.4 0.7 collective-permute-start.70
  157.1 0.8 broadcast_select_fusion
  157.8 7.7 %conditional.9 = (f32[80,128]{1,0:T(8,128)S(1)}) conditional(s32[]{:T(128)} %bitcast.12, f32[80,128]{1,0:T(8,128)S(1)} %broadcast_select_fusion, f32[80,128]{1,0:T(8,128)S(1)} %broadcast_select_fusion, f32[80,128]{1,0:T(8,128)S(1)} %broadcast_select_fusion, f32[80,128]{1,0:T(8,128)S(1)} %broadcast_select_fusion, ...), branch_computations={%region_24.25_spmd, %region_25.26_spmd, %region_26.27_spmd, %regio... | conditional | bytes 245808 | solution.py:337
  157.8 1.9 %collective-permute-start.35 = (f32[80,128]{1,0:T(8,128)S(1)}, f32[80,128]{1,0:T(8,128)S(1)}, u32[]{:S(2)}, u32[]{:S(2)}) collective-permute-start(f32[80,128]{1,0:T(8,128)S(1)} %param.37), channel_id=1, source_target_pairs={{0,104},{2,106},{4,108},{6,110},{8,112},{10,114},{12,116},{14,118}... | collective-permute-start | bytes 122888 | tf_op jit(solution)/shard_map/cond/branch_13_fun/ppermute | solution.py:334
  159.8 5.8 %collective-permute-done.35 = f32[80,128]{1,0:T(8,128)S(1)} collective-permute-done((f32[80,128]{1,0:T(8,128)S(1)}, f32[80,128]{1,0:T(8,128)S(1)}, u32[]{:S(2)}, u32[]{:S(2)}) %collective-permute-start.35) | collective-permute-done | bytes 40992 | tf_op jit(solution)/shard_map/cond/branch_13_fun/ppermute | solution.py:334
  165.7 9.0 %conditional.10 = (f32[80,128]{1,0:T(8,128)S(1)}) conditional(s32[]{:T(128)} %bitcast.15, f32[80,128]{1,0:T(8,128)S(1)} %add.63, f32[80,128]{1,0:T(8,128)S(1)} %add.63, f32[80,128]{1,0:T(8,128)S(1)} %add.63, f32[80,128]{1,0:T(8,128)S(1)} %add.63, f32[80,128]{1,0:T(8,128)S(1)} %add.63, ...), branch_computations={%region_40.41_spmd, %region_41.42_spmd, %region_42.43_spmd, %regio... | conditional | bytes 245808 | solution.py:337
  165.8 1.9 %collective-permute-start.40 = (f32[80,128]{1,0:T(8,128)S(1)}, f32[80,128]{1,0:T(8,128)S(1)}, u32[]{:S(2)}, u32[]{:S(2)}) collective-permute-start(f32[80,128]{1,0:T(8,128)S(1)} %param.43), channel_id=1, source_target_pairs={{0,24},{2,26},{4,28},{6,30},{8,32},{10,34},{12,36},{14,38},{16,40}... | collective-permute-start | bytes 122888 | tf_op jit(solution)/shard_map/cond/branch_3_fun/ppermute | solution.py:334
  167.7 7.0 %collective-permute-done.40 = f32[80,128]{1,0:T(8,128)S(1)} collective-permute-done((f32[80,128]{1,0:T(8,128)S(1)}, f32[80,128]{1,0:T(8,128)S(1)}, u32[]{:S(2)}, u32[]{:S(2)}) %collective-permute-start.40) | collective-permute-done | bytes 40992 | tf_op jit(solution)/shard_map/cond/branch_3_fun/ppermute | solution.py:334
  174.7 6.9 %conditional.11 = (f32[80,128]{1,0:T(8,128)}) conditional(s32[]{:T(128)} %bitcast.14, f32[80,128]{1,0:T(8,128)S(1)} %get-tuple-element.165, f32[80,128]{1,0:T(8,128)S(1)} %get-tuple-element.165, f32[80,128]{1,0:T(8,128)S(1)} %get-tuple-element.165, f32[80,128]{1,0:T(8,128)S(1)} %get-tuple-element.165), branch_computations={%region_56.57_spmd, %region_57.58_spmd, %region_58.59_spmd, %regio... | conditional | bytes 163888 | solution.py:326
  174.7 1.9 %collective-permute-start.53 = (f32[80,128]{1,0:T(8,128)S(1)}, f32[80,128]{1,0:T(8,128)}, u32[]{:S(2)}, u32[]{:S(2)}) collective-permute-start(f32[80,128]{1,0:T(8,128)S(1)} %param.56), channel_id=1, source_target_pairs={{128,256},{130,258},{132,260},{134,262},{136,264},{138,266},{140,2... | collective-permute-start | bytes 122888 | tf_op jit(solution)/shard_map/cond/branch_0_fun/ppermute | solution.py:324
  176.6 5.0 %collective-permute-done.53 = f32[80,128]{1,0:T(8,128)} collective-permute-done((f32[80,128]{1,0:T(8,128)S(1)}, f32[80,128]{1,0:T(8,128)}, u32[]{:S(2)}, u32[]{:S(2)}) %collective-permute-start.53) | collective-permute-done | bytes 40992 | tf_op jit(solution)/shard_map/cond/branch_0_fun/ppermute | solution.py:324
  181.6 1.8 shard_map.91
  (29 shorter events, 3.7 us)
Async XLA Ops:
  2.4 21.5 %collective-permute-start.57 = (f32[1152,128]{1,0:T(8,128)S(1)}, f32[1152,128]{1,0:T(8,128)S(1)}, u32[]{:S(2)}, u32[]{:S(2)}) collective-permute-start(f32[1152,128]{1,0:T(8,128)S(1)} %shard_map.77.both_ref), channel_id=1, source_target_pairs={{0,2},{2,4},{4,6},{6,8},{8,10},{10,12},{12,14},{14,16},{16,18},{18... | collective-permute-start | bytes 1769480 | tf_op jit(solution)/shard_map/ppermute | solution.py:356
  24.2 16.1 %collective-permute-start.59 = (f32[672,128]{1,0:T(8,128)S(1)}, f32[672,128]{1,0:T(8,128)S(1)}, u32[]{:S(2)}, u32[]{:S(2)}) collective-permute-start(f32[672,128]{1,0:T(8,128)S(1)} %shard_map.79.b_ref), channel_id=1, source_target_pairs={{0,4},{2,6},{4,8},{6,10},{8,12},{10,14},{12,16},{14,18},{16,20},{1... | collective-permute-start | bytes 1032200 | tf_op jit(solution)/shard_map/ppermute | solution.py:356
  26.7 13.0 %collective-permute-start.58 = (f32[480,128]{1,0:T(8,128)S(1)}, f32[480,128]{1,0:T(8,128)S(1)}, u32[]{:S(2)}, u32[]{:S(2)}) collective-permute-start(f32[480,128]{1,0:T(8,128)S(1)} %shard_map.78.a_ref), channel_id=1, source_target_pairs={{0,4},{2,6},{4,8},{6,10},{8,12},{10,14},{12,16},{14,18},{16,20},{1... | collective-permute-start | bytes 737288 | tf_op jit(solution)/shard_map/ppermute | solution.py:356
  40.7 13.6 %collective-permute-start.61 = (f32[672,128]{1,0:T(8,128)S(1)}, f32[672,128]{1,0:T(8,128)S(1)}, u32[]{:S(2)}, u32[]{:S(2)}) collective-permute-start(f32[672,128]{1,0:T(8,128)S(1)} %shard_map.81.b_ref), channel_id=1, source_target_pairs={{0,8},{2,10},{4,12},{6,14},{8,16},{10,18},{12,20},{14,22},{16,24},... | collective-permute-start | bytes 1032200 | tf_op jit(solution)/shard_map/ppermute | solution.py:356
  42.7 11.1 %collective-permute-start.60 = (f32[480,128]{1,0:T(8,128)S(1)}, f32[480,128]{1,0:T(8,128)S(1)}, u32[]{:S(2)}, u32[]{:S(2)}) collective-permute-start(f32[480,128]{1,0:T(8,128)S(1)} %shard_map.80.a_ref), channel_id=1, source_target_pairs={{0,8},{2,10},{4,12},{6,14},{8,16},{10,18},{12,20},{14,22},{16,24},... | collective-permute-start | bytes 737288 | tf_op jit(solution)/shard_map/ppermute | solution.py:356
  54.7 20.8 %collective-permute-start.62 = (f32[672,128]{1,0:T(8,128)S(1)}, f32[672,128]{1,0:T(8,128)S(1)}, u32[]{:S(2)}, u32[]{:S(2)}) collective-permute-start(f32[672,128]{1,0:T(8,128)S(1)} %shard_map.83.b_ref), channel_id=1, source_target_pairs={{0,16},{2,18},{4,20},{6,22},{8,24},{10,26},{12,28},{14,30},{16,32}... | collective-permute-start | bytes 1032200 | tf_op jit(solution)/shard_map/ppermute | solution.py:356
  56.6 18.3 %collective-permute-start.63 = (f32[480,128]{1,0:T(8,128)S(1)}, f32[480,128]{1,0:T(8,128)S(1)}, u32[]{:S(2)}, u32[]{:S(2)}) collective-permute-start(f32[480,128]{1,0:T(8,128)S(1)} %shard_map.82.a_ref), channel_id=1, source_target_pairs={{0,16},{2,18},{4,20},{6,22},{8,24},{10,26},{12,28},{14,30},{16,32}... | collective-permute-start | bytes 737288 | tf_op jit(solution)/shard_map/ppermute | solution.py:356
  75.5 11.4 %copy-start = (f32[1,1,1,80,320]{4,3,2,1,0:T(8,128)S(1)}, f32[1,1,1,80,320]{4,3,2,1,0:T(8,128)}, u32[]{:S(2)}) copy-start(f32[1,1,1,80,320]{4,3,2,1,0:T(8,128)} %param.69) | copy-start | bytes 307204
  75.5 11.4 %copy-start.1 = (f32[1,1,1,320,80]{3,4,2,1,0:T(8,128)S(1)}, f32[1,1,1,320,80]{3,4,2,1,0:T(8,128)}, u32[]{:S(2)}) copy-start(f32[1,1,1,320,80]{3,4,2,1,0:T(8,128)} %param.70) | copy-start | bytes 307204
  76.0 29.7 %collective-permute-start.64 = (f32[400,128]{1,0:T(8,128)S(1)}, f32[400,128]{1,0:T(8,128)S(1)}, u32[]{:S(2)}, u32[]{:S(2)}) collective-permute-start(f32[400,128]{1,0:T(8,128)S(1)} %get-tuple-element.148), channel_id=1, source_target_pairs={{0,32},{2,34},{4,36},{6,38},{8,40},{10,42},{12,44},{14,46},{16,48}... | collective-permute-start | bytes 614408 | tf_op jit(solution)/shard_map/ppermute | solution.py:356
  77.9 21.2 %collective-permute-start.66 = (f32[320,128]{1,0:T(8,128)S(1)}, f32[320,128]{1,0:T(8,128)S(1)}, u32[]{:S(2)}, u32[]{:S(2)}) collective-permute-start(f32[320,128]{1,0:T(8,128)S(1)} %get-tuple-element.147.s_ref), channel_id=1, source_target_pairs={{0,32},{2,34},{4,36},{6,38},{8,40},{10,42},{12,44},{14,46},{16,48}... | collective-permute-start | bytes 491528 | tf_op jit(solution)/shard_map/ppermute | solution.py:356
  99.4 17.4 %collective-permute-start.68 = (f32[320,128]{1,0:T(8,128)S(1)}, f32[320,128]{1,0:T(8,128)S(1)}, u32[]{:S(2)}, u32[]{:S(2)}) collective-permute-start(f32[320,128]{1,0:T(8,128)S(1)} %shard_map.88.s_ref), channel_id=1, source_target_pairs={{0,64},{2,66},{4,68},{6,70},{8,72},{10,74},{12,76},{14,78},{16,80}... | collective-permute-start | bytes 491528 | tf_op jit(solution)/shard_map/ppermute | solution.py:418
  105.7 7.7 %collective-permute-start.65 = (f32[400,128]{1,0:T(8,128)S(1)}, f32[400,128]{1,0:T(8,128)S(1)}, u32[]{:S(2)}, u32[]{:S(2)}) collective-permute-start(f32[400,128]{1,0:T(8,128)S(1)} %collective-permute-done.64.mine_ref), channel_id=1, source_target_pairs={{0,1},{1,0},{2,3},{3,2},{4,5},{5,4},{6,7},{7,6},{8,9},{9,8},{10,11... | collective-permute-start | bytes 614408 | tf_op jit(solution)/shard_map/ppermute | solution.py:419
  108.4 0.8 copy-start.2
  108.5 22.1 %collective-permute-start.69 = (f32[80,400]{1,0:T(8,128)S(1)}, f32[80,400]{1,0:T(8,128)S(1)}, u32[]{:S(2)}, u32[]{:S(2)}) collective-permute-start(f32[80,400]{1,0:T(8,128)S(1)} %pad_maximum_fusion), channel_id=1, source_target_pairs={{128,194},{130,196},{132,198},{134,200},{136,202},{138,204},{140,2... | collective-permute-start | bytes 384008 | tf_op jit(solution)/shard_map/ppermute | solution.py:382
  114.4 16.1 %collective-permute-start.67 = (f32[320,128]{1,0:T(8,128)S(1)}, f32[320,128]{1,0:T(8,128)S(1)}, u32[]{:S(2)}, u32[]{:S(2)}) collective-permute-start(f32[320,128]{1,0:T(8,128)S(1)} %get-tuple-element.150.s_ref), channel_id=1, source_target_pairs={{128,192},{130,194},{132,196},{134,198},{136,200},{138,202},{140,2... | collective-permute-start | bytes 491528 | tf_op jit(solution)/shard_map/ppermute | solution.py:431
  117.5 11.8 %collective-permute-start.11 = (f32[80,128]{1,0:T(8,128)S(1)}, f32[80,128]{1,0:T(8,128)S(1)}, u32[]{:S(2)}, u32[]{:S(2)}) collective-permute-start(f32[80,128]{1,0:T(8,128)S(1)} %param.12), channel_id=1, source_target_pairs={{0,96},{2,98},{4,100},{6,102},{8,104},{10,106},{12,108},{14,110},{... | collective-permute-start | bytes 122888 | tf_op jit(solution)/shard_map/cond/branch_12_fun/ppermute | solution.py:334
  129.3 1.3 collective-permute-start.15
  131.6 24.8 %collective-permute-start.20 = (f32[80,128]{1,0:T(8,128)S(1)}, f32[80,128]{1,0:T(8,128)}, u32[]{:S(2)}, u32[]{:S(2)}) collective-permute-start(f32[80,128]{1,0:T(8,128)S(1)} %param.21), channel_id=1, source_target_pairs={{128,258},{130,260},{132,262},{134,264},{136,266},{138,268},{140,2... | collective-permute-start | bytes 122888 | tf_op jit(solution)/shard_map/cond/branch_1_fun/ppermute | solution.py:324
  156.4 25.2 %collective-permute-start.70 = (f32[400,128]{1,0:T(8,128)S(1)}, f32[400,128]{1,0:T(8,128)S(1)}, u32[]{:S(2)}, u32[]{:S(2)}) collective-permute-start(f32[400,128]{1,0:T(8,128)S(1)} %get-tuple-element.153.going_ref), channel_id=1, source_target_pairs={{128,190},{130,192},{132,194},{134,196},{136,198},{138,200},{140,2... | collective-permute-start | bytes 614408 | tf_op jit(solution)/shard_map/ppermute | solution.py:459
  157.8 7.7 %collective-permute-start.35 = (f32[80,128]{1,0:T(8,128)S(1)}, f32[80,128]{1,0:T(8,128)S(1)}, u32[]{:S(2)}, u32[]{:S(2)}) collective-permute-start(f32[80,128]{1,0:T(8,128)S(1)} %param.37), channel_id=1, source_target_pairs={{0,104},{2,106},{4,108},{6,110},{8,112},{10,114},{12,116},{14,118}... | collective-permute-start | bytes 122888 | tf_op jit(solution)/shard_map/cond/branch_13_fun/ppermute | solution.py:334
  165.8 8.9 %collective-permute-start.40 = (f32[80,128]{1,0:T(8,128)S(1)}, f32[80,128]{1,0:T(8,128)S(1)}, u32[]{:S(2)}, u32[]{:S(2)}) collective-permute-start(f32[80,128]{1,0:T(8,128)S(1)} %param.43), channel_id=1, source_target_pairs={{0,24},{2,26},{4,28},{6,30},{8,32},{10,34},{12,36},{14,38},{16,40}... | collective-permute-start | bytes 122888 | tf_op jit(solution)/shard_map/cond/branch_3_fun/ppermute | solution.py:334
  174.7 6.9 %collective-permute-start.53 = (f32[80,128]{1,0:T(8,128)S(1)}, f32[80,128]{1,0:T(8,128)}, u32[]{:S(2)}, u32[]{:S(2)}) collective-permute-start(f32[80,128]{1,0:T(8,128)S(1)} %param.56), channel_id=1, source_target_pairs={{128,256},{130,258},{132,260},{134,262},{136,264},{138,266},{140,2... | collective-permute-start | bytes 122888 | tf_op jit(solution)/shard_map/cond/branch_0_fun/ppermute | solution.py:324

commit v7 on v6

--- a/solution.py
+++ b/solution.py
@@ -434,7 +434,7 @@
     mask = sectors - 1
     state = call(close_kernel, [VMEM] * 3, [(n, LANES)], matrix, ahead, got_ahead)
     shift = (mortar_shift[0] - (half - 1)) & mask
-    moved = hop(turn(exact_dot(flux, state), shift, rows, sectors), shift, [0], sectors)
+    moved = hop(turn(exact_dot(flux, state), shift, rows, sectors), shift, range(0, rows - 1, 2), sectors)
 
     row = jnp.reshape(row_index, (1,)).astype(jnp.int32)
     face = (flux.shape[0], LANES)
@@ -453,15 +453,14 @@
         gain,
     )
     shift = (mortar_shift[1] + (half - 1)) & mask
-    moved = hop(leaving, shift, range(1, rows - 1), sectors)
+    moved = hop(leaving, shift, range(1, rows - 1, 2), sectors)
     going, moved = lax.optimization_barrier((going, moved))
     route = sector_route(rows, sectors, lambda row: half - 1 if is_mirrored(row) else None)
     homed = lax.ppermute(going, axes, route)
-    moved = jnp.where(shift >= 0, moved, 0.0)
     second = turn(moved, shift, rows, sectors)
     shift = mortar_shift[2] & mask
     leaving = turn(base + exact_dot(gain, second), shift, rows, sectors)
-    third = hop(leaving, shift, range(1, rows - 1), sectors)
+    third = hop(leaving, shift, range(0, rows - 1, 2), sectors)
     return call(
         last_kernel,
         [SMEM] + [VMEM] * 7,

time: 185 us -> 181 us (0.978)
  waiting for transfers between devices: 111 us -> 106 us
    ppermute x6, waiting for transfers between devices: 42.2 us -> 37.8 us  [send(): return lax.ppermute(trace, ('row', 'sector'), route)]
  transfers between devices with their start and end apart: 20 -> 20, of which waited for: 12 -> 13; matrix products, arithmetic and copies ran while one was open for 1% -> 2% of each run, Pallas kernels for 2% -> 2%
where the time goes in v7:
time: 181 us; the launch traced here: 180 us
  waiting for transfers between devices  106 us (59%)
  starting transfers between devices  57.1 us (32%)
  Pallas kernels  10.2 us (6%)
  between operations  2.86 us (2%)
    ppermute x9, waiting for transfers between devices, move(): return lax.ppermute(block, axes, route)  65.1 us
    ppermute x6, waiting for transfers between devices, send(): return lax.ppermute(trace, ('row', 'sector'), route)  37.8 us
    ppermute x9, starting transfers between devices, move(): return lax.ppermute(block, axes, route)  27.2 us
    ppermute x6, starting transfers between devices, send(): return lax.ppermute(trace, ('row', 'sector'), route)  19 us
    pallas_call x15, Pallas kernels, call(): pl.pallas_call(kernel, out_shape=shapes, in_specs=specs, out_specs=[VMEM]...  10.2 us
    ppermute x1, starting transfers between devices, on_device(): got_ahead = lax.ppermute(ahead, axes, route)  6.26 us
  transfers between devices with their start and end apart: 20, of which 13 were waited for; matrix products, arithmetic and copies ran while one was open for 2% of the time, Pallas kernels for 2%

profile of v7, /device:TPU:24, one launch (start us, length us, event | category | flops | bytes accessed | tf_op | source)
XLA Modules:
  0.0 179.6 jit_solution(9990530379430761764)
XLA Ops:
  0.6 1.7 shard_map.77.both_ref
  2.4 3.4 %collective-permute-start.57 = (f32[1152,128]{1,0:T(8,128)S(1)}, f32[1152,128]{1,0:T(8,128)S(1)}, u32[]{:S(2)}, u32[]{:S(2)}) collective-permute-start(f32[1152,128]{1,0:T(8,128)S(1)} %shard_map.77.both_ref), channel_id=1, source_target_pairs={{0,2},{2,4},{4,6},{6,8},{8,10},{10,12},{12,14},{14,16},{16,18},{18... | collective-permute-start | bytes 1769480 | tf_op jit(solution)/shard_map/ppermute | solution.py:356
  5.8 18.0 %collective-permute-done.57.got_ref = f32[1152,128]{1,0:T(8,128)S(1)} collective-permute-done((f32[1152,128]{1,0:T(8,128)S(1)}, f32[1152,128]{1,0:T(8,128)S(1)}, u32[]{:S(2)}, u32[]{:S(2)}) %collective-permute-start.57) | collective-permute-done | bytes 589856 | tf_op jit(solution)/shard_map/ppermute | solution.py:356
  24.2 1.9 %collective-permute-start.59 = (f32[672,128]{1,0:T(8,128)S(1)}, f32[672,128]{1,0:T(8,128)S(1)}, u32[]{:S(2)}, u32[]{:S(2)}) collective-permute-start(f32[672,128]{1,0:T(8,128)S(1)} %shard_map.79.b_ref), channel_id=1, source_target_pairs={{0,4},{2,6},{4,8},{6,10},{8,12},{10,14},{12,16},{14,18},{16,20},{1... | collective-permute-start | bytes 1032200 | tf_op jit(solution)/shard_map/ppermute | solution.py:356
  26.2 0.6 shard_map.78.a_ref
  26.7 1.9 %collective-permute-start.58 = (f32[480,128]{1,0:T(8,128)S(1)}, f32[480,128]{1,0:T(8,128)S(1)}, u32[]{:S(2)}, u32[]{:S(2)}) collective-permute-start(f32[480,128]{1,0:T(8,128)S(1)} %shard_map.78.a_ref), channel_id=1, source_target_pairs={{0,4},{2,6},{4,8},{6,10},{8,12},{10,14},{12,16},{14,18},{16,20},{1... | collective-permute-start | bytes 737288 | tf_op jit(solution)/shard_map/ppermute | solution.py:356
  28.7 11.1 %collective-permute-done.58.got_ref = f32[480,128]{1,0:T(8,128)S(1)} collective-permute-done((f32[480,128]{1,0:T(8,128)S(1)}, f32[480,128]{1,0:T(8,128)S(1)}, u32[]{:S(2)}, u32[]{:S(2)}) %collective-permute-start.58) | collective-permute-done | bytes 245792 | tf_op jit(solution)/shard_map/ppermute | solution.py:356
  39.7 0.6 shard_map.80.a_ref
  40.7 1.9 %collective-permute-start.61 = (f32[672,128]{1,0:T(8,128)S(1)}, f32[672,128]{1,0:T(8,128)S(1)}, u32[]{:S(2)}, u32[]{:S(2)}) collective-permute-start(f32[672,128]{1,0:T(8,128)S(1)} %shard_map.81.b_ref), channel_id=1, source_target_pairs={{0,8},{2,10},{4,12},{6,14},{8,16},{10,18},{12,20},{14,22},{16,24},... | collective-permute-start | bytes 1032200 | tf_op jit(solution)/shard_map/ppermute | solution.py:356
  42.7 1.9 %collective-permute-start.60 = (f32[480,128]{1,0:T(8,128)S(1)}, f32[480,128]{1,0:T(8,128)S(1)}, u32[]{:S(2)}, u32[]{:S(2)}) collective-permute-start(f32[480,128]{1,0:T(8,128)S(1)} %shard_map.80.a_ref), channel_id=1, source_target_pairs={{0,8},{2,10},{4,12},{6,14},{8,16},{10,18},{12,20},{14,22},{16,24},... | collective-permute-start | bytes 737288 | tf_op jit(solution)/shard_map/ppermute | solution.py:356
  44.6 9.1 %collective-permute-done.60.got_ref = f32[480,128]{1,0:T(8,128)S(1)} collective-permute-done((f32[480,128]{1,0:T(8,128)S(1)}, f32[480,128]{1,0:T(8,128)S(1)}, u32[]{:S(2)}, u32[]{:S(2)}) %collective-permute-start.60) | collective-permute-done | bytes 245792 | tf_op jit(solution)/shard_map/ppermute | solution.py:356
  53.7 0.6 shard_map.82.a_ref
  54.7 1.9 %collective-permute-start.62 = (f32[672,128]{1,0:T(8,128)S(1)}, f32[672,128]{1,0:T(8,128)S(1)}, u32[]{:S(2)}, u32[]{:S(2)}) collective-permute-start(f32[672,128]{1,0:T(8,128)S(1)} %shard_map.83.b_ref), channel_id=1, source_target_pairs={{0,16},{2,18},{4,20},{6,22},{8,24},{10,26},{12,28},{14,30},{16,32}... | collective-permute-start | bytes 1032200 | tf_op jit(solution)/shard_map/ppermute | solution.py:356
  56.6 3.3 %collective-permute-start.63 = (f32[480,128]{1,0:T(8,128)S(1)}, f32[480,128]{1,0:T(8,128)S(1)}, u32[]{:S(2)}, u32[]{:S(2)}) collective-permute-start(f32[480,128]{1,0:T(8,128)S(1)} %shard_map.82.a_ref), channel_id=1, source_target_pairs={{0,16},{2,18},{4,20},{6,22},{8,24},{10,26},{12,28},{14,30},{16,32}... | collective-permute-start | bytes 737288 | tf_op jit(solution)/shard_map/ppermute | solution.py:356
  60.0 15.0 %collective-permute-done.63.got_ref = f32[480,128]{1,0:T(8,128)S(1)} collective-permute-done((f32[480,128]{1,0:T(8,128)S(1)}, f32[480,128]{1,0:T(8,128)S(1)}, u32[]{:S(2)}, u32[]{:S(2)}) %collective-permute-start.63) | collective-permute-done | bytes 245792 | tf_op jit(solution)/shard_map/ppermute | solution.py:356
  74.9 0.6 shard_map.84.new_a_ref
  76.0 1.9 %collective-permute-start.64 = (f32[400,128]{1,0:T(8,128)S(1)}, f32[400,128]{1,0:T(8,128)S(1)}, u32[]{:S(2)}, u32[]{:S(2)}) collective-permute-start(f32[400,128]{1,0:T(8,128)S(1)} %get-tuple-element.148), channel_id=1, source_target_pairs={{0,32},{2,34},{4,36},{6,38},{8,40},{10,42},{12,44},{14,46},{16,48}... | collective-permute-start | bytes 614408 | tf_op jit(solution)/shard_map/ppermute | solution.py:356
  77.9 9.0 %collective-permute-start.66 = (f32[320,128]{1,0:T(8,128)S(1)}, f32[320,128]{1,0:T(8,128)S(1)}, u32[]{:S(2)}, u32[]{:S(2)}) collective-permute-start(f32[320,128]{1,0:T(8,128)S(1)} %get-tuple-element.147.s_ref), channel_id=1, source_target_pairs={{0,32},{2,34},{4,36},{6,38},{8,40},{10,42},{12,44},{14,46},{16,48}... | collective-permute-start | bytes 491528 | tf_op jit(solution)/shard_map/ppermute | solution.py:356
  87.2 11.9 %collective-permute-done.66.got_ref = f32[320,128]{1,0:T(8,128)S(1)} collective-permute-done((f32[320,128]{1,0:T(8,128)S(1)}, f32[320,128]{1,0:T(8,128)S(1)}, u32[]{:S(2)}, u32[]{:S(2)}) %collective-permute-start.66) | collective-permute-done | bytes 163872 | tf_op jit(solution)/shard_map/ppermute | solution.py:356
  99.4 6.3 %collective-permute-start.68 = (f32[320,128]{1,0:T(8,128)S(1)}, f32[320,128]{1,0:T(8,128)S(1)}, u32[]{:S(2)}, u32[]{:S(2)}) collective-permute-start(f32[320,128]{1,0:T(8,128)S(1)} %shard_map.88.s_ref), channel_id=1, source_target_pairs={{0,64},{2,66},{4,68},{6,70},{8,72},{10,74},{12,76},{14,78},{16,80}... | collective-permute-start | bytes 491528 | tf_op jit(solution)/shard_map/ppermute | solution.py:418
  105.7 2.7 %collective-permute-start.65 = (f32[400,128]{1,0:T(8,128)S(1)}, f32[400,128]{1,0:T(8,128)S(1)}, u32[]{:S(2)}, u32[]{:S(2)}) collective-permute-start(f32[400,128]{1,0:T(8,128)S(1)} %collective-permute-done.64.mine_ref), channel_id=1, source_target_pairs={{0,1},{1,0},{2,3},{3,2},{4,5},{5,4},{6,7},{7,6},{8,9},{9,8},{10,11... | collective-permute-start | bytes 614408 | tf_op jit(solution)/shard_map/ppermute | solution.py:419
  108.5 0.7 collective-permute-start.69
  109.2 0.7 fusion.4
  111.7 1.7 collective-permute-done.65.other_ref
  113.8 0.6 shard_map.87.m_ref
  114.4 0.7 collective-permute-start.67
  115.1 1.8 collective-permute-done.68.got_ref
  117.5 11.8 %conditional.6 = (f32[80,128]{1,0:T(8,128)S(1)}) conditional(s32[]{:T(128)} %bitcast.7, f32[80,128]{1,0:T(8,128)S(1)} %convolution_bitcast_fusion, f32[80,128]{1,0:T(8,128)S(1)} %convolution_bitcast_fusion, f32[80,128]{1,0:T(8,128)S(1)} %convolution_bitcast_fusion, ...), branch_computations={%region_0.1_spmd, %region_1.2_spmd, %region_2.3_spmd, %region_3.4_... | conditional | bytes 245808 | solution.py:337
  117.5 10.1 %collective-permute-start.11 = (f32[80,128]{1,0:T(8,128)S(1)}, f32[80,128]{1,0:T(8,128)S(1)}, u32[]{:S(2)}, u32[]{:S(2)}) collective-permute-start(f32[80,128]{1,0:T(8,128)S(1)} %param.12), channel_id=1, source_target_pairs={{0,96},{2,98},{4,100},{6,102},{8,104},{10,106},{12,108},{14,110},{... | collective-permute-start | bytes 122888 | tf_op jit(solution)/shard_map/cond/branch_12_fun/ppermute | solution.py:334
  127.6 1.7 collective-permute-done.11
  129.3 2.3 %conditional.7 = (f32[80,128]{1,0:T(8,128)}) conditional(s32[]{:T(128)} %bitcast.6, f32[80,128]{1,0:T(8,128)S(1)} %get-tuple-element.161, f32[80,128]{1,0:T(8,128)S(1)} %get-tuple-element.161, f32[80,128]{1,0:T(8,128)S(1)} %get-tuple-element.161, f32[80,128]{1,0:T(8,128)S(1)} %get-tuple-element.161), branch_computations={%region_16.17_spmd, %region_17.18_spmd, %region_18.19_spmd, %regio... | conditional | bytes 163888 | solution.py:326
  129.3 1.9 %collective-permute-start.15 = (f32[80,128]{1,0:T(8,128)S(1)}, f32[80,128]{1,0:T(8,128)}, u32[]{:S(2)}, u32[]{:S(2)}) collective-permute-start(f32[80,128]{1,0:T(8,128)S(1)} %param.16), channel_id=1, source_target_pairs={{0,128},{2,130},{4,132},{6,134},{8,136},{10,138},{12,140},{14,142}... | collective-permute-start | bytes 122888 | tf_op jit(solution)/shard_map/cond/branch_0_fun/ppermute | solution.py:324
  131.6 1.0 shard_map.90
  132.6 23.8 %conditional.8 = (f32[80,128]{1,0:T(8,128)}) conditional(s32[]{:T(128)} %bitcast.11, f32[80,128]{1,0:T(8,128)S(1)} %get-tuple-element.152, f32[80,128]{1,0:T(8,128)S(1)} %get-tuple-element.152, f32[80,128]{1,0:T(8,128)S(1)} %get-tuple-element.152, f32[80,128]{1,0:T(8,128)S(1)} %get-tuple-element.152), branch_computations={%region_20.21_spmd, %region_21.22_spmd, %region_22.23_spmd, %regio... | conditional | bytes 163888 | solution.py:326
  132.6 1.3 collective-permute-start.20
  133.9 22.5 %collective-permute-done.20 = f32[80,128]{1,0:T(8,128)} collective-permute-done((f32[80,128]{1,0:T(8,128)S(1)}, f32[80,128]{1,0:T(8,128)}, u32[]{:S(2)}, u32[]{:S(2)}) %collective-permute-start.20) | collective-permute-done | bytes 40992 | tf_op jit(solution)/shard_map/cond/branch_1_fun/ppermute | solution.py:324
  156.4 0.7 collective-permute-start.70
  157.1 8.6 %conditional.9 = (f32[80,128]{1,0:T(8,128)}) conditional(s32[]{:T(128)} %bitcast.12, f32[80,128]{1,0:T(8,128)} %get-tuple-element.163, f32[80,128]{1,0:T(8,128)} %get-tuple-element.163, f32[80,128]{1,0:T(8,128)} %get-tuple-element.163, f32[80,128]{1,0:T(8,128)} %get-tuple-element.163, ...), branch_computations={%region_24.25_spmd, %region_25.26_spmd, %region_26.27_spmd, %regio... | conditional | bytes 245808 | solution.py:337
  157.1 1.9 %collective-permute-start.35 = (f32[80,128]{1,0:T(8,128)}, f32[80,128]{1,0:T(8,128)S(1)}, u32[]{:S(2)}, u32[]{:S(2)}) collective-permute-start(f32[80,128]{1,0:T(8,128)} %param.37), channel_id=1, source_target_pairs={{0,104},{2,106},{4,108},{6,110},{8,112},{10,114},{12,116},{14,118}... | collective-permute-start | bytes 122888 | tf_op jit(solution)/shard_map/cond/branch_13_fun/ppermute | solution.py:334
  159.0 6.0 %collective-permute-done.35 = f32[80,128]{1,0:T(8,128)S(1)} collective-permute-done((f32[80,128]{1,0:T(8,128)}, f32[80,128]{1,0:T(8,128)S(1)}, u32[]{:S(2)}, u32[]{:S(2)}) %collective-permute-start.35) | collective-permute-done | bytes 40992 | tf_op jit(solution)/shard_map/cond/branch_13_fun/ppermute | solution.py:334
  165.0 0.6 copy.45
  165.6 0.9 fusion.5
  166.6 9.0 %conditional.10 = (f32[80,128]{1,0:T(8,128)S(1)}) conditional(s32[]{:T(128)} %bitcast.14, f32[80,128]{1,0:T(8,128)S(1)} %add.63, f32[80,128]{1,0:T(8,128)S(1)} %add.63, f32[80,128]{1,0:T(8,128)S(1)} %add.63, f32[80,128]{1,0:T(8,128)S(1)} %add.63, f32[80,128]{1,0:T(8,128)S(1)} %add.63, ...), branch_computations={%region_40.41_spmd, %region_41.42_spmd, %region_42.43_spmd, %regio... | conditional | bytes 245808 | solution.py:337
  166.6 1.9 %collective-permute-start.40 = (f32[80,128]{1,0:T(8,128)S(1)}, f32[80,128]{1,0:T(8,128)S(1)}, u32[]{:S(2)}, u32[]{:S(2)}) collective-permute-start(f32[80,128]{1,0:T(8,128)S(1)} %param.43), channel_id=1, source_target_pairs={{0,24},{2,26},{4,28},{6,30},{8,32},{10,34},{12,36},{14,38},{16,40}... | collective-permute-start | bytes 122888 | tf_op jit(solution)/shard_map/cond/branch_3_fun/ppermute | solution.py:334
  168.6 7.0 %collective-permute-done.40 = f32[80,128]{1,0:T(8,128)S(1)} collective-permute-done((f32[80,128]{1,0:T(8,128)S(1)}, f32[80,128]{1,0:T(8,128)S(1)}, u32[]{:S(2)}, u32[]{:S(2)}) %collective-permute-start.40) | collective-permute-done | bytes 40992 | tf_op jit(solution)/shard_map/cond/branch_3_fun/ppermute | solution.py:334
  175.5 2.3 %conditional.11 = (f32[80,128]{1,0:T(8,128)}) conditional(s32[]{:T(128)} %bitcast.13, f32[80,128]{1,0:T(8,128)S(1)} %get-tuple-element.165, f32[80,128]{1,0:T(8,128)S(1)} %get-tuple-element.165, f32[80,128]{1,0:T(8,128)S(1)} %get-tuple-element.165, f32[80,128]{1,0:T(8,128)S(1)} %get-tuple-element.165), branch_computations={%region_56.57_spmd, %region_57.58_spmd, %region_58.59_spmd, %regio... | conditional | bytes 163888 | solution.py:326
  175.5 1.9 %collective-permute-start.53 = (f32[80,128]{1,0:T(8,128)S(1)}, f32[80,128]{1,0:T(8,128)}, u32[]{:S(2)}, u32[]{:S(2)}) collective-permute-start(f32[80,128]{1,0:T(8,128)S(1)} %param.56), channel_id=1, source_target_pairs={{0,128},{2,130},{4,132},{6,134},{8,136},{10,138},{12,140},{14,142}... | collective-permute-start | bytes 122888 | tf_op jit(solution)/shard_map/cond/branch_0_fun/ppermute | solution.py:324
  177.8 1.8 %shard_map.91 = (f32[1,320,128]{2,1,0:T(8,128)}, f32[1,80,128]{2,1,0:T(8,128)}) custom-call(s32[1]{0:T(128)} %bitcast.row_ref, f32[400,128]{1,0:T(8,128)S(1)} %get-tuple-element.153.going_ref, f32[400,128]{1,0:T(8,128)S(1)} %collective-permute-done.70.homed_ref, f32[80,128]{1,0:T(8,128)} %get-tuple-element.164.second_ref, ...), custom_call_target="tpu_custom_call" | custom-call | tf_op jit(solution)/shard_map/pallas_call | solution.py:293
  (28 shorter events, 4.3 us)
Async XLA Ops:
  2.4 21.5 %collective-permute-start.57 = (f32[1152,128]{1,0:T(8,128)S(1)}, f32[1152,128]{1,0:T(8,128)S(1)}, u32[]{:S(2)}, u32[]{:S(2)}) collective-permute-start(f32[1152,128]{1,0:T(8,128)S(1)} %shard_map.77.both_ref), channel_id=1, source_target_pairs={{0,2},{2,4},{4,6},{6,8},{8,10},{10,12},{12,14},{14,16},{16,18},{18... | collective-permute-start | bytes 1769480 | tf_op jit(solution)/shard_map/ppermute | solution.py:356
  24.2 16.1 %collective-permute-start.59 = (f32[672,128]{1,0:T(8,128)S(1)}, f32[672,128]{1,0:T(8,128)S(1)}, u32[]{:S(2)}, u32[]{:S(2)}) collective-permute-start(f32[672,128]{1,0:T(8,128)S(1)} %shard_map.79.b_ref), channel_id=1, source_target_pairs={{0,4},{2,6},{4,8},{6,10},{8,12},{10,14},{12,16},{14,18},{16,20},{1... | collective-permute-start | bytes 1032200 | tf_op jit(solution)/shard_map/ppermute | solution.py:356
  26.7 13.0 %collective-permute-start.58 = (f32[480,128]{1,0:T(8,128)S(1)}, f32[480,128]{1,0:T(8,128)S(1)}, u32[]{:S(2)}, u32[]{:S(2)}) collective-permute-start(f32[480,128]{1,0:T(8,128)S(1)} %shard_map.78.a_ref), channel_id=1, source_target_pairs={{0,4},{2,6},{4,8},{6,10},{8,12},{10,14},{12,16},{14,18},{16,20},{1... | collective-permute-start | bytes 737288 | tf_op jit(solution)/shard_map/ppermute | solution.py:356
  40.7 13.6 %collective-permute-start.61 = (f32[672,128]{1,0:T(8,128)S(1)}, f32[672,128]{1,0:T(8,128)S(1)}, u32[]{:S(2)}, u32[]{:S(2)}) collective-permute-start(f32[672,128]{1,0:T(8,128)S(1)} %shard_map.81.b_ref), channel_id=1, source_target_pairs={{0,8},{2,10},{4,12},{6,14},{8,16},{10,18},{12,20},{14,22},{16,24},... | collective-permute-start | bytes 1032200 | tf_op jit(solution)/shard_map/ppermute | solution.py:356
  42.7 11.1 %collective-permute-start.60 = (f32[480,128]{1,0:T(8,128)S(1)}, f32[480,128]{1,0:T(8,128)S(1)}, u32[]{:S(2)}, u32[]{:S(2)}) collective-permute-start(f32[480,128]{1,0:T(8,128)S(1)} %shard_map.80.a_ref), channel_id=1, source_target_pairs={{0,8},{2,10},{4,12},{6,14},{8,16},{10,18},{12,20},{14,22},{16,24},... | collective-permute-start | bytes 737288 | tf_op jit(solution)/shard_map/ppermute | solution.py:356
  54.7 20.8 %collective-permute-start.62 = (f32[672,128]{1,0:T(8,128)S(1)}, f32[672,128]{1,0:T(8,128)S(1)}, u32[]{:S(2)}, u32[]{:S(2)}) collective-permute-start(f32[672,128]{1,0:T(8,128)S(1)} %shard_map.83.b_ref), channel_id=1, source_target_pairs={{0,16},{2,18},{4,20},{6,22},{8,24},{10,26},{12,28},{14,30},{16,32}... | collective-permute-start | bytes 1032200 | tf_op jit(solution)/shard_map/ppermute | solution.py:356
  56.6 18.3 %collective-permute-start.63 = (f32[480,128]{1,0:T(8,128)S(1)}, f32[480,128]{1,0:T(8,128)S(1)}, u32[]{:S(2)}, u32[]{:S(2)}) collective-permute-start(f32[480,128]{1,0:T(8,128)S(1)} %shard_map.82.a_ref), channel_id=1, source_target_pairs={{0,16},{2,18},{4,20},{6,22},{8,24},{10,26},{12,28},{14,30},{16,32}... | collective-permute-start | bytes 737288 | tf_op jit(solution)/shard_map/ppermute | solution.py:356
  75.5 11.4 %copy-start = (f32[1,1,1,80,320]{4,3,2,1,0:T(8,128)S(1)}, f32[1,1,1,80,320]{4,3,2,1,0:T(8,128)}, u32[]{:S(2)}) copy-start(f32[1,1,1,80,320]{4,3,2,1,0:T(8,128)} %param.69) | copy-start | bytes 307204
  75.5 11.4 %copy-start.1 = (f32[1,1,1,320,80]{3,4,2,1,0:T(8,128)S(1)}, f32[1,1,1,320,80]{3,4,2,1,0:T(8,128)}, u32[]{:S(2)}) copy-start(f32[1,1,1,320,80]{3,4,2,1,0:T(8,128)} %param.70) | copy-start | bytes 307204
  76.0 29.7 %collective-permute-start.64 = (f32[400,128]{1,0:T(8,128)S(1)}, f32[400,128]{1,0:T(8,128)S(1)}, u32[]{:S(2)}, u32[]{:S(2)}) collective-permute-start(f32[400,128]{1,0:T(8,128)S(1)} %get-tuple-element.148), channel_id=1, source_target_pairs={{0,32},{2,34},{4,36},{6,38},{8,40},{10,42},{12,44},{14,46},{16,48}... | collective-permute-start | bytes 614408 | tf_op jit(solution)/shard_map/ppermute | solution.py:356
  77.9 21.2 %collective-permute-start.66 = (f32[320,128]{1,0:T(8,128)S(1)}, f32[320,128]{1,0:T(8,128)S(1)}, u32[]{:S(2)}, u32[]{:S(2)}) collective-permute-start(f32[320,128]{1,0:T(8,128)S(1)} %get-tuple-element.147.s_ref), channel_id=1, source_target_pairs={{0,32},{2,34},{4,36},{6,38},{8,40},{10,42},{12,44},{14,46},{16,48}... | collective-permute-start | bytes 491528 | tf_op jit(solution)/shard_map/ppermute | solution.py:356
  99.4 17.4 %collective-permute-start.68 = (f32[320,128]{1,0:T(8,128)S(1)}, f32[320,128]{1,0:T(8,128)S(1)}, u32[]{:S(2)}, u32[]{:S(2)}) collective-permute-start(f32[320,128]{1,0:T(8,128)S(1)} %shard_map.88.s_ref), channel_id=1, source_target_pairs={{0,64},{2,66},{4,68},{6,70},{8,72},{10,74},{12,76},{14,78},{16,80}... | collective-permute-start | bytes 491528 | tf_op jit(solution)/shard_map/ppermute | solution.py:418
  105.7 7.7 %collective-permute-start.65 = (f32[400,128]{1,0:T(8,128)S(1)}, f32[400,128]{1,0:T(8,128)S(1)}, u32[]{:S(2)}, u32[]{:S(2)}) collective-permute-start(f32[400,128]{1,0:T(8,128)S(1)} %collective-permute-done.64.mine_ref), channel_id=1, source_target_pairs={{0,1},{1,0},{2,3},{3,2},{4,5},{5,4},{6,7},{7,6},{8,9},{9,8},{10,11... | collective-permute-start | bytes 614408 | tf_op jit(solution)/shard_map/ppermute | solution.py:419
  108.4 0.8 copy-start.2
  108.5 23.1 %collective-permute-start.69 = (f32[80,400]{1,0:T(8,128)S(1)}, f32[80,400]{1,0:T(8,128)S(1)}, u32[]{:S(2)}, u32[]{:S(2)}) collective-permute-start(f32[80,400]{1,0:T(8,128)S(1)} %pad_maximum_fusion), channel_id=1, source_target_pairs={{128,194},{130,196},{132,198},{134,200},{136,202},{138,204},{140,2... | collective-permute-start | bytes 384008 | tf_op jit(solution)/shard_map/ppermute | solution.py:382
  114.4 17.1 %collective-permute-start.67 = (f32[320,128]{1,0:T(8,128)S(1)}, f32[320,128]{1,0:T(8,128)S(1)}, u32[]{:S(2)}, u32[]{:S(2)}) collective-permute-start(f32[320,128]{1,0:T(8,128)S(1)} %get-tuple-element.150.s_ref), channel_id=1, source_target_pairs={{128,192},{130,194},{132,196},{134,198},{136,200},{138,202},{140,2... | collective-permute-start | bytes 491528 | tf_op jit(solution)/shard_map/ppermute | solution.py:431
  117.5 11.8 %collective-permute-start.11 = (f32[80,128]{1,0:T(8,128)S(1)}, f32[80,128]{1,0:T(8,128)S(1)}, u32[]{:S(2)}, u32[]{:S(2)}) collective-permute-start(f32[80,128]{1,0:T(8,128)S(1)} %param.12), channel_id=1, source_target_pairs={{0,96},{2,98},{4,100},{6,102},{8,104},{10,106},{12,108},{14,110},{... | collective-permute-start | bytes 122888 | tf_op jit(solution)/shard_map/cond/branch_12_fun/ppermute | solution.py:334
  129.3 2.3 %collective-permute-start.15 = (f32[80,128]{1,0:T(8,128)S(1)}, f32[80,128]{1,0:T(8,128)}, u32[]{:S(2)}, u32[]{:S(2)}) collective-permute-start(f32[80,128]{1,0:T(8,128)S(1)} %param.16), channel_id=1, source_target_pairs={{0,128},{2,130},{4,132},{6,134},{8,136},{10,138},{12,140},{14,142}... | collective-permute-start | bytes 122888 | tf_op jit(solution)/shard_map/cond/branch_0_fun/ppermute | solution.py:324
  132.6 23.8 %collective-permute-start.20 = (f32[80,128]{1,0:T(8,128)S(1)}, f32[80,128]{1,0:T(8,128)}, u32[]{:S(2)}, u32[]{:S(2)}) collective-permute-start(f32[80,128]{1,0:T(8,128)S(1)} %param.21), channel_id=1, source_target_pairs={{128,258},{130,260},{132,262},{134,264},{136,266},{138,268},{140,2... | collective-permute-start | bytes 122888 | tf_op jit(solution)/shard_map/cond/branch_1_fun/ppermute | solution.py:324
  156.4 21.4 %collective-permute-start.70 = (f32[400,128]{1,0:T(8,128)S(1)}, f32[400,128]{1,0:T(8,128)S(1)}, u32[]{:S(2)}, u32[]{:S(2)}) collective-permute-start(f32[400,128]{1,0:T(8,128)S(1)} %get-tuple-element.153.going_ref), channel_id=1, source_target_pairs={{128,190},{130,192},{132,194},{134,196},{136,198},{138,200},{140,2... | collective-permute-start | bytes 614408 | tf_op jit(solution)/shard_map/ppermute | solution.py:459
  157.1 7.9 %collective-permute-start.35 = (f32[80,128]{1,0:T(8,128)}, f32[80,128]{1,0:T(8,128)S(1)}, u32[]{:S(2)}, u32[]{:S(2)}) collective-permute-start(f32[80,128]{1,0:T(8,128)} %param.37), channel_id=1, source_target_pairs={{0,104},{2,106},{4,108},{6,110},{8,112},{10,114},{12,116},{14,118}... | collective-permute-start | bytes 122888 | tf_op jit(solution)/shard_map/cond/branch_13_fun/ppermute | solution.py:334
  166.6 8.9 %collective-permute-start.40 = (f32[80,128]{1,0:T(8,128)S(1)}, f32[80,128]{1,0:T(8,128)S(1)}, u32[]{:S(2)}, u32[]{:S(2)}) collective-permute-start(f32[80,128]{1,0:T(8,128)S(1)} %param.43), channel_id=1, source_target_pairs={{0,24},{2,26},{4,28},{6,30},{8,32},{10,34},{12,36},{14,38},{16,40}... | collective-permute-start | bytes 122888 | tf_op jit(solution)/shard_map/cond/branch_3_fun/ppermute | solution.py:334
  175.5 2.3 %collective-permute-start.53 = (f32[80,128]{1,0:T(8,128)S(1)}, f32[80,128]{1,0:T(8,128)}, u32[]{:S(2)}, u32[]{:S(2)}) collective-permute-start(f32[80,128]{1,0:T(8,128)S(1)} %param.56), channel_id=1, source_target_pairs={{0,128},{2,130},{4,132},{6,134},{8,136},{10,138},{12,140},{14,142}... | collective-permute-start | bytes 122888 | tf_op jit(solution)/shard_map/cond/branch_0_fun/ppermute | solution.py:324

commit v8 on v7

--- a/solution.py
+++ b/solution.py
@@ -226,8 +226,9 @@
         out_ref[...] = dot(whole(gotm_ref, n), whole(m_ref, n))
 
 
-def close_kernel(m_ref, s_ref, got_ref, out_ref):
+def close_kernel(m_ref, s_ref, got_ref, flux_ref, out_ref, trace_ref):
     out_ref[...] = s_ref[...] + dot(m_ref[...], got_ref[...])
+    trace_ref[...] = dot(flux_ref[...], out_ref[...])
 
 
 def second_kernel(
@@ -259,28 +260,23 @@
         out_ref[...] = base
 
 
+def third_kernel(base_ref, gain_ref, moved_ref, out_ref):
+    out_ref[...] = base_ref[...] + dot(gain_ref[...], moved_ref[...])
+
+
 def last_kernel(
-    row_ref, going_ref, homed_ref, second_ref, third_ref, lift_ref, flux_ref, gain_ref, state_ref, trace_ref, all_ref
+    row_ref, going_ref, homed_ref, second_ref, third_ref, lift_ref, flux_ref, gain_ref, state_ref, trace_ref
 ):
     n = state_ref.shape[1]
-    row = row_ref[0]
-
-    @pl.when(row % 2 == 1)
-    def _():
-        all_ref[...] = homed_ref[...]
-
-    @pl.when(row % 2 == 0)
-    def _():
-        all_ref[...] = going_ref[...]
-
-    for section, moved_ref in ((2, second_ref), (3, third_ref)):
-
-        @pl.when(row == section)
-        def _(moved_ref=moved_ref):
-            all_ref[n:] = moved_ref[...]
-
-    state_ref[0] = all_ref[0:n] + dot(lift_ref[...], all_ref[n:], (0, 0))
-    trace_ref[0] = dot(flux_ref[...], all_ref[0:n]) + dot(gain_ref[...], all_ref[n:])
+    inlets = (going_ref.at[n:], homed_ref.at[n:], second_ref, third_ref)
+    for row, inlet_ref in enumerate(inlets):
+        held_ref = homed_ref if is_mirrored(row) else going_ref
+
+        @pl.when(row_ref[0] == row)
+        def _(held_ref=held_ref, inlet_ref=inlet_ref):
+            state, inlet = held_ref[0:n], inlet_ref[...]
+            state_ref[0] = state + dot(lift_ref[...], inlet, (0, 0))
+            trace_ref[0] = dot(flux_ref[...], state) + dot(gain_ref[...], inlet)
 
 
 VMEM = pl.BlockSpec(memory_space=pltpu.VMEM)
@@ -432,12 +428,15 @@
     matrix = step(square_kernel, [(n, n)], matrix, got_matrix)
 
     mask = sectors - 1
-    state = call(close_kernel, [VMEM] * 3, [(n, LANES)], matrix, ahead, got_ahead)
-    shift = (mortar_shift[0] - (half - 1)) & mask
-    moved = hop(turn(exact_dot(flux, state), shift, rows, sectors), shift, range(0, rows - 1, 2), sectors)
+    shifts = [mortar_shift[k] for k in range(rows - 1)]
+    face = (flux.shape[0], LANES)
+    state, trace = call(
+        close_kernel, [VMEM] * 4, [(n, LANES), face], matrix, ahead, got_ahead, flux
+    )
+    shift = (shifts[0] - (half - 1)) & mask
+    moved = hop(turn(trace, shift, rows, sectors), shift, range(0, rows - 1, 2), sectors)
 
     row = jnp.reshape(row_index, (1,)).astype(jnp.int32)
-    face = (flux.shape[0], LANES)
     going, base, leaving = call(
         second_kernel,
         [SMEM] + [VMEM] * 8,
@@ -452,14 +451,15 @@
         flux,
         gain,
     )
-    shift = (mortar_shift[1] + (half - 1)) & mask
+    shift = (shifts[1] + (half - 1)) & mask
     moved = hop(leaving, shift, range(1, rows - 1, 2), sectors)
     going, moved = lax.optimization_barrier((going, moved))
     route = sector_route(rows, sectors, lambda row: half - 1 if is_mirrored(row) else None)
     homed = lax.ppermute(going, axes, route)
     second = turn(moved, shift, rows, sectors)
-    shift = mortar_shift[2] & mask
-    leaving = turn(base + exact_dot(gain, second), shift, rows, sectors)
+    shift = shifts[2] & mask
+    leaving = call(third_kernel, [VMEM] * 3, [face], base, gain, second)
+    leaving = turn(leaving, shift, rows, sectors)
     third = hop(leaving, shift, range(0, rows - 1, 2), sectors)
     return call(
         last_kernel,
@@ -473,7 +473,6 @@
         lift.T,
         flux,
         gain,
-        scratch=[pltpu.VMEM((n + face[0], LANES), jnp.float32)],
     )
 
 

time: 181 us -> 175 us (0.967)
  starting transfers between devices: 57.1 us -> 51.9 us
  waiting for transfers between devices: 106 us -> 104 us
    ppermute x1, waiting for transfers between devices: 1.75 us -> 9.95 us  [on_device(): got_ahead = lax.ppermute(ahead, axes, route)]
    ppermute x6, waiting for transfers between devices: 37.8 us -> 30.6 us  [send(): return lax.ppermute(trace, ('row', 'sector'), route)]
    ppermute x6, starting transfers between devices: 19 us -> 15 us  [send(): return lax.ppermute(trace, ('row', 'sector'), route)]
    pallas_call x15 -> x16, Pallas kernels: 10.2 us -> 11.6 us  [call(): pl.pallas_call(kernel, out_shape=shapes, in_specs=specs, out_specs=[VMEM]...]
  transfers between devices with their start and end apart: 20 -> 20, of which waited for: 13 -> 12; matrix products, arithmetic and copies ran while one was open for 2% -> 1% of each run, Pallas kernels for 2% -> 3%
where the time goes in v8:
time: 175 us; the launch traced here: 172 us
  waiting for transfers between devices  104 us (59%)
  starting transfers between devices  51.9 us (30%)
  Pallas kernels  11.6 us (7%)
  between operations  2.86 us (2%)
    ppermute x9, waiting for transfers between devices, move(): return lax.ppermute(block, axes, route)  63.6 us
    ppermute x6, waiting for transfers between devices, send(): return lax.ppermute(trace, ('row', 'sector'), route)  30.6 us
    ppermute x9, starting transfers between devices, move(): return lax.ppermute(block, axes, route)  27.2 us
    ppermute x6, starting transfers between devices, send(): return lax.ppermute(trace, ('row', 'sector'), route)  15 us
    pallas_call x16, Pallas kernels, call(): pl.pallas_call(kernel, out_shape=shapes, in_specs=specs, out_specs=[VMEM]...  11.6 us
    ppermute x1, waiting for transfers between devices, on_device(): got_ahead = lax.ppermute(ahead, axes, route)  9.95 us
    ppermute x1, starting transfers between devices, on_device(): got_ahead = lax.ppermute(ahead, axes, route)  5.07 us
  transfers between devices with their start and end apart: 20, of which 12 were waited for; matrix products, arithmetic and copies ran while one was open for 1% of the time, Pallas kernels for 3%

profile of v8, /device:TPU:24, one launch (start us, length us, event | category | flops | bytes accessed | tf_op | source)
XLA Modules:
  0.0 172.3 jit_solution(18340943406110149365)
XLA Ops:
  0.6 1.7 shard_map.77.both_ref
  2.4 3.4 %collective-permute-start.57 = (f32[1152,128]{1,0:T(8,128)S(1)}, f32[1152,128]{1,0:T(8,128)S(1)}, u32[]{:S(2)}, u32[]{:S(2)}) collective-permute-start(f32[1152,128]{1,0:T(8,128)S(1)} %shard_map.77.both_ref), channel_id=1, source_target_pairs={{0,2},{2,4},{4,6},{6,8},{8,10},{10,12},{12,14},{14,16},{16,18},{18... | collective-permute-start | bytes 1769480 | tf_op jit(solution)/shard_map/ppermute | solution.py:352
  5.8 18.0 %collective-permute-done.57.got_ref = f32[1152,128]{1,0:T(8,128)S(1)} collective-permute-done((f32[1152,128]{1,0:T(8,128)S(1)}, f32[1152,128]{1,0:T(8,128)S(1)}, u32[]{:S(2)}, u32[]{:S(2)}) %collective-permute-start.57) | collective-permute-done | bytes 589856 | tf_op jit(solution)/shard_map/ppermute | solution.py:352
  24.2 1.9 %collective-permute-start.59 = (f32[672,128]{1,0:T(8,128)S(1)}, f32[672,128]{1,0:T(8,128)S(1)}, u32[]{:S(2)}, u32[]{:S(2)}) collective-permute-start(f32[672,128]{1,0:T(8,128)S(1)} %shard_map.79.b_ref), channel_id=1, source_target_pairs={{0,4},{2,6},{4,8},{6,10},{8,12},{10,14},{12,16},{14,18},{16,20},{1... | collective-permute-start | bytes 1032200 | tf_op jit(solution)/shard_map/ppermute | solution.py:352
  26.2 0.6 shard_map.78.a_ref
  26.7 1.9 %collective-permute-start.58 = (f32[480,128]{1,0:T(8,128)S(1)}, f32[480,128]{1,0:T(8,128)S(1)}, u32[]{:S(2)}, u32[]{:S(2)}) collective-permute-start(f32[480,128]{1,0:T(8,128)S(1)} %shard_map.78.a_ref), channel_id=1, source_target_pairs={{0,4},{2,6},{4,8},{6,10},{8,12},{10,14},{12,16},{14,18},{16,20},{1... | collective-permute-start | bytes 737288 | tf_op jit(solution)/shard_map/ppermute | solution.py:352
  28.7 11.1 %collective-permute-done.58.got_ref = f32[480,128]{1,0:T(8,128)S(1)} collective-permute-done((f32[480,128]{1,0:T(8,128)S(1)}, f32[480,128]{1,0:T(8,128)S(1)}, u32[]{:S(2)}, u32[]{:S(2)}) %collective-permute-start.58) | collective-permute-done | bytes 245792 | tf_op jit(solution)/shard_map/ppermute | solution.py:352
  39.7 0.6 shard_map.80.a_ref
  40.7 1.9 %collective-permute-start.61 = (f32[672,128]{1,0:T(8,128)S(1)}, f32[672,128]{1,0:T(8,128)S(1)}, u32[]{:S(2)}, u32[]{:S(2)}) collective-permute-start(f32[672,128]{1,0:T(8,128)S(1)} %shard_map.81.b_ref), channel_id=1, source_target_pairs={{0,8},{2,10},{4,12},{6,14},{8,16},{10,18},{12,20},{14,22},{16,24},... | collective-permute-start | bytes 1032200 | tf_op jit(solution)/shard_map/ppermute | solution.py:352
  42.7 1.9 %collective-permute-start.60 = (f32[480,128]{1,0:T(8,128)S(1)}, f32[480,128]{1,0:T(8,128)S(1)}, u32[]{:S(2)}, u32[]{:S(2)}) collective-permute-start(f32[480,128]{1,0:T(8,128)S(1)} %shard_map.80.a_ref), channel_id=1, source_target_pairs={{0,8},{2,10},{4,12},{6,14},{8,16},{10,18},{12,20},{14,22},{16,24},... | collective-permute-start | bytes 737288 | tf_op jit(solution)/shard_map/ppermute | solution.py:352
  44.6 9.1 %collective-permute-done.60.got_ref = f32[480,128]{1,0:T(8,128)S(1)} collective-permute-done((f32[480,128]{1,0:T(8,128)S(1)}, f32[480,128]{1,0:T(8,128)S(1)}, u32[]{:S(2)}, u32[]{:S(2)}) %collective-permute-start.60) | collective-permute-done | bytes 245792 | tf_op jit(solution)/shard_map/ppermute | solution.py:352
  53.7 0.6 shard_map.82.a_ref
  54.7 1.9 %collective-permute-start.62 = (f32[672,128]{1,0:T(8,128)S(1)}, f32[672,128]{1,0:T(8,128)S(1)}, u32[]{:S(2)}, u32[]{:S(2)}) collective-permute-start(f32[672,128]{1,0:T(8,128)S(1)} %shard_map.83.b_ref), channel_id=1, source_target_pairs={{0,16},{2,18},{4,20},{6,22},{8,24},{10,26},{12,28},{14,30},{16,32}... | collective-permute-start | bytes 1032200 | tf_op jit(solution)/shard_map/ppermute | solution.py:352
  56.6 3.3 %collective-permute-start.63 = (f32[480,128]{1,0:T(8,128)S(1)}, f32[480,128]{1,0:T(8,128)S(1)}, u32[]{:S(2)}, u32[]{:S(2)}) collective-permute-start(f32[480,128]{1,0:T(8,128)S(1)} %shard_map.82.a_ref), channel_id=1, source_target_pairs={{0,16},{2,18},{4,20},{6,22},{8,24},{10,26},{12,28},{14,30},{16,32}... | collective-permute-start | bytes 737288 | tf_op jit(solution)/shard_map/ppermute | solution.py:352
  60.0 15.0 %collective-permute-done.63.got_ref = f32[480,128]{1,0:T(8,128)S(1)} collective-permute-done((f32[480,128]{1,0:T(8,128)S(1)}, f32[480,128]{1,0:T(8,128)S(1)}, u32[]{:S(2)}, u32[]{:S(2)}) %collective-permute-start.63) | collective-permute-done | bytes 245792 | tf_op jit(solution)/shard_map/ppermute | solution.py:352
  74.9 0.6 shard_map.84.new_a_ref
  76.0 1.9 %collective-permute-start.64 = (f32[400,128]{1,0:T(8,128)S(1)}, f32[400,128]{1,0:T(8,128)S(1)}, u32[]{:S(2)}, u32[]{:S(2)}) collective-permute-start(f32[400,128]{1,0:T(8,128)S(1)} %get-tuple-element.150), channel_id=1, source_target_pairs={{0,32},{2,34},{4,36},{6,38},{8,40},{10,42},{12,44},{14,46},{16,48}... | collective-permute-start | bytes 614408 | tf_op jit(solution)/shard_map/ppermute | solution.py:352
  77.9 9.0 %collective-permute-start.66 = (f32[320,128]{1,0:T(8,128)S(1)}, f32[320,128]{1,0:T(8,128)S(1)}, u32[]{:S(2)}, u32[]{:S(2)}) collective-permute-start(f32[320,128]{1,0:T(8,128)S(1)} %get-tuple-element.149.s_ref), channel_id=1, source_target_pairs={{0,32},{2,34},{4,36},{6,38},{8,40},{10,42},{12,44},{14,46},{16,48}... | collective-permute-start | bytes 491528 | tf_op jit(solution)/shard_map/ppermute | solution.py:352
  86.9 10.4 %collective-permute-done.64.mine_ref = f32[400,128]{1,0:T(8,128)S(1)} collective-permute-done((f32[400,128]{1,0:T(8,128)S(1)}, f32[400,128]{1,0:T(8,128)S(1)}, u32[]{:S(2)}, u32[]{:S(2)}) %collective-permute-start.64) | collective-permute-done | bytes 204832 | tf_op jit(solution)/shard_map/ppermute | solution.py:352
  97.2 2.6 %collective-permute-start.65 = (f32[400,128]{1,0:T(8,128)S(1)}, f32[400,128]{1,0:T(8,128)S(1)}, u32[]{:S(2)}, u32[]{:S(2)}) collective-permute-start(f32[400,128]{1,0:T(8,128)S(1)} %collective-permute-done.64.mine_ref), channel_id=1, source_target_pairs={{0,1},{1,0},{2,3},{3,2},{4,5},{5,4},{6,7},{7,6},{8,9},{9,8},{10,11... | collective-permute-start | bytes 614408 | tf_op jit(solution)/shard_map/ppermute | solution.py:415
  100.6 5.1 %collective-permute-start.68 = (f32[320,128]{1,0:T(8,128)S(1)}, f32[320,128]{1,0:T(8,128)S(1)}, u32[]{:S(2)}, u32[]{:S(2)}) collective-permute-start(f32[320,128]{1,0:T(8,128)S(1)} %shard_map.88.s_ref), channel_id=1, source_target_pairs={{0,64},{2,66},{4,68},{6,70},{8,72},{10,74},{12,76},{14,78},{16,80}... | collective-permute-start | bytes 491528 | tf_op jit(solution)/shard_map/ppermute | solution.py:414
  106.1 0.7 collective-permute-start.67
  106.9 0.7 collective-permute-start.69
  107.6 0.7 fusion.3
  109.5 0.6 shard_map.87.m_ref
  110.1 9.9 %collective-permute-done.68.got_ref = f32[320,128]{1,0:T(8,128)S(1)} collective-permute-done((f32[320,128]{1,0:T(8,128)S(1)}, f32[320,128]{1,0:T(8,128)S(1)}, u32[]{:S(2)}, u32[]{:S(2)}) %collective-permute-start.68) | collective-permute-done | bytes 163872 | tf_op jit(solution)/shard_map/ppermute | solution.py:414
  120.1 0.5 shard_map.89
  120.6 9.8 %conditional.6 = (f32[80,128]{1,0:T(8,128)S(1)}) conditional(s32[]{:T(128)} %bitcast.8, f32[80,128]{1,0:T(8,128)S(1)} %get-tuple-element.154, f32[80,128]{1,0:T(8,128)S(1)} %get-tuple-element.154, f32[80,128]{1,0:T(8,128)S(1)} %get-tuple-element.154, f32[80,128]{1,0:T(8,128)S(1)} %get-tuple-element.154, ...), branch_computations={%region_0.1_spmd, %region_1.2_spmd, %region_2.3_spmd, %region_3.4_... | conditional | bytes 245808 | solution.py:333
  120.7 4.6 %collective-permute-start.11 = (f32[80,128]{1,0:T(8,128)S(1)}, f32[80,128]{1,0:T(8,128)S(1)}, u32[]{:S(2)}, u32[]{:S(2)}) collective-permute-start(f32[80,128]{1,0:T(8,128)S(1)} %param.12), channel_id=1, source_target_pairs={{0,96},{2,98},{4,100},{6,102},{8,104},{10,106},{12,108},{14,110},{... | collective-permute-start | bytes 122888 | tf_op jit(solution)/shard_map/cond/branch_12_fun/ppermute | solution.py:330
  125.2 5.2 %collective-permute-done.11 = f32[80,128]{1,0:T(8,128)S(1)} collective-permute-done((f32[80,128]{1,0:T(8,128)S(1)}, f32[80,128]{1,0:T(8,128)S(1)}, u32[]{:S(2)}, u32[]{:S(2)}) %collective-permute-start.11) | collective-permute-done | bytes 40992 | tf_op jit(solution)/shard_map/cond/branch_12_fun/ppermute | solution.py:330
  130.5 2.3 %conditional.7 = (f32[80,128]{1,0:T(8,128)}) conditional(s32[]{:T(128)} %bitcast.7, f32[80,128]{1,0:T(8,128)S(1)} %get-tuple-element.165, f32[80,128]{1,0:T(8,128)S(1)} %get-tuple-element.165, f32[80,128]{1,0:T(8,128)S(1)} %get-tuple-element.165, f32[80,128]{1,0:T(8,128)S(1)} %get-tuple-element.165), branch_computations={%region_16.17_spmd, %region_17.18_spmd, %region_18.19_spmd, %regio... | conditional | bytes 163888 | solution.py:322
  130.5 1.9 %collective-permute-start.15 = (f32[80,128]{1,0:T(8,128)S(1)}, f32[80,128]{1,0:T(8,128)}, u32[]{:S(2)}, u32[]{:S(2)}) collective-permute-start(f32[80,128]{1,0:T(8,128)S(1)} %param.16), channel_id=1, source_target_pairs={{0,128},{2,130},{4,132},{6,134},{8,136},{10,138},{12,140},{14,142}... | collective-permute-start | bytes 122888 | tf_op jit(solution)/shard_map/cond/branch_0_fun/ppermute | solution.py:320
  132.8 1.2 shard_map.90
  133.9 14.4 %conditional.8 = (f32[80,128]{1,0:T(8,128)}) conditional(s32[]{:T(128)} %bitcast.10, f32[80,128]{1,0:T(8,128)S(1)} %get-tuple-element.156, f32[80,128]{1,0:T(8,128)S(1)} %get-tuple-element.156, f32[80,128]{1,0:T(8,128)S(1)} %get-tuple-element.156, f32[80,128]{1,0:T(8,128)S(1)} %get-tuple-element.156), branch_computations={%region_20.21_spmd, %region_21.22_spmd, %region_22.23_spmd, %regio... | conditional | bytes 163888 | solution.py:322
  134.0 1.3 collective-permute-start.20
  135.3 13.1 %collective-permute-done.20 = f32[80,128]{1,0:T(8,128)} collective-permute-done((f32[80,128]{1,0:T(8,128)S(1)}, f32[80,128]{1,0:T(8,128)}, u32[]{:S(2)}, u32[]{:S(2)}) %collective-permute-start.20) | collective-permute-done | bytes 40992 | tf_op jit(solution)/shard_map/cond/branch_1_fun/ppermute | solution.py:320
  148.4 0.7 collective-permute-start.70
  149.7 8.6 %conditional.9 = (f32[80,128]{1,0:T(8,128)}) conditional(s32[]{:T(128)} %bitcast.11, f32[80,128]{1,0:T(8,128)} %get-tuple-element.167, f32[80,128]{1,0:T(8,128)} %get-tuple-element.167, f32[80,128]{1,0:T(8,128)} %get-tuple-element.167, f32[80,128]{1,0:T(8,128)} %get-tuple-element.167, ...), branch_computations={%region_24.25_spmd, %region_25.26_spmd, %region_26.27_spmd, %regio... | conditional | bytes 245808 | solution.py:333
  149.7 3.4 %collective-permute-start.35 = (f32[80,128]{1,0:T(8,128)}, f32[80,128]{1,0:T(8,128)S(1)}, u32[]{:S(2)}, u32[]{:S(2)}) collective-permute-start(f32[80,128]{1,0:T(8,128)} %param.37), channel_id=1, source_target_pairs={{0,104},{2,106},{4,108},{6,110},{8,112},{10,114},{12,116},{14,118}... | collective-permute-start | bytes 122888 | tf_op jit(solution)/shard_map/cond/branch_13_fun/ppermute | solution.py:330
  153.2 4.5 %collective-permute-done.35 = f32[80,128]{1,0:T(8,128)S(1)} collective-permute-done((f32[80,128]{1,0:T(8,128)}, f32[80,128]{1,0:T(8,128)S(1)}, u32[]{:S(2)}, u32[]{:S(2)}) %collective-permute-start.35) | collective-permute-done | bytes 40992 | tf_op jit(solution)/shard_map/cond/branch_13_fun/ppermute | solution.py:330
  157.7 0.6 copy.45
  158.3 0.9 shard_map.91
  159.2 9.0 %conditional.10 = (f32[80,128]{1,0:T(8,128)S(1)}) conditional(s32[]{:T(128)} %bitcast.13, f32[80,128]{1,0:T(8,128)S(1)} %shard_map.91, f32[80,128]{1,0:T(8,128)S(1)} %shard_map.91, f32[80,128]{1,0:T(8,128)S(1)} %shard_map.91, f32[80,128]{1,0:T(8,128)S(1)} %shard_map.91, f32[80,128]{1,0:T(8,128)S(1)} %shard_map.91, ...), branch_computations={%region_40.41_spmd, %region_41.42_spmd, %region_42.43_spmd, %regio... | conditional | bytes 245808 | solution.py:333
  159.2 1.9 %collective-permute-start.40 = (f32[80,128]{1,0:T(8,128)S(1)}, f32[80,128]{1,0:T(8,128)S(1)}, u32[]{:S(2)}, u32[]{:S(2)}) collective-permute-start(f32[80,128]{1,0:T(8,128)S(1)} %param.43), channel_id=1, source_target_pairs={{0,24},{2,26},{4,28},{6,30},{8,32},{10,34},{12,36},{14,38},{16,40}... | collective-permute-start | bytes 122888 | tf_op jit(solution)/shard_map/cond/branch_3_fun/ppermute | solution.py:330
  161.2 7.0 %collective-permute-done.40 = f32[80,128]{1,0:T(8,128)S(1)} collective-permute-done((f32[80,128]{1,0:T(8,128)S(1)}, f32[80,128]{1,0:T(8,128)S(1)}, u32[]{:S(2)}, u32[]{:S(2)}) %collective-permute-start.40) | collective-permute-done | bytes 40992 | tf_op jit(solution)/shard_map/cond/branch_3_fun/ppermute | solution.py:330
  168.2 2.3 %conditional.11 = (f32[80,128]{1,0:T(8,128)}) conditional(s32[]{:T(128)} %bitcast.12, f32[80,128]{1,0:T(8,128)S(1)} %get-tuple-element.169, f32[80,128]{1,0:T(8,128)S(1)} %get-tuple-element.169, f32[80,128]{1,0:T(8,128)S(1)} %get-tuple-element.169, f32[80,128]{1,0:T(8,128)S(1)} %get-tuple-element.169), branch_computations={%region_56.57_spmd, %region_57.58_spmd, %region_58.59_spmd, %regio... | conditional | bytes 163888 | solution.py:322
  168.2 1.9 %collective-permute-start.53 = (f32[80,128]{1,0:T(8,128)S(1)}, f32[80,128]{1,0:T(8,128)}, u32[]{:S(2)}, u32[]{:S(2)}) collective-permute-start(f32[80,128]{1,0:T(8,128)S(1)} %param.56), channel_id=1, source_target_pairs={{0,128},{2,130},{4,132},{6,134},{8,136},{10,138},{12,140},{14,142}... | collective-permute-start | bytes 122888 | tf_op jit(solution)/shard_map/cond/branch_0_fun/ppermute | solution.py:320
  170.4 1.8 %shard_map.92 = (f32[1,320,128]{2,1,0:T(8,128)}, f32[1,80,128]{2,1,0:T(8,128)}) custom-call(s32[1]{0:T(128)} %bitcast.row_ref, f32[400,128]{1,0:T(8,128)S(1)} %get-tuple-element.157.going_ref, f32[400,128]{1,0:T(8,128)S(1)} %collective-permute-done.70.homed_ref, f32[80,128]{1,0:T(8,128)} %get-tuple-element.168.moved_ref.second_ref, ...), custom_call_target="tpu_custom_call" | custom-call | tf_op jit(solution)/shard_map/pallas_call | solution.py:289
  (26 shorter events, 3.7 us)
Async XLA Ops:
  2.4 21.5 %collective-permute-start.57 = (f32[1152,128]{1,0:T(8,128)S(1)}, f32[1152,128]{1,0:T(8,128)S(1)}, u32[]{:S(2)}, u32[]{:S(2)}) collective-permute-start(f32[1152,128]{1,0:T(8,128)S(1)} %shard_map.77.both_ref), channel_id=1, source_target_pairs={{0,2},{2,4},{4,6},{6,8},{8,10},{10,12},{12,14},{14,16},{16,18},{18... | collective-permute-start | bytes 1769480 | tf_op jit(solution)/shard_map/ppermute | solution.py:352
  24.2 16.1 %collective-permute-start.59 = (f32[672,128]{1,0:T(8,128)S(1)}, f32[672,128]{1,0:T(8,128)S(1)}, u32[]{:S(2)}, u32[]{:S(2)}) collective-permute-start(f32[672,128]{1,0:T(8,128)S(1)} %shard_map.79.b_ref), channel_id=1, source_target_pairs={{0,4},{2,6},{4,8},{6,10},{8,12},{10,14},{12,16},{14,18},{16,20},{1... | collective-permute-start | bytes 1032200 | tf_op jit(solution)/shard_map/ppermute | solution.py:352
  26.7 13.0 %collective-permute-start.58 = (f32[480,128]{1,0:T(8,128)S(1)}, f32[480,128]{1,0:T(8,128)S(1)}, u32[]{:S(2)}, u32[]{:S(2)}) collective-permute-start(f32[480,128]{1,0:T(8,128)S(1)} %shard_map.78.a_ref), channel_id=1, source_target_pairs={{0,4},{2,6},{4,8},{6,10},{8,12},{10,14},{12,16},{14,18},{16,20},{1... | collective-permute-start | bytes 737288 | tf_op jit(solution)/shard_map/ppermute | solution.py:352
  40.7 13.6 %collective-permute-start.61 = (f32[672,128]{1,0:T(8,128)S(1)}, f32[672,128]{1,0:T(8,128)S(1)}, u32[]{:S(2)}, u32[]{:S(2)}) collective-permute-start(f32[672,128]{1,0:T(8,128)S(1)} %shard_map.81.b_ref), channel_id=1, source_target_pairs={{0,8},{2,10},{4,12},{6,14},{8,16},{10,18},{12,20},{14,22},{16,24},... | collective-permute-start | bytes 1032200 | tf_op jit(solution)/shard_map/ppermute | solution.py:352
  42.7 11.1 %collective-permute-start.60 = (f32[480,128]{1,0:T(8,128)S(1)}, f32[480,128]{1,0:T(8,128)S(1)}, u32[]{:S(2)}, u32[]{:S(2)}) collective-permute-start(f32[480,128]{1,0:T(8,128)S(1)} %shard_map.80.a_ref), channel_id=1, source_target_pairs={{0,8},{2,10},{4,12},{6,14},{8,16},{10,18},{12,20},{14,22},{16,24},... | collective-permute-start | bytes 737288 | tf_op jit(solution)/shard_map/ppermute | solution.py:352
  54.7 20.8 %collective-permute-start.62 = (f32[672,128]{1,0:T(8,128)S(1)}, f32[672,128]{1,0:T(8,128)S(1)}, u32[]{:S(2)}, u32[]{:S(2)}) collective-permute-start(f32[672,128]{1,0:T(8,128)S(1)} %shard_map.83.b_ref), channel_id=1, source_target_pairs={{0,16},{2,18},{4,20},{6,22},{8,24},{10,26},{12,28},{14,30},{16,32}... | collective-permute-start | bytes 1032200 | tf_op jit(solution)/shard_map/ppermute | solution.py:352
  56.6 18.3 %collective-permute-start.63 = (f32[480,128]{1,0:T(8,128)S(1)}, f32[480,128]{1,0:T(8,128)S(1)}, u32[]{:S(2)}, u32[]{:S(2)}) collective-permute-start(f32[480,128]{1,0:T(8,128)S(1)} %shard_map.82.a_ref), channel_id=1, source_target_pairs={{0,16},{2,18},{4,20},{6,22},{8,24},{10,26},{12,28},{14,30},{16,32}... | collective-permute-start | bytes 737288 | tf_op jit(solution)/shard_map/ppermute | solution.py:352
  75.5 24.4 %copy-start = (f32[1,1,1,80,320]{4,3,2,1,0:T(8,128)S(1)}, f32[1,1,1,80,320]{4,3,2,1,0:T(8,128)}, u32[]{:S(2)}) copy-start(f32[1,1,1,80,320]{4,3,2,1,0:T(8,128)} %param.69) | copy-start | bytes 307204
  75.5 24.4 %copy-start.1 = (f32[1,1,1,320,80]{3,4,2,1,0:T(8,128)S(1)}, f32[1,1,1,320,80]{3,4,2,1,0:T(8,128)}, u32[]{:S(2)}) copy-start(f32[1,1,1,320,80]{3,4,2,1,0:T(8,128)} %param.70) | copy-start | bytes 307204
  76.0 21.3 %collective-permute-start.64 = (f32[400,128]{1,0:T(8,128)S(1)}, f32[400,128]{1,0:T(8,128)S(1)}, u32[]{:S(2)}, u32[]{:S(2)}) collective-permute-start(f32[400,128]{1,0:T(8,128)S(1)} %get-tuple-element.150), channel_id=1, source_target_pairs={{0,32},{2,34},{4,36},{6,38},{8,40},{10,42},{12,44},{14,46},{16,48}... | collective-permute-start | bytes 614408 | tf_op jit(solution)/shard_map/ppermute | solution.py:352
  77.9 22.3 %collective-permute-start.66 = (f32[320,128]{1,0:T(8,128)S(1)}, f32[320,128]{1,0:T(8,128)S(1)}, u32[]{:S(2)}, u32[]{:S(2)}) collective-permute-start(f32[320,128]{1,0:T(8,128)S(1)} %get-tuple-element.149.s_ref), channel_id=1, source_target_pairs={{0,32},{2,34},{4,36},{6,38},{8,40},{10,42},{12,44},{14,46},{16,48}... | collective-permute-start | bytes 491528 | tf_op jit(solution)/shard_map/ppermute | solution.py:352
  97.2 8.4 %collective-permute-start.65 = (f32[400,128]{1,0:T(8,128)S(1)}, f32[400,128]{1,0:T(8,128)S(1)}, u32[]{:S(2)}, u32[]{:S(2)}) collective-permute-start(f32[400,128]{1,0:T(8,128)S(1)} %collective-permute-done.64.mine_ref), channel_id=1, source_target_pairs={{0,1},{1,0},{2,3},{3,2},{4,5},{5,4},{6,7},{7,6},{8,9},{9,8},{10,11... | collective-permute-start | bytes 614408 | tf_op jit(solution)/shard_map/ppermute | solution.py:415
  100.6 19.5 %collective-permute-start.68 = (f32[320,128]{1,0:T(8,128)S(1)}, f32[320,128]{1,0:T(8,128)S(1)}, u32[]{:S(2)}, u32[]{:S(2)}) collective-permute-start(f32[320,128]{1,0:T(8,128)S(1)} %shard_map.88.s_ref), channel_id=1, source_target_pairs={{0,64},{2,66},{4,68},{6,70},{8,72},{10,74},{12,76},{14,78},{16,80}... | collective-permute-start | bytes 491528 | tf_op jit(solution)/shard_map/ppermute | solution.py:414
  106.1 26.6 %collective-permute-start.67 = (f32[320,128]{1,0:T(8,128)S(1)}, f32[320,128]{1,0:T(8,128)S(1)}, u32[]{:S(2)}, u32[]{:S(2)}) collective-permute-start(f32[320,128]{1,0:T(8,128)S(1)} %get-tuple-element.152.s_ref), channel_id=1, source_target_pairs={{128,192},{130,194},{132,196},{134,198},{136,200},{138,202},{140,2... | collective-permute-start | bytes 491528 | tf_op jit(solution)/shard_map/ppermute | solution.py:427
  106.8 0.8 copy-start.2
  106.9 25.8 %collective-permute-start.69 = (f32[80,400]{1,0:T(8,128)S(1)}, f32[80,400]{1,0:T(8,128)S(1)}, u32[]{:S(2)}, u32[]{:S(2)}) collective-permute-start(f32[80,400]{1,0:T(8,128)S(1)} %pad_maximum_fusion), channel_id=1, source_target_pairs={{128,194},{130,196},{132,198},{134,200},{136,202},{138,204},{140,2... | collective-permute-start | bytes 384008 | tf_op jit(solution)/shard_map/ppermute | solution.py:378
  120.7 9.8 %collective-permute-start.11 = (f32[80,128]{1,0:T(8,128)S(1)}, f32[80,128]{1,0:T(8,128)S(1)}, u32[]{:S(2)}, u32[]{:S(2)}) collective-permute-start(f32[80,128]{1,0:T(8,128)S(1)} %param.12), channel_id=1, source_target_pairs={{0,96},{2,98},{4,100},{6,102},{8,104},{10,106},{12,108},{14,110},{... | collective-permute-start | bytes 122888 | tf_op jit(solution)/shard_map/cond/branch_12_fun/ppermute | solution.py:330
  130.5 2.3 %collective-permute-start.15 = (f32[80,128]{1,0:T(8,128)S(1)}, f32[80,128]{1,0:T(8,128)}, u32[]{:S(2)}, u32[]{:S(2)}) collective-permute-start(f32[80,128]{1,0:T(8,128)S(1)} %param.16), channel_id=1, source_target_pairs={{0,128},{2,130},{4,132},{6,134},{8,136},{10,138},{12,140},{14,142}... | collective-permute-start | bytes 122888 | tf_op jit(solution)/shard_map/cond/branch_0_fun/ppermute | solution.py:320
  134.0 14.4 %collective-permute-start.20 = (f32[80,128]{1,0:T(8,128)S(1)}, f32[80,128]{1,0:T(8,128)}, u32[]{:S(2)}, u32[]{:S(2)}) collective-permute-start(f32[80,128]{1,0:T(8,128)S(1)} %param.21), channel_id=1, source_target_pairs={{128,258},{130,260},{132,262},{134,264},{136,266},{138,268},{140,2... | collective-permute-start | bytes 122888 | tf_op jit(solution)/shard_map/cond/branch_1_fun/ppermute | solution.py:320
  148.4 22.1 %collective-permute-start.70 = (f32[400,128]{1,0:T(8,128)S(1)}, f32[400,128]{1,0:T(8,128)S(1)}, u32[]{:S(2)}, u32[]{:S(2)}) collective-permute-start(f32[400,128]{1,0:T(8,128)S(1)} %get-tuple-element.157.going_ref), channel_id=1, source_target_pairs={{128,190},{130,192},{132,194},{134,196},{136,198},{138,200},{140,2... | collective-permute-start | bytes 614408 | tf_op jit(solution)/shard_map/ppermute | solution.py:458
  149.7 7.9 %collective-permute-start.35 = (f32[80,128]{1,0:T(8,128)}, f32[80,128]{1,0:T(8,128)S(1)}, u32[]{:S(2)}, u32[]{:S(2)}) collective-permute-start(f32[80,128]{1,0:T(8,128)} %param.37), channel_id=1, source_target_pairs={{0,104},{2,106},{4,108},{6,110},{8,112},{10,114},{12,116},{14,118}... | collective-permute-start | bytes 122888 | tf_op jit(solution)/shard_map/cond/branch_13_fun/ppermute | solution.py:330
  159.2 8.9 %collective-permute-start.40 = (f32[80,128]{1,0:T(8,128)S(1)}, f32[80,128]{1,0:T(8,128)S(1)}, u32[]{:S(2)}, u32[]{:S(2)}) collective-permute-start(f32[80,128]{1,0:T(8,128)S(1)} %param.43), channel_id=1, source_target_pairs={{0,24},{2,26},{4,28},{6,30},{8,32},{10,34},{12,36},{14,38},{16,40}... | collective-permute-start | bytes 122888 | tf_op jit(solution)/shard_map/cond/branch_3_fun/ppermute | solution.py:330
  168.2 2.3 %collective-permute-start.53 = (f32[80,128]{1,0:T(8,128)S(1)}, f32[80,128]{1,0:T(8,128)}, u32[]{:S(2)}, u32[]{:S(2)}) collective-permute-start(f32[80,128]{1,0:T(8,128)S(1)} %param.56), channel_id=1, source_target_pairs={{0,128},{2,130},{4,132},{6,134},{8,136},{10,138},{12,140},{14,142}... | collective-permute-start | bytes 122888 | tf_op jit(solution)/shard_map/cond/branch_0_fun/ppermute | solution.py:320
